TPU v7x, 512 devices: a whole 4x8x8 slice. The times are simulated.
512 devices in a mesh: gx: 32 (over x, z), gy: 16 (over y, core).
Axes of the slice: x: 4, y: 8, z: 8, core: 2. Of those that a mesh axis runs over, the one named last changes fastest.
Arguments:
- load: float32 [512, 256, 512], P('gx', 'gy'), may hold values from -130 to 130
- conductivity: bfloat16 [512, 256, 512], P('gx', 'gy'), may hold values from 0.29882812 to 3
- flags: int32 [512, 256, 512], P('gx', 'gy'), may hold values from 0 to 1, as said below
- region: int32 [64, 32, 64], P('gx', 'gy'), may hold values from 0 to 2
- kappa_table: float32 [3], replicated, may hold values from 10 to 100
Outputs:
- solution: float32 [512, 256, 512], P('gx', 'gy')
- residual: float32 [512, 256, 512], P('gx', 'gy')
- direction: float32 [512, 256, 512], P('gx', 'gy')
Inputs may be any that keep to these rules, and one draw needn't show every extreme that they name: flags are 1 only at nodes of the first layer along the third dimension, and all copies of one shared node carry the same flag.
All inputs are finite; a program needn't handle non-finite values.
Results may differ from a plain program's by a relative error of at most 0.0003.
Values sent between devices are 32-bit elements; how exact they have to be, the bound alone decides.
No kernel may reach another device: no remote copies, remote signals or barrier semaphores. Data moves between devices by JAX's collectives and lax.ppermute only.
A program may use at most 64 MiB of HBM per device.

v0:
```python
import jax
import jax.numpy as jnp
import numpy as np
from jax import lax
from jax.sharding import PartitionSpec as P

NREG = 3


CHEB_CENTER = 24.0
CHEB_HALF = 23.0


def padded_2(array, sides, width):
    for axis, dim in sides:
        count, length = (lax.axis_size(axis), array.shape[dim])
        up = [(i, (i + 1) % count) for i in range(count - 1)]
        down = [(j, i) for i, j in up]
        last = lax.slice_in_dim(array, length - width, length, axis=dim)
        first = lax.slice_in_dim(array, 0, width, axis=dim)
        before = lax.ppermute(last, axis, up)
        after = lax.ppermute(first, axis, down)
        array = jnp.concatenate([before, array, after], axis=dim)
    return array


def gll_tables():
    nodes_gll = np.array(
        [
            -1.0,
            -0.8717401485096066,
            -0.5917001814331423,
            -0.2092992179024789,
            0.2092992179024789,
            0.5917001814331423,
            0.8717401485096066,
            1.0,
        ]
    )
    legendre_prev = np.ones(8)
    legendre_now = nodes_gll.copy()
    for degree in range(1, 7):
        legendre_next = ((2 * degree + 1) * nodes_gll * legendre_now - degree * legendre_prev) / (
            degree + 1
        )
        legendre_prev = legendre_now
        legendre_now = legendre_next
    weights_gll = 2.0 / (56.0 * legendre_now**2)
    diff_table = np.zeros((8, 8))
    for row_index in range(8):
        for col_index in range(8):
            if row_index != col_index:
                diff_table[row_index, col_index] = legendre_now[row_index] / (
                    legendre_now[col_index] * (nodes_gll[row_index] - nodes_gll[col_index])
                )
    diff_table[0, 0] = -14.0
    diff_table[7, 7] = 14.0
    return (diff_table, weights_gll)


def pair_fold(padded, which_dim):
    length = padded.shape[which_dim]
    blocks = (length - 2) // 8
    lower_rows = lax.slice_in_dim(padded, 0, length, 8, which_dim)
    upper_rows = lax.slice_in_dim(padded, 1, length, 8, which_dim)
    joined = lower_rows + upper_rows
    inner_rows = lax.slice_in_dim(padded, 1, length - 1, 1, which_dim)
    inner_rows = inner_rows.reshape(
        inner_rows.shape[:which_dim] + (blocks, 8) + inner_rows.shape[which_dim + 1 :]
    )
    first_rows = jnp.expand_dims(lax.slice_in_dim(joined, 0, blocks, 1, which_dim), which_dim + 1)
    last_rows = jnp.expand_dims(
        lax.slice_in_dim(joined, 1, blocks + 1, 1, which_dim), which_dim + 1
    )
    middle = lax.slice_in_dim(inner_rows, 1, 7, 1, which_dim + 1)
    result = jnp.concatenate([first_rows, middle, last_rows], axis=which_dim + 1)
    return result.reshape(
        inner_rows.shape[:which_dim] + (blocks * 8,) + inner_rows.shape[which_dim + 2 :]
    )


def apply_local(vector, coefficient, reaction, derivative, block_deriv):
    rows_x, rows_y, rows_z = vector.shape
    block_z = block_deriv.shape[0]
    highest = lax.Precision.HIGHEST
    shape_x = (rows_x // 8, 8, rows_y, rows_z)
    grad_x = jnp.einsum("ab,ebyz->eayz", derivative, vector.reshape(shape_x), precision=highest)
    back_x = jnp.einsum(
        "ab,eayz->ebyz", derivative, grad_x * coefficient.reshape(shape_x), precision=highest
    )
    shape_y = (rows_x, rows_y // 8, 8, rows_z)
    grad_y = jnp.einsum("ab,xebz->xeaz", derivative, vector.reshape(shape_y), precision=highest)
    back_y = jnp.einsum(
        "ab,xeaz->xebz", derivative, grad_y * coefficient.reshape(shape_y), precision=highest
    )
    shape_z = (rows_x, rows_y, rows_z // block_z, block_z)
    grad_z = jnp.einsum("xykb,ab->xyka", vector.reshape(shape_z), block_deriv, precision=highest)
    back_z = jnp.einsum(
        "xyka,ab->xykb", grad_z * coefficient.reshape(shape_z), block_deriv, precision=highest
    )
    return (
        back_x.reshape(vector.shape)
        + back_y.reshape(vector.shape)
        + back_z.reshape(vector.shape)
        + reaction * vector
    )


def diag_local(coefficient, reaction, derivative, block_deriv):
    rows_x, rows_y, rows_z = coefficient.shape
    block_z = block_deriv.shape[0]
    highest = lax.Precision.HIGHEST
    square_d = derivative * derivative
    square_block = block_deriv * block_deriv
    part_x = jnp.einsum(
        "qa,eqyz->eayz",
        square_d,
        coefficient.reshape(rows_x // 8, 8, rows_y, rows_z),
        precision=highest,
    )
    part_y = jnp.einsum(
        "qa,xeqz->xeaz",
        square_d,
        coefficient.reshape(rows_x, rows_y // 8, 8, rows_z),
        precision=highest,
    )
    part_z = jnp.einsum(
        "xykq,qa->xyka",
        coefficient.reshape(rows_x, rows_y, rows_z // block_z, block_z),
        square_block,
        precision=highest,
    )
    return (
        part_x.reshape(coefficient.shape)
        + part_y.reshape(coefficient.shape)
        + part_z.reshape(coefficient.shape)
        + reaction
    )


def share_weights(count, offset, total):
    position = offset + jnp.arange(count, dtype=jnp.int32)
    within = position % 8
    shared = (within == 7) & (position != total - 1) | (within == 0) & (position != 0)
    return jnp.where(shared, 0.5, 1.0).astype(jnp.float32)


def precondition(residual_in, diagonal, operator):
    update = residual_in / (CHEB_CENTER * diagonal)
    approx = update
    rho_prev = CHEB_HALF / CHEB_CENTER
    for sweep_index in range(2):
        rho_next = 1.0 / (2.0 * CHEB_CENTER / CHEB_HALF - rho_prev)
        update = (
            rho_next * rho_prev * update
            + 2.0 * rho_next / CHEB_HALF * (residual_in - operator(approx)) / diagonal
        )
        approx = approx + update
        rho_prev = rho_next
    return approx


def node_kappa(region, kappa_table):
    element_kappa = jnp.zeros(region.shape, jnp.float32)
    for region_id in range(NREG):
        element_kappa = (
            element_kappa + (region == region_id).astype(jnp.float32) * kappa_table[region_id]
        )
    return jnp.repeat(jnp.repeat(jnp.repeat(element_kappa, 8, axis=0), 8, axis=1), 8, axis=2)


def assemble_nodes(stacked, pair_matrix):
    summed_z = jnp.einsum("kxyz,zw->kxyw", stacked, pair_matrix, precision=lax.Precision.HIGHEST)
    padded = padded_2(summed_z, (("gx", 1),), 1)
    folded = pair_fold(padded, 1)
    padded = padded_2(folded, (("gy", 2),), 1)
    return pair_fold(padded, 2)


def per_device(load, conductivity, flags, region, kappa_table):
    rows_x, rows_y, rows_z = load.shape
    diff_np, weights_np = gll_tables()
    derivative = jnp.asarray(diff_np, dtype=jnp.float32)
    gll_weights = jnp.asarray(weights_np, dtype=jnp.float32)
    block_z = 128
    block_deriv = jnp.kron(jnp.eye(block_z // 8, dtype=jnp.float32), derivative)
    row_ids = jnp.arange(rows_z, dtype=jnp.int32)[:, None]
    col_ids = jnp.arange(rows_z, dtype=jnp.int32)[None, :]
    pair_matrix = (
        (row_ids == col_ids)
        | (row_ids % 8 == 7) & (col_ids == row_ids + 1)
        | (col_ids % 8 == 7) & (row_ids == col_ids + 1)
    ).astype(jnp.float32)
    weight_x = jnp.tile(gll_weights, rows_x // 8)
    weight_y = jnp.tile(gll_weights, rows_y // 8)
    weight_z = jnp.tile(gll_weights, rows_z // 8)
    quad_weights = weight_x[:, None, None] * weight_y[None, :, None] * weight_z[None, None, :]
    coefficient = quad_weights * conductivity.astype(jnp.float32)
    reaction = quad_weights * node_kappa(region, kappa_table)
    keep_mask = (1 - flags).astype(jnp.float32)
    share_x = share_weights(rows_x, lax.axis_index("gx") * rows_x, rows_x * lax.axis_size("gx"))
    share_y = share_weights(rows_y, lax.axis_index("gy") * rows_y, rows_y * lax.axis_size("gy"))
    share_z = share_weights(rows_z, 0, rows_z)
    mult_weights = share_x[:, None, None] * share_y[None, :, None] * share_z[None, None, :]

    def operator(vector):
        local_out = apply_local(keep_mask * vector, coefficient, reaction, derivative, block_deriv)
        return (
            keep_mask * assemble_nodes(local_out[None], pair_matrix)[0] + (1.0 - keep_mask) * vector
        )

    stacked = jnp.stack([load, diag_local(coefficient, reaction, derivative, block_deriv)])
    assembled = assemble_nodes(stacked, pair_matrix)
    first_res = keep_mask * assembled[0]
    diagonal = keep_mask * assembled[1] + (1.0 - keep_mask)
    first_z = precondition(first_res, diagonal, operator)
    first_dot = lax.psum(jnp.sum(first_res * first_z * mult_weights), ("gx", "gy"))
    image_vec = operator(first_z)
    curv_dot = lax.psum(jnp.sum(first_z * image_vec * mult_weights), ("gx", "gy"))
    step_length = first_dot / curv_dot
    solution = step_length * first_z
    residual = first_res - step_length * image_vec
    next_z = precondition(residual, diagonal, operator)
    next_dot = lax.psum(jnp.sum(residual * next_z * mult_weights), ("gx", "gy"))
    direction = next_z + next_dot / first_dot * first_z
    return (solution, residual, direction)


def solution(mesh):
    placed = (
        P("gx", "gy", None),
        P("gx", "gy", None),
        P("gx", "gy", None),
        P("gx", "gy", None),
        P(),
    )
    return jax.shard_map(
        per_device,
        mesh=mesh,
        in_specs=placed,
        out_specs=(P("gx", "gy", None), P("gx", "gy", None), P("gx", "gy", None)),
        check_vma=False,
    )
```

profile of v0, /device:TPU:1, one launch (start us, length us, event | category | flops | bytes accessed | tf_op | source)
XLA Modules:
  0.0 398.1 jit_solution(5841265896493109897)
XLA Ops:
  3.6 2.6 fusion.125
  12.3 4.3 %broadcast_bitcast_fusion = (f32[16,16,512]{1,2,0:T(8,128)}, f32[1,16,16,512]{2,3,1,0:T(8,128)}) fusion(f32[16,16,64]{1,2,0:T(8,128)S(1)} %copy.189), kind=kLoop, calls=%fused_computation | loop fusion | bytes 1114112 | tf_op jit(solution)/shard_map/reshape | solution.py:169
  16.6 2.9 copy.190
  21.9 4.8 %collective-permute-start = (f32[2,1,16,512]{3,2,1,0:T(8,128)S(1)}, f32[2,1,16,512]{3,2,1,0:T(8,128)S(1)}, u32[]{:S(2)}, u32[]{:S(2)}) collective-permute-start(f32[2,1,16,512]{3,2,1,0:T(8,128)S(1)} %get-tuple-element.15), channel_id=1, source_target_pairs={{0,16},{16,32},{32,48},{48,64},{64,80},{80,96},{96,112},{112,128},... | collective-permute-start | bytes 196616 | tf_op jit(solution)/shard_map/ppermute | solution.py:21
  28.1 4.3 %collective-permute-done.1 = f32[2,1,16,512]{3,2,1,0:T(8,128)S(1)} collective-permute-done((f32[2,1,16,512]{3,2,1,0:T(8,128)S(1)}, f32[2,1,16,512]{3,2,1,0:T(8,128)S(1)}, u32[]{:S(2)}, u32[]{:S(2)}) %collective-permute-start.1) | collective-permute-done | bytes 65568 | tf_op jit(solution)/shard_map/ppermute | solution.py:22
  32.7 4.9 %collective-permute-start.2 = (f32[2,16,1,512]{3,2,1,0:T(1,128)S(1)}, f32[2,16,1,512]{3,2,1,0:T(1,128)S(1)}, u32[]{:S(2)}, u32[]{:S(2)}) collective-permute-start(f32[2,16,1,512]{3,2,1,0:T(1,128)S(1)} %get-tuple-element.13), channel_id=1, source_target_pairs={{0,1},{1,2},{2,3},{3,4},{4,5},{5,6},{6,7},{7,8},{8,9},{9,10},{10,1... | collective-permute-start | bytes 196616 | tf_op jit(solution)/shard_map/ppermute | solution.py:21
  37.7 2.7 collective-permute-start.3
  42.0 2.8 copy.202
  47.5 3.2 slice.282
  50.6 3.2 slice.281
  62.2 3.8 collective-permute-start.4
  67.3 5.2 %collective-permute-done.5 = f32[1,1,16,512]{3,2,1,0:T(8,128)S(1)} collective-permute-done((f32[1,1,16,512]{3,2,1,0:T(8,128)S(1)}, f32[1,1,16,512]{3,2,1,0:T(8,128)S(1)}, u32[]{:S(2)}, u32[]{:S(2)}) %collective-permute-start.5) | collective-permute-done | bytes 32800 | tf_op jit(solution)/shard_map/ppermute | solution.py:22
  72.7 4.8 %collective-permute-start.6 = (f32[1,16,1,512]{3,0,2,1:T(1,128)S(1)}, f32[1,16,1,512]{3,0,2,1:T(1,128)S(1)}, u32[]{:S(2)}, u32[]{:S(2)}) collective-permute-start(f32[1,16,1,512]{3,0,2,1:T(1,128)S(1)} %copy.357), channel_id=1, source_target_pairs={{0,1},{1,2},{2,3},{3,4},{4,5},{5,6},{6,7},{7,8},{8,9},{9,10},{10,1... | collective-permute-start | bytes 98312 | tf_op jit(solution)/shard_map/ppermute | solution.py:21
  90.5 5.4 %collective-permute-start.8 = (f32[1,1,16,512]{3,2,1,0:T(8,128)}, f32[1,1,16,512]{3,2,1,0:T(8,128)}, u32[]{:S(2)}, u32[]{:S(2)}) collective-permute-start(f32[1,1,16,512]{3,2,1,0:T(8,128)} %get-tuple-element.33), channel_id=1, source_target_pairs={{0,16},{16,32},{32,48},{48,64},{64,80},{80,96},{96,112},{112,128},... | collective-permute-start | bytes 98312 | tf_op jit(solution)/shard_map/ppermute | solution.py:21
  102.2 3.5 collective-permute-start.10
  117.7 3.1 collective-permute-start.12
  122.2 3.2 collective-permute-done.13
  125.7 3.3 collective-permute-start.14
  135.7 105.4 %all-reduce = (f32[]{:T(128)}, f32[]{:T(128)}) all-reduce(f32[]{:T(128)} %get-tuple-element.4, f32[]{:T(128)} %get-tuple-element.3), channel_id=1, replica_groups=mesh['gx'=32,'gy'=16] {'gx','gy'}, use_global_device_ids=true, to_apply=%region_1.2 | all-reduce | flops 2 | bytes 16 | tf_op jit(solution)/shard_map/psum | solution.py:217
  252.4 3.3 collective-permute-done.17
  256.0 6.2 %collective-permute-start.18 = (f32[1,16,1,512]{3,0,2,1:T(1,128)S(1)}, f32[1,16,1,512]{3,0,2,1:T(1,128)S(1)}, u32[]{:S(2)}, u32[]{:S(2)}) collective-permute-start(f32[1,16,1,512]{3,0,2,1:T(1,128)S(1)} %copy.363), channel_id=1, source_target_pairs={{0,1},{1,2},{2,3},{3,4},{4,5},{5,6},{6,7},{7,8},{8,9},{9,10},{10,1... | collective-permute-start | bytes 98312 | tf_op jit(solution)/shard_map/ppermute | solution.py:21
  276.7 3.3 collective-permute-done.21
  280.3 3.3 collective-permute-start.22
  290.6 104.6 %psum.23 = f32[]{:T(128)} all-reduce(f32[]{:T(128)} %get-tuple-element.7), channel_id=1, replica_groups=mesh['gx'=32,'gy'=16] {'gx','gy'}, use_global_device_ids=true, to_apply=%region_5.6 | all-reduce | flops 1 | bytes 8 | tf_op jit(solution)/shard_map/psum | solution.py:224
  (253 shorter events, 98.7 us)
Async XLA Ops:
  21.9 6.2 %collective-permute-start = (f32[2,1,16,512]{3,2,1,0:T(8,128)S(1)}, f32[2,1,16,512]{3,2,1,0:T(8,128)S(1)}, u32[]{:S(2)}, u32[]{:S(2)}) collective-permute-start(f32[2,1,16,512]{3,2,1,0:T(8,128)S(1)} %get-tuple-element.15), channel_id=1, source_target_pairs={{0,16},{16,32},{32,48},{48,64},{64,80},{80,96},{96,112},{112,128},... | collective-permute-start | bytes 196616 | tf_op jit(solution)/shard_map/ppermute | solution.py:21
  26.7 5.7 %collective-permute-start.1 = (f32[2,1,16,512]{3,2,1,0:T(8,128)S(1)}, f32[2,1,16,512]{3,2,1,0:T(8,128)S(1)}, u32[]{:S(2)}, u32[]{:S(2)}) collective-permute-start(f32[2,1,16,512]{3,2,1,0:T(8,128)S(1)} %get-tuple-element.16), channel_id=1, source_target_pairs={{16,0},{32,16},{48,32},{64,48},{80,64},{96,80},{112,96},{128,112},... | collective-permute-start | bytes 196616 | tf_op jit(solution)/shard_map/ppermute | solution.py:22
  32.7 13.2 %collective-permute-start.2 = (f32[2,16,1,512]{3,2,1,0:T(1,128)S(1)}, f32[2,16,1,512]{3,2,1,0:T(1,128)S(1)}, u32[]{:S(2)}, u32[]{:S(2)}) collective-permute-start(f32[2,16,1,512]{3,2,1,0:T(1,128)S(1)} %get-tuple-element.13), channel_id=1, source_target_pairs={{0,1},{1,2},{2,3},{3,4},{4,5},{5,6},{6,7},{7,8},{8,9},{9,10},{10,1... | collective-permute-start | bytes 196616 | tf_op jit(solution)/shard_map/ppermute | solution.py:21
  37.7 8.3 %collective-permute-start.3 = (f32[2,16,1,512]{3,2,1,0:T(1,128)S(1)}, f32[2,16,1,512]{3,2,1,0:T(1,128)S(1)}, u32[]{:S(2)}, u32[]{:S(2)}) collective-permute-start(f32[2,16,1,512]{3,2,1,0:T(1,128)S(1)} %get-tuple-element.14), channel_id=1, source_target_pairs={{1,0},{2,1},{3,2},{4,3},{5,4},{6,5},{7,6},{8,7},{9,8},{10,9},{11,1... | collective-permute-start | bytes 196616 | tf_op jit(solution)/shard_map/ppermute | solution.py:22
  62.2 5.1 %collective-permute-start.4 = (f32[1,1,16,512]{3,2,1,0:T(8,128)S(1)}, f32[1,1,16,512]{3,2,1,0:T(8,128)S(1)}, u32[]{:S(2)}, u32[]{:S(2)}) collective-permute-start(f32[1,1,16,512]{3,2,1,0:T(8,128)S(1)} %get-tuple-element.37), channel_id=1, source_target_pairs={{0,16},{16,32},{32,48},{48,64},{64,80},{80,96},{96,112},{112,128},... | collective-permute-start | bytes 98312 | tf_op jit(solution)/shard_map/ppermute | solution.py:21
  65.9 6.5 %collective-permute-start.5 = (f32[1,1,16,512]{3,2,1,0:T(8,128)S(1)}, f32[1,1,16,512]{3,2,1,0:T(8,128)S(1)}, u32[]{:S(2)}, u32[]{:S(2)}) collective-permute-start(f32[1,1,16,512]{3,2,1,0:T(8,128)S(1)} %get-tuple-element.38), channel_id=1, source_target_pairs={{16,0},{32,16},{48,32},{64,48},{80,64},{96,80},{112,96},{128,112},... | collective-permute-start | bytes 98312 | tf_op jit(solution)/shard_map/ppermute | solution.py:22
  72.7 7.0 %collective-permute-start.6 = (f32[1,16,1,512]{3,0,2,1:T(1,128)S(1)}, f32[1,16,1,512]{3,0,2,1:T(1,128)S(1)}, u32[]{:S(2)}, u32[]{:S(2)}) collective-permute-start(f32[1,16,1,512]{3,0,2,1:T(1,128)S(1)} %copy.357), channel_id=1, source_target_pairs={{0,1},{1,2},{2,3},{3,4},{4,5},{5,6},{6,7},{7,8},{8,9},{9,10},{10,1... | collective-permute-start | bytes 98312 | tf_op jit(solution)/shard_map/ppermute | solution.py:21
  77.5 5.2 %collective-permute-start.7 = (f32[1,16,1,512]{3,0,2,1:T(1,128)S(1)}, f32[1,16,1,512]{3,0,2,1:T(1,128)S(1)}, u32[]{:S(2)}, u32[]{:S(2)}) collective-permute-start(f32[1,16,1,512]{3,0,2,1:T(1,128)S(1)} %copy.358), channel_id=1, source_target_pairs={{1,0},{2,1},{3,2},{4,3},{5,4},{6,5},{7,6},{8,7},{9,8},{10,9},{11,1... | collective-permute-start | bytes 98312 | tf_op jit(solution)/shard_map/ppermute | solution.py:22
  90.5 7.8 %collective-permute-start.8 = (f32[1,1,16,512]{3,2,1,0:T(8,128)}, f32[1,1,16,512]{3,2,1,0:T(8,128)}, u32[]{:S(2)}, u32[]{:S(2)}) collective-permute-start(f32[1,1,16,512]{3,2,1,0:T(8,128)} %get-tuple-element.33), channel_id=1, source_target_pairs={{0,16},{16,32},{32,48},{48,64},{64,80},{80,96},{96,112},{112,128},... | collective-permute-start | bytes 98312 | tf_op jit(solution)/shard_map/ppermute | solution.py:21
  95.9 5.0 %collective-permute-start.9 = (f32[1,1,16,512]{3,2,1,0:T(8,128)}, f32[1,1,16,512]{3,2,1,0:T(8,128)}, u32[]{:S(2)}, u32[]{:S(2)}) collective-permute-start(f32[1,1,16,512]{3,2,1,0:T(8,128)} %get-tuple-element.34), channel_id=1, source_target_pairs={{16,0},{32,16},{48,32},{64,48},{80,64},{96,80},{112,96},{128,112},... | collective-permute-start | bytes 98312 | tf_op jit(solution)/shard_map/ppermute | solution.py:22
  102.2 5.8 %collective-permute-start.10 = (f32[1,16,1,512]{3,0,2,1:T(1,128)S(1)}, f32[1,16,1,512]{3,0,2,1:T(1,128)S(1)}, u32[]{:S(2)}, u32[]{:S(2)}) collective-permute-start(f32[1,16,1,512]{3,0,2,1:T(1,128)S(1)} %copy.359), channel_id=1, source_target_pairs={{0,1},{1,2},{2,3},{3,4},{4,5},{5,6},{6,7},{7,8},{8,9},{9,10},{10,1... | collective-permute-start | bytes 98312 | tf_op jit(solution)/shard_map/ppermute | solution.py:21
  105.8 5.2 %collective-permute-start.11 = (f32[1,16,1,512]{3,0,2,1:T(1,128)S(1)}, f32[1,16,1,512]{3,0,2,1:T(1,128)S(1)}, u32[]{:S(2)}, u32[]{:S(2)}) collective-permute-start(f32[1,16,1,512]{3,0,2,1:T(1,128)S(1)} %copy.360), channel_id=1, source_target_pairs={{1,0},{2,1},{3,2},{4,3},{5,4},{6,5},{7,6},{8,7},{9,8},{10,9},{11,1... | collective-permute-start | bytes 98312 | tf_op jit(solution)/shard_map/ppermute | solution.py:22
  117.7 4.5 %collective-permute-start.12 = (f32[1,1,16,512]{3,2,1,0:T(8,128)S(1)}, f32[1,1,16,512]{3,2,1,0:T(8,128)S(1)}, u32[]{:S(2)}, u32[]{:S(2)}) collective-permute-start(f32[1,1,16,512]{3,2,1,0:T(8,128)S(1)} %get-tuple-element.29), channel_id=1, source_target_pairs={{0,16},{16,32},{32,48},{48,64},{64,80},{80,96},{96,112},{112,128},... | collective-permute-start | bytes 98312 | tf_op jit(solution)/shard_map/ppermute | solution.py:21
  120.8 4.7 %collective-permute-start.13 = (f32[1,1,16,512]{3,2,1,0:T(8,128)S(1)}, f32[1,1,16,512]{3,2,1,0:T(8,128)S(1)}, u32[]{:S(2)}, u32[]{:S(2)}) collective-permute-start(f32[1,1,16,512]{3,2,1,0:T(8,128)S(1)} %get-tuple-element.30), channel_id=1, source_target_pairs={{16,0},{32,16},{48,32},{64,48},{80,64},{96,80},{112,96},{128,112},... | collective-permute-start | bytes 98312 | tf_op jit(solution)/shard_map/ppermute | solution.py:22
  125.7 5.4 %collective-permute-start.14 = (f32[1,16,1,512]{3,0,2,1:T(1,128)S(1)}, f32[1,16,1,512]{3,0,2,1:T(1,128)S(1)}, u32[]{:S(2)}, u32[]{:S(2)}) collective-permute-start(f32[1,16,1,512]{3,0,2,1:T(1,128)S(1)} %copy.361), channel_id=1, source_target_pairs={{0,1},{1,2},{2,3},{3,4},{4,5},{5,6},{6,7},{7,8},{8,9},{9,10},{10,1... | collective-permute-start | bytes 98312 | tf_op jit(solution)/shard_map/ppermute | solution.py:21
  129.1 5.2 %collective-permute-start.15 = (f32[1,16,1,512]{3,0,2,1:T(1,128)S(1)}, f32[1,16,1,512]{3,0,2,1:T(1,128)S(1)}, u32[]{:S(2)}, u32[]{:S(2)}) collective-permute-start(f32[1,16,1,512]{3,0,2,1:T(1,128)S(1)} %copy.362), channel_id=1, source_target_pairs={{1,0},{2,1},{3,2},{4,3},{5,4},{6,5},{7,6},{8,7},{9,8},{10,9},{11,1... | collective-permute-start | bytes 98312 | tf_op jit(solution)/shard_map/ppermute | solution.py:22
  249.8 2.6 collective-permute-start.16
  251.1 4.7 %collective-permute-start.17 = (f32[1,1,16,512]{3,2,1,0:T(8,128)S(1)}, f32[1,1,16,512]{3,2,1,0:T(8,128)S(1)}, u32[]{:S(2)}, u32[]{:S(2)}) collective-permute-start(f32[1,1,16,512]{3,2,1,0:T(8,128)S(1)} %get-tuple-element.26), channel_id=1, source_target_pairs={{16,0},{32,16},{48,32},{64,48},{80,64},{96,80},{112,96},{128,112},... | collective-permute-start | bytes 98312 | tf_op jit(solution)/shard_map/ppermute | solution.py:22
  256.0 8.5 %collective-permute-start.18 = (f32[1,16,1,512]{3,0,2,1:T(1,128)S(1)}, f32[1,16,1,512]{3,0,2,1:T(1,128)S(1)}, u32[]{:S(2)}, u32[]{:S(2)}) collective-permute-start(f32[1,16,1,512]{3,0,2,1:T(1,128)S(1)} %copy.363), channel_id=1, source_target_pairs={{0,1},{1,2},{2,3},{3,4},{4,5},{5,6},{6,7},{7,8},{8,9},{9,10},{10,1... | collective-permute-start | bytes 98312 | tf_op jit(solution)/shard_map/ppermute | solution.py:21
  262.2 5.2 %collective-permute-start.19 = (f32[1,16,1,512]{3,0,2,1:T(1,128)S(1)}, f32[1,16,1,512]{3,0,2,1:T(1,128)S(1)}, u32[]{:S(2)}, u32[]{:S(2)}) collective-permute-start(f32[1,16,1,512]{3,0,2,1:T(1,128)S(1)} %copy.364), channel_id=1, source_target_pairs={{1,0},{2,1},{3,2},{4,3},{5,4},{6,5},{7,6},{8,7},{9,8},{10,9},{11,1... | collective-permute-start | bytes 98312 | tf_op jit(solution)/shard_map/ppermute | solution.py:22
  273.7 3.0 collective-permute-start.20
  275.4 4.7 %collective-permute-start.21 = (f32[1,1,16,512]{3,2,1,0:T(8,128)S(1)}, f32[1,1,16,512]{3,2,1,0:T(8,128)S(1)}, u32[]{:S(2)}, u32[]{:S(2)}) collective-permute-start(f32[1,1,16,512]{3,2,1,0:T(8,128)S(1)} %get-tuple-element.22), channel_id=1, source_target_pairs={{16,0},{32,16},{48,32},{64,48},{80,64},{96,80},{112,96},{128,112},... | collective-permute-start | bytes 98312 | tf_op jit(solution)/shard_map/ppermute | solution.py:22
  280.3 5.4 %collective-permute-start.22 = (f32[1,16,1,512]{3,0,2,1:T(1,128)S(1)}, f32[1,16,1,512]{3,0,2,1:T(1,128)S(1)}, u32[]{:S(2)}, u32[]{:S(2)}) collective-permute-start(f32[1,16,1,512]{3,0,2,1:T(1,128)S(1)} %copy.365), channel_id=1, source_target_pairs={{0,1},{1,2},{2,3},{3,4},{4,5},{5,6},{6,7},{7,8},{8,9},{9,10},{10,1... | collective-permute-start | bytes 98312 | tf_op jit(solution)/shard_map/ppermute | solution.py:21
  283.7 5.2 %collective-permute-start.23 = (f32[1,16,1,512]{3,0,2,1:T(1,128)S(1)}, f32[1,16,1,512]{3,0,2,1:T(1,128)S(1)}, u32[]{:S(2)}, u32[]{:S(2)}) collective-permute-start(f32[1,16,1,512]{3,0,2,1:T(1,128)S(1)} %copy.366), channel_id=1, source_target_pairs={{1,0},{2,1},{3,2},{4,3},{5,4},{6,5},{7,6},{8,7},{9,8},{10,9},{11,1... | collective-permute-start | bytes 98312 | tf_op jit(solution)/shard_map/ppermute | solution.py:22
  (29 other events, 305.1 us)
where the time goes:
time: 405 us; the launch traced here: 398 us
  blocking collectives  210 us (52%)
  starting transfers between devices  66.8 us (16%)
  waiting for transfers between devices  34.4 us (8%)
  local copies, waits for them, and re-layouts  33.8 us (8%)
  matrix products  29.8 us (7%)
  other arithmetic  17.9 us (4%)
  between operations  5.41 us (1%)
    psum x1, blocking collectives, per_device(): lax.psum(jnp.sum(first_res * first_z * mult_weights), ('gx', 'gy'))  105 us
    psum x1, blocking collectives, per_device(): next_dot = lax.psum(jnp.sum(residual * next_z * mult_weights), ('gx', 'gy'))  105 us
    ppermute x12, starting transfers between devices, padded_2(): before = lax.ppermute(last, axis, up)  46.1 us
    ppermute x12, waiting for transfers between devices, padded_2(): after = lax.ppermute(first, axis, down)  34.4 us
    ppermute x12, starting transfers between devices, padded_2(): after = lax.ppermute(first, axis, down)  20.7 us
    reshape x3, local copies, waits for them, and re-layouts, node_kappa(): jnp.repeat(jnp.repeat(jnp.repeat(element_kappa, 8, axis=0), 8, axis=1), 8...  9.96 us
  transfers between devices with their start and end apart: 24, of which 11 were waited for; matrix products, arithmetic and copies ran while one was open for 3% of the time, Pallas kernels for 0%

commit v1 on v0

v1 whole, which is shorter than its diff:
```python
import jax
import jax.numpy as jnp
import ml_dtypes
import numpy as np
from jax import lax
from jax.experimental import pallas as pl
from jax.experimental.pallas import tpu as pltpu
from jax.sharding import PartitionSpec as P

NREG = 3
CENTER = 24.0
HALF = 23.0
RHO0 = HALF / CENTER
RHO1 = 1.0 / (2.0 * CENTER / HALF - RHO0)
RHO2 = 1.0 / (2.0 * CENTER / HALF - RHO1)
MIX1, GAIN1 = RHO1 * RHO0, 2.0 * RHO1 / HALF
MIX2, GAIN2 = RHO2 * RHO1, 2.0 * RHO2 / HALF

F32 = jnp.float32
BF16 = jnp.bfloat16
ROWS, COLS = 256, 512


def gll_tables():
    nodes = np.array(
        [
            -1.0,
            -0.8717401485096066,
            -0.5917001814331423,
            -0.2092992179024789,
            0.2092992179024789,
            0.5917001814331423,
            0.8717401485096066,
            1.0,
        ]
    )
    prev = np.ones(8)
    now = nodes.copy()
    for degree in range(1, 7):
        prev, now = now, ((2 * degree + 1) * nodes * now - degree * prev) / (degree + 1)
    weights = 2.0 / (56.0 * now**2)
    table = np.zeros((8, 8))
    for a in range(8):
        for b in range(8):
            if a != b:
                table[a, b] = now[a] / (now[b] * (nodes[a] - nodes[b]))
    table[0, 0] = -14.0
    table[7, 7] = 14.0
    return table, weights


def split_np(mat):
    high = mat.astype(ml_dtypes.bfloat16)
    low = (mat - high.astype(np.float64)).astype(ml_dtypes.bfloat16)
    return high, low


def left_pair(mat):
    high, low = split_np(mat)
    return np.stack([np.concatenate([high, high], 1), np.concatenate([low, low], 1)])


def right_pair(mat):
    high, low = split_np(mat)
    both = np.concatenate([high, low], 1)
    return np.concatenate([both, both], 0)


def constants():
    table, weights = gll_tables()
    table = table.astype(np.float32).astype(np.float64)
    weights = weights.astype(np.float32)
    eye8, eye2, eye16 = np.eye(8), np.eye(2), np.eye(16)
    d_x = np.kron(table, eye16)
    d_y = np.kron(eye8, np.kron(eye2, table))
    square = (table * table).astype(np.float32).astype(np.float64)
    q_x = np.kron(square, eye16)
    q_y = np.kron(eye8, np.kron(eye2, square))
    d_z = np.kron(eye16, table)
    q_z = np.kron(eye16, square)
    grad = left_pair(np.concatenate([d_x, d_y], 0))
    back_h, back_l = split_np(np.concatenate([d_x.T, d_y.T], 1))
    back = np.stack([back_h, back_l])
    sq = left_pair(q_x.T + q_y.T)
    grad_z = right_pair(d_z.T)
    back_z = right_pair(d_z)
    sq_z = right_pair(q_z)
    w_xy = (weights[:, None] * weights[None, :]).astype(np.float32)
    w_xy = np.tile(w_xy, (2, 2)).reshape(ROWS, 1)
    w_rows = np.ascontiguousarray(np.broadcast_to(w_xy, (ROWS, 128)))
    w_z = np.tile(weights, COLS // 8).reshape(1, COLS).astype(np.float32)
    return dict(grad=grad, back=back, sq=sq, grad_z=grad_z, back_z=back_z, sq_z=sq_z, w_rows=w_rows, w_z=w_z)


def dot(a, b):
    return lax.dot_general(a, b, (((1,), (0,)), ((), ())), preferred_element_type=F32)


def halves(v):
    high = v.astype(BF16)
    low = (v - high.astype(F32)).astype(BF16)
    return high, low


def mul_z(high, low, mat):
    outs = []
    for k in range(COLS // 128):
        part = slice(128 * k, 128 * (k + 1))
        both = dot(jnp.concatenate([high[:, part], low[:, part]], 1), mat)
        outs.append(both[:, :128] + both[:, 128:])
    return jnp.concatenate(outs, 1)


def local_op(v, coef, react, grad, back, grad_z, back_z):
    high, low = halves(v)
    rows = []
    for e in range(2):
        part = slice(128 * e, 128 * (e + 1))
        pair = jnp.concatenate([high[part], low[part]], 0)
        flux = dot(grad[0], pair) + dot(grad[1], pair)
        c = coef[part]
        f_h, f_l = halves(flux * jnp.concatenate([c, c], 0))
        rows.append(dot(back[0], f_h) + (dot(back[0], f_l) + dot(back[1], f_h)))
    out = jnp.concatenate(rows, 0)
    flux_z = mul_z(high, low, grad_z) * coef
    return out + mul_z(*halves(flux_z), back_z) + react * v


def join_z(f):
    lane = lax.broadcasted_iota(jnp.int32, (1, COLS), 1)
    upper = ((lane % 8) == 7) & (lane != COLS - 1)
    lower = ((lane % 8) == 0) & (lane != 0)
    nxt = pltpu.roll(f, COLS - 1, 1)
    prv = pltpu.roll(f, 1, 1)
    return f + jnp.where(upper, nxt, jnp.where(lower, prv, 0.0))


def emit_partial(f, p_ref, x_ref, y_ref):
    p_ref[...] = join_z(f)
    p_ref[112:128, :] = p_ref[112:128, :] + p_ref[128:144, :]
    p_ref[128:144, :] = p_ref[112:128, :]
    for x in range(16):
        r = 16 * x
        mid = p_ref[r + 7:r + 8, :] + p_ref[r + 8:r + 9, :]
        p_ref[r + 7:r + 8, :] = mid
        p_ref[r + 8:r + 9, :] = mid
        y_ref[0, x:x + 1, :] = p_ref[r:r + 1, :]
        y_ref[1, x:x + 1, :] = p_ref[r + 15:r + 16, :]
    x_ref[0] = p_ref[0:16, :]
    x_ref[1] = p_ref[240:256, :]


def take_sum(p_ref, recv, s_ref):
    left, right, below, above = recv
    s_ref[...] = p_ref[...]
    s_ref[0:16, :] = s_ref[0:16, :] + left
    s_ref[240:256, :] = s_ref[240:256, :] + right
    for x in range(16):
        r = 16 * x
        s_ref[r:r + 1, :] = s_ref[r:r + 1, :] + below[x:x + 1, :]
        s_ref[r + 15:r + 16, :] = s_ref[r + 15:r + 16, :] + above[x:x + 1, :]
    return s_ref[...]


def fold(prod):
    part = prod.reshape(ROWS // 8, 8, COLS).sum(axis=0)
    return part[:, 0:128] + part[:, 128:256] + part[:, 256:384] + part[:, 384:512]


def first_kernel(table_ref, load_ref, cond_ref, region_ref, sq_ref, sqz_ref, wr_ref, wz_ref,
                 coef_ref, react_ref, pl_ref, pd_ref, x_ref, y_ref):
    w_row = wr_ref[...]
    w_row = jnp.concatenate([w_row] * 4, axis=1)
    quad_z = wz_ref[...]
    coef = (w_row * quad_z) * cond_ref[...].reshape(ROWS, COLS).astype(F32)
    coef_ref[...] = coef
    elem = lax.broadcasted_iota(jnp.int32, (COLS // 8, COLS), 0)
    lane = lax.broadcasted_iota(jnp.int32, (COLS // 8, COLS), 1)
    spread = (lane // 8 == elem).astype(F32)
    for ex in range(2):
        ids = region_ref[ex]
        kappa = jnp.zeros(ids.shape, F32)
        for k in range(NREG):
            kappa = kappa + jnp.where(ids == k, table_ref[k], 0.0)
        kappa = lax.dot_general(kappa, spread, (((1,), (0,)), ((), ())),
                                precision=lax.Precision.HIGHEST, preferred_element_type=F32)
        for x in range(8):
            for ey in range(2):
                r = (ex * 8 + x) * 16 + ey * 8
                react_ref[r:r + 8, :] = (w_row[r:r + 8] * quad_z) * kappa[ey:ey + 1, :]
    high, low = halves(coef)
    rows = []
    for e in range(2):
        part = slice(128 * e, 128 * (e + 1))
        pair = jnp.concatenate([high[part], low[part]], 0)
        rows.append(dot(sq_ref[0], pair) + dot(sq_ref[1], pair))
    diag = jnp.concatenate(rows, 0) + mul_z(high, low, sqz_ref[...]) + react_ref[...]
    emit_partial(diag, pd_ref, x_ref.at[1], y_ref.at[1])
    emit_partial(load_ref[...].reshape(ROWS, COLS), pl_ref, x_ref.at[0], y_ref.at[0])


def second_kernel(pl_ref, pd_ref, xl_ref, xr_ref, yb_ref, ya_ref, flags_ref, coef_ref, react_ref,
                  grad_ref, back_ref, gz_ref, bz_ref,
                  r_ref, dinv_ref, p_ref, x_ref, y_ref, s_ref):
    diag = take_sum(pd_ref, (xl_ref[1], xr_ref[1], yb_ref[1], ya_ref[1]), s_ref)
    dinv_ref[...] = 1.0 / diag
    keep = (1 - flags_ref[...].reshape(ROWS, 128)).astype(F32)
    dinv_ref[:, 0:128] = keep * dinv_ref[:, 0:128]
    r = take_sum(pl_ref, (xl_ref[0], xr_ref[0], yb_ref[0], ya_ref[0]), s_ref)
    r_ref[...] = r
    r_ref[:, 0:128] = keep * r_ref[:, 0:128]
    a0 = dinv_ref[...] * r_ref[...] * (1.0 / CENTER)
    f = local_op(a0, coef_ref[...], react_ref[...], grad_ref, back_ref, gz_ref[...], bz_ref[...])
    emit_partial(f, p_ref, x_ref, y_ref)


def sweep1_kernel(pin_ref, xl_ref, xr_ref, yb_ref, ya_ref, r_ref, dinv_ref, coef_ref, react_ref,
                  grad_ref, back_ref, gz_ref, bz_ref,
                  a1_ref, p_ref, x_ref, y_ref, s_ref):
    image = take_sum(pin_ref, (xl_ref[0], xr_ref[0], yb_ref[0], ya_ref[0]), s_ref)
    dinv, r = dinv_ref[...], r_ref[...]
    a0 = dinv * r * (1.0 / CENTER)
    a1 = (1.0 + MIX1) * a0 + GAIN1 * (dinv * (r - image))
    a1_ref[...] = a1
    f = local_op(a1, coef_ref[...], react_ref[...], grad_ref, back_ref, gz_ref[...], bz_ref[...])
    emit_partial(f, p_ref, x_ref, y_ref)


def sweep2(image, a1, r, dinv):
    a0 = dinv * r * (1.0 / CENTER)
    return a1 + (MIX2 * (a1 - a0) + GAIN2 * (dinv * (r - image)))


def third_kernel(pin_ref, xl_ref, xr_ref, yb_ref, ya_ref, r_ref, dinv_ref, a1_ref, load_ref, coef_ref, react_ref,
                 grad_ref, back_ref, gz_ref, bz_ref,
                 z_ref, p_ref, x_ref, y_ref, dots_ref, s_ref):
    image = take_sum(pin_ref, (xl_ref[0], xr_ref[0], yb_ref[0], ya_ref[0]), s_ref)
    z = sweep2(image, a1_ref[...], r_ref[...], dinv_ref[...])
    z_ref[...] = z
    dots_ref[0] = fold(load_ref[...].reshape(ROWS, COLS) * z)
    f = local_op(z, coef_ref[...], react_ref[...], grad_ref, back_ref, gz_ref[...], bz_ref[...])
    dots_ref[1] = fold(f * z)
    emit_partial(f, p_ref, x_ref, y_ref)


def fourth_kernel(pin_ref, xl_ref, xr_ref, yb_ref, ya_ref, dinv_ref, z_ref, coef_ref, react_ref,
                  grad_ref, back_ref, gz_ref, bz_ref,
                  im_ref, p_ref, x_ref, y_ref, dots_ref, s_ref):
    image = take_sum(pin_ref, (xl_ref[0], xr_ref[0], yb_ref[0], ya_ref[0]), s_ref)
    dinv = dinv_ref[...]
    im = jnp.where(dinv != 0.0, image, 0.0)
    im_ref[...] = im
    b0 = dinv * im * (1.0 / CENTER)
    f = local_op(b0, coef_ref[...], react_ref[...], grad_ref, back_ref, gz_ref[...], bz_ref[...])
    dots_ref[...] = fold(f * z_ref[...])
    emit_partial(f, p_ref, x_ref, y_ref)


def fifth_kernel(pin_ref, xl_ref, xr_ref, yb_ref, ya_ref, im_ref, dinv_ref, z_ref, d34_ref, d5_ref, coef_ref, react_ref,
                 grad_ref, back_ref, gz_ref, bz_ref,
                 b1_ref, p_ref, x_ref, y_ref, dots_ref, s_ref):
    image = take_sum(pin_ref, (xl_ref[0], xr_ref[0], yb_ref[0], ya_ref[0]), s_ref)
    dinv, im = dinv_ref[...], im_ref[...]
    b0 = dinv * im * (1.0 / CENTER)
    b1 = (1.0 + MIX1) * b0 + GAIN1 * (dinv * (im - image))
    b1_ref[...] = b1
    f = local_op(b1, coef_ref[...], react_ref[...], grad_ref, back_ref, gz_ref[...], bz_ref[...])
    emit_partial(f, p_ref, x_ref, y_ref)
    last = fold(f * ((1.0 + MIX2) * z_ref[...] - (CENTER * GAIN2) * b0))
    both = last + (CENTER * GAIN2 - MIX2) * d5_ref[...]
    lane = lax.broadcasted_iota(jnp.int32, (1, 128), 1)
    dots_ref[...] = jnp.where(
        lane == 0, jnp.sum(d34_ref[0]), jnp.where(lane == 1, jnp.sum(d34_ref[1]), jnp.sum(both)))


def last_kernel(dots_ref, pin_ref, xl_ref, xr_ref, yb_ref, ya_ref, im_ref, dinv_ref, b1_ref, z_ref, r_ref,
                sol_ref, res_ref, dir_ref, s_ref):
    first, curv, quad = dots_ref[0], dots_ref[1], dots_ref[2]
    step = first / curv
    ratio = (first - 2.0 * step * curv + step * step * quad) / first
    image = take_sum(pin_ref, (xl_ref[0], xr_ref[0], yb_ref[0], ya_ref[0]), s_ref)
    im = im_ref[...]
    b2 = sweep2(image, b1_ref[...], im, dinv_ref[...])
    z = z_ref[...]
    shape = (16, 16, COLS)
    sol_ref[...] = (step * z).reshape(shape)
    res_ref[...] = (r_ref[...] - step * im).reshape(shape)
    dir_ref[...] = ((z - step * b2) + ratio * z).reshape(shape)


VM = pl.BlockSpec(memory_space=pltpu.VMEM)
SM = pl.BlockSpec(memory_space=pltpu.SMEM)
BIG = jax.ShapeDtypeStruct((ROWS, COLS), F32)
FACES = jax.ShapeDtypeStruct((2, 16, COLS), F32)
SCRATCH = [pltpu.VMEM((ROWS, COLS), F32)]
PARAMS = pltpu.CompilerParams(vmem_limit_bytes=24 << 20)


def call(kernel, outs, n_in, smem_first=False, scratch=True):
    specs = [VM] * n_in
    if smem_first:
        specs[0] = SM
    return pl.pallas_call(
        kernel, out_shape=outs, in_specs=specs, out_specs=jax.tree.map(lambda _: VM, outs),
        scratch_shapes=SCRATCH if scratch else [], compiler_params=PARAMS)


def per_device(load, conductivity, flags, region, kappa_table):
    k = {name: jnp.asarray(value) for name, value in constants().items()}
    mats = (k["grad"], k["back"], k["grad_z"], k["back_z"])
    n_x, n_y = lax.axis_size("gx"), lax.axis_size("gy")
    up_x = [(i, i + 1) for i in range(n_x - 1)]
    up_y = [(i, i + 1) for i in range(n_y - 1)]
    down_x = [(j, i) for i, j in up_x]
    down_y = [(j, i) for i, j in up_y]

    def exchange(faces_x, faces_y):
        left = lax.ppermute(faces_x[:, 1], "gx", up_x)
        right = lax.ppermute(faces_x[:, 0], "gx", down_x)

        def with_corners(side, row):
            face = faces_y[:, side]
            fields = face.shape[0]
            inner = jnp.zeros((fields, 14, COLS), F32)
            return face + jnp.concatenate([left[:, row:row + 1], inner, right[:, row:row + 1]], axis=1)

        below = lax.ppermute(with_corners(1, 15), "gy", up_y)
        above = lax.ppermute(with_corners(0, 0), "gy", down_y)
        return left, right, below, above

    two = jax.ShapeDtypeStruct((2, 2, 16, COLS), F32)
    coef, react, part_l, part_d, fx, fy = call(first_kernel, (BIG, BIG, BIG, BIG, two, two), 8, True, False)(
        kappa_table, load, conductivity, region, k["sq"], k["sq_z"], k["w_rows"], k["w_z"])
    recv = exchange(fx, fy)
    flags0 = lax.slice_in_dim(flags, 0, 128, axis=2)
    r, dinv, part, fx, fy = call(second_kernel, (BIG, BIG, BIG, FACES, FACES), 13)(
        part_l, part_d, *recv, flags0, coef, react, *mats)
    recv = exchange(fx[None], fy[None])
    a1, part, fx, fy = call(sweep1_kernel, (BIG, BIG, FACES, FACES), 13)(part, *recv, r, dinv, coef, react, *mats)
    recv = exchange(fx[None], fy[None])
    z, part, fx, fy, d34 = call(
        third_kernel, (BIG, BIG, FACES, FACES, jax.ShapeDtypeStruct((2, 8, 128), F32)), 15)(
        part, *recv, r, dinv, a1, load, coef, react, *mats)
    recv = exchange(fx[None], fy[None])
    im, part, fx, fy, d5 = call(fourth_kernel, (BIG, BIG, FACES, FACES, jax.ShapeDtypeStruct((8, 128), F32)), 13)(
        part, *recv, dinv, z, coef, react, *mats)
    recv = exchange(fx[None], fy[None])
    b1, part, fx, fy, dots = call(fifth_kernel, (BIG, BIG, FACES, FACES, jax.ShapeDtypeStruct((1, 128), F32)), 16)(
        part, *recv, im, dinv, z, d34, d5, coef, react, *mats)
    total = lax.all_to_all(jnp.broadcast_to(dots, (n_y, 128)), "gy", 0, 0, tiled=True).sum(0)
    total = lax.all_to_all(jnp.broadcast_to(total, (n_x, 128)), "gx", 0, 0, tiled=True).sum(0)
    recv = exchange(fx[None], fy[None])
    shape = jax.ShapeDtypeStruct((16, 16, COLS), F32)
    return call(last_kernel, (shape, shape, shape), 11, True)(
        total, part, *recv, im, dinv, b1, z, r)


def solution(mesh):
    placed = P("gx", "gy", None)
    return jax.shard_map(
        per_device,
        mesh=mesh,
        in_specs=(placed, placed, placed, placed, P()),
        out_specs=(placed, placed, placed),
        check_vma=False,
    )
```

time: 405 us -> 160 us (0.40); the launches traced: 398 us -> 159 us
  blocking collectives: 210 us -> 30.7 us
  matrix products: 29.8 us -> 0 us
  starting transfers between devices: 66.8 us -> 95.3 us
  local copies, waits for them, and re-layouts: 33.8 us -> 8.47 us
  waiting for transfers between devices: 34.4 us -> 10.5 us
  other arithmetic: 17.9 us -> 0.51 us
  Pallas kernels: 0 us -> 12 us
  between operations: 5.41 us -> 1.13 us
    psum x2 -> x0, blocking collectives: 210 us -> none  [the longest x1 105 us: per_device(): lax.psum(jnp.sum(first_res * first_z * mult_weights), ('gx', 'gy'))]
    all_to_all x0 -> x1, blocking collectives: none -> 30.7 us  [per_device(): lax.all_to_all(jnp.broadcast_to(total, (n_x, 128)), 'gx', 0, 0, tiled=True)]
    dot_general x39 -> x0, matrix products: 29.8 us -> none  [the longest x6 6.09 us: assemble_nodes(): jnp.einsum('kxyz,zw->kxyw', stacked, pair_matrix, precision=lax.Precision...]
    ppermute x24, waiting for transfers between devices: 34.4 us -> 10.5 us  [the longest x6 6.11 us: exchange(): left = lax.ppermute(faces_x[:, 1], 'gx', up_x)]
    ppermute x24, starting transfers between devices: 66.8 us -> 82.3 us  [the longest x6 29.6 us: exchange(): left = lax.ppermute(faces_x[:, 1], 'gx', up_x)]
    all_to_all x0 -> x1, starting transfers between devices: none -> 13 us  [per_device(): lax.all_to_all(jnp.broadcast_to(dots, (n_y, 128)), 'gy', 0, 0, tiled=True)]
    pallas_call x0 -> x7, Pallas kernels: none -> 12 us  [the longest x1 2.07 us: per_device(): call(last_kernel, (shape, shape, shape), 11, True)]
    slice x27 -> x13, local copies, waits for them, and re-layouts: 11.4 us -> 0.99 us  [the longest x1 0.92 us: per_device(): flags0 = lax.slice_in_dim(flags, 0, 128, axis=2)]
  transfers between devices with their start and end apart: 24 -> 25, of which waited for: 11 -> 11; matrix products, arithmetic and copies ran while one was open for 3% -> 1% of each run, Pallas kernels for 0% -> 0%
where the time goes in v1:
time: 160 us; the launch traced here: 159 us
  starting transfers between devices  95.3 us (60%)
  blocking collectives  30.7 us (19%)
  Pallas kernels  12 us (8%)
  waiting for transfers between devices  10.5 us (7%)
  local copies, waits for them, and re-layouts  8.47 us (5%)
    all_to_all x1, blocking collectives, per_device(): lax.all_to_all(jnp.broadcast_to(total, (n_x, 128)), 'gx', 0, 0, tiled=True)  30.7 us
    ppermute x6, starting transfers between devices, exchange(): left = lax.ppermute(faces_x[:, 1], 'gx', up_x)  29.6 us
    ppermute x6, starting transfers between devices, exchange(): below = lax.ppermute(with_corners(1, 15), 'gy', up_y)  24.9 us
    ppermute x6, starting transfers between devices, exchange(): above = lax.ppermute(with_corners(0, 0), 'gy', down_y)  19.9 us
    all_to_all x1, starting transfers between devices, per_device(): lax.all_to_all(jnp.broadcast_to(dots, (n_y, 128)), 'gy', 0, 0, tiled=True)  13 us
    ppermute x6, starting transfers between devices, exchange(): right = lax.ppermute(faces_x[:, 0], 'gx', down_x)  7.88 us
    unnamed x26, local copies, waits for them, and re-layouts  6.74 us
    ppermute x6, waiting for transfers between devices, exchange(): left = lax.ppermute(faces_x[:, 1], 'gx', up_x)  6.11 us
  transfers between devices with their start and end apart: 25, of which 11 were waited for; matrix products, arithmetic and copies ran while one was open for 1% of the time, Pallas kernels for 0%

profile of v1, /device:TPU:1, one launch (start us, length us, event | category | flops | bytes accessed | tf_op | source)
XLA Modules:
  0.0 158.6 jit_solution(17394405650057112450)
XLA Ops:
  10.4 5.5 %collective-permute-start = (f32[2,16,512]{2,1,0:T(8,128)S(1)}, f32[2,16,512]{2,1,0:T(8,128)S(1)}, u32[]{:S(2)}, u32[]{:S(2)}) collective-permute-start(f32[2,16,512]{2,1,0:T(8,128)S(1)} %get-tuple-element.66), channel_id=1, source_target_pairs={{0,16},{16,32},{32,48},{48,64},{64,80},{80,96},{96,112},{112,128},... | collective-permute-start | bytes 196616 | tf_op jit(solution)/shard_map/ppermute | solution.py:318
  17.3 8.5 %collective-permute-start.3 = (f32[2,16,512]{2,1,0:T(8,128)S(1)}, f32[2,16,512]{2,1,0:T(8,128)S(1)}, u32[]{:S(2)}, u32[]{:S(2)}) collective-permute-start(f32[2,16,512]{2,1,0:T(8,128)S(1)} %get-tuple-element.63), channel_id=1, source_target_pairs={{1,0},{2,1},{3,2},{4,3},{5,4},{6,5},{7,6},{8,7},{9,8},{10,9},{11,1... | collective-permute-start | bytes 196616 | tf_op jit(solution)/shard_map/ppermute | solution.py:328
  25.8 2.1 %collective-permute-start.2 = (f32[2,16,512]{2,1,0:T(8,128)S(1)}, f32[2,16,512]{2,1,0:T(8,128)S(1)}, u32[]{:S(2)}, u32[]{:S(2)}) collective-permute-start(f32[2,16,512]{2,1,0:T(8,128)S(1)} %get-tuple-element.64), channel_id=1, source_target_pairs={{0,1},{1,2},{2,3},{3,4},{4,5},{5,6},{6,7},{7,8},{8,9},{9,10},{10,1... | collective-permute-start | bytes 196616 | tf_op jit(solution)/shard_map/ppermute | solution.py:327
  29.1 1.7 %shard_map.149 = (f32[256,512]{1,0:T(8,128)S(1)}, f32[256,512]{1,0:T(8,128)S(1)}, f32[256,512]{1,0:T(8,128)S(1)}, f32[2,16,512]{2,1,0:T(8,128)S(1)}, f32[2,16,512]{2,1,0:T(8,128)S(1)}) custom-call(f32[256,512]{1,0:T(8,128)S(1)} %get-tuple-element.33.pl_ref, f32[256,512]{1,0:T(8,128)S(1)} %get-tuple-element.34.pd_ref, ...), custom_call_target="tpu_custom_call" | custom-call | tf_op jit(solution)/shard_map/pallas_call | solution.py:336
  32.2 4.6 %collective-permute-start.4 = (f32[1,16,512]{2,1,0:T(8,128)S(1)}, f32[1,16,512]{2,1,0:T(8,128)S(1)}, u32[]{:S(2)}, u32[]{:S(2)}) collective-permute-start(f32[1,16,512]{2,1,0:T(8,128)S(1)} %get-tuple-element.86), channel_id=1, source_target_pairs={{0,16},{16,32},{32,48},{48,64},{64,80},{80,96},{96,112},{112,128},... | collective-permute-start | bytes 98312 | tf_op jit(solution)/shard_map/ppermute | solution.py:318
  37.9 2.9 %collective-permute-start.7 = (f32[1,16,512]{2,1,0:T(8,128)S(1)}, f32[1,16,512]{2,1,0:T(8,128)S(1)}, u32[]{:S(2)}, u32[]{:S(2)}) collective-permute-start(f32[1,16,512]{2,1,0:T(8,128)S(1)} %get-tuple-element.75), channel_id=1, source_target_pairs={{1,0},{2,1},{3,2},{4,3},{5,4},{6,5},{7,6},{8,7},{9,8},{10,9},{11,1... | collective-permute-start | bytes 98312 | tf_op jit(solution)/shard_map/ppermute | solution.py:328
  40.8 4.1 %collective-permute-start.6 = (f32[1,16,512]{2,1,0:T(8,128)S(1)}, f32[1,16,512]{2,1,0:T(8,128)S(1)}, u32[]{:S(2)}, u32[]{:S(2)}) collective-permute-start(f32[1,16,512]{2,1,0:T(8,128)S(1)} %get-tuple-element.76), channel_id=1, source_target_pairs={{0,1},{1,2},{2,3},{3,4},{4,5},{5,6},{6,7},{7,8},{8,9},{9,10},{10,1... | collective-permute-start | bytes 98312 | tf_op jit(solution)/shard_map/ppermute | solution.py:327
  48.9 4.6 %collective-permute-start.8 = (f32[1,16,512]{2,1,0:T(8,128)S(1)}, f32[1,16,512]{2,1,0:T(8,128)S(1)}, u32[]{:S(2)}, u32[]{:S(2)}) collective-permute-start(f32[1,16,512]{2,1,0:T(8,128)S(1)} %get-tuple-element.84), channel_id=1, source_target_pairs={{0,16},{16,32},{32,48},{48,64},{64,80},{80,96},{96,112},{112,128},... | collective-permute-start | bytes 98312 | tf_op jit(solution)/shard_map/ppermute | solution.py:318
  54.5 1.9 %collective-permute-start.11 = (f32[1,16,512]{2,1,0:T(8,128)S(1)}, f32[1,16,512]{2,1,0:T(8,128)S(1)}, u32[]{:S(2)}, u32[]{:S(2)}) collective-permute-start(f32[1,16,512]{2,1,0:T(8,128)S(1)} %get-tuple-element.73), channel_id=1, source_target_pairs={{1,0},{2,1},{3,2},{4,3},{5,4},{6,5},{7,6},{8,7},{9,8},{10,9},{11,1... | collective-permute-start | bytes 98312 | tf_op jit(solution)/shard_map/ppermute | solution.py:328
  56.5 5.1 %collective-permute-start.10 = (f32[1,16,512]{2,1,0:T(8,128)S(1)}, f32[1,16,512]{2,1,0:T(8,128)S(1)}, u32[]{:S(2)}, u32[]{:S(2)}) collective-permute-start(f32[1,16,512]{2,1,0:T(8,128)S(1)} %get-tuple-element.74), channel_id=1, source_target_pairs={{0,1},{1,2},{2,3},{3,4},{4,5},{5,6},{6,7},{7,8},{8,9},{9,10},{10,1... | collective-permute-start | bytes 98312 | tf_op jit(solution)/shard_map/ppermute | solution.py:327
  62.6 1.7 %shard_map.151 = (f32[256,512]{1,0:T(8,128)S(1)}, f32[256,512]{1,0:T(8,128)S(1)}, f32[2,16,512]{2,1,0:T(8,128)S(1)}, f32[2,16,512]{2,1,0:T(8,128)S(1)}, f32[2,8,128]{2,1,0:T(8,128)S(1)}) custom-call(f32[256,512]{1,0:T(8,128)S(1)} %get-tuple-element.44.pin_ref, f32[1,16,512]{2,1,0:T(8,128)S(1)} %collective-permute-done.8.xl_ref, ...), custom_call_target="tpu_custom_call" | custom-call | tf_op jit(solution)/shard_map/pallas_call | solution.py:341
  65.6 4.6 %collective-permute-start.12 = (f32[1,16,512]{2,1,0:T(8,128)S(1)}, f32[1,16,512]{2,1,0:T(8,128)S(1)}, u32[]{:S(2)}, u32[]{:S(2)}) collective-permute-start(f32[1,16,512]{2,1,0:T(8,128)S(1)} %get-tuple-element.82), channel_id=1, source_target_pairs={{0,16},{16,32},{32,48},{48,64},{64,80},{80,96},{96,112},{112,128},... | collective-permute-start | bytes 98312 | tf_op jit(solution)/shard_map/ppermute | solution.py:318
  71.3 1.9 %collective-permute-start.15 = (f32[1,16,512]{2,1,0:T(8,128)S(1)}, f32[1,16,512]{2,1,0:T(8,128)S(1)}, u32[]{:S(2)}, u32[]{:S(2)}) collective-permute-start(f32[1,16,512]{2,1,0:T(8,128)S(1)} %get-tuple-element.71), channel_id=1, source_target_pairs={{1,0},{2,1},{3,2},{4,3},{5,4},{6,5},{7,6},{8,7},{9,8},{10,9},{11,1... | collective-permute-start | bytes 98312 | tf_op jit(solution)/shard_map/ppermute | solution.py:328
  73.2 5.1 %collective-permute-start.14 = (f32[1,16,512]{2,1,0:T(8,128)S(1)}, f32[1,16,512]{2,1,0:T(8,128)S(1)}, u32[]{:S(2)}, u32[]{:S(2)}) collective-permute-start(f32[1,16,512]{2,1,0:T(8,128)S(1)} %get-tuple-element.72), channel_id=1, source_target_pairs={{0,1},{1,2},{2,3},{3,4},{4,5},{5,6},{6,7},{7,8},{8,9},{9,10},{10,1... | collective-permute-start | bytes 98312 | tf_op jit(solution)/shard_map/ppermute | solution.py:327
  82.2 4.6 %collective-permute-start.16 = (f32[1,16,512]{2,1,0:T(8,128)S(1)}, f32[1,16,512]{2,1,0:T(8,128)S(1)}, u32[]{:S(2)}, u32[]{:S(2)}) collective-permute-start(f32[1,16,512]{2,1,0:T(8,128)S(1)} %get-tuple-element.80), channel_id=1, source_target_pairs={{0,16},{16,32},{32,48},{48,64},{64,80},{80,96},{96,112},{112,128},... | collective-permute-start | bytes 98312 | tf_op jit(solution)/shard_map/ppermute | solution.py:318
  87.9 1.9 %collective-permute-start.19 = (f32[1,16,512]{2,1,0:T(8,128)S(1)}, f32[1,16,512]{2,1,0:T(8,128)S(1)}, u32[]{:S(2)}, u32[]{:S(2)}) collective-permute-start(f32[1,16,512]{2,1,0:T(8,128)S(1)} %get-tuple-element.69), channel_id=1, source_target_pairs={{1,0},{2,1},{3,2},{4,3},{5,4},{6,5},{7,6},{8,7},{9,8},{10,9},{11,1... | collective-permute-start | bytes 98312 | tf_op jit(solution)/shard_map/ppermute | solution.py:328
  89.8 5.1 %collective-permute-start.18 = (f32[1,16,512]{2,1,0:T(8,128)S(1)}, f32[1,16,512]{2,1,0:T(8,128)S(1)}, u32[]{:S(2)}, u32[]{:S(2)}) collective-permute-start(f32[1,16,512]{2,1,0:T(8,128)S(1)} %get-tuple-element.70), channel_id=1, source_target_pairs={{0,1},{1,2},{2,3},{3,4},{4,5},{5,6},{6,7},{7,8},{8,9},{9,10},{10,1... | collective-permute-start | bytes 98312 | tf_op jit(solution)/shard_map/ppermute | solution.py:327
  95.9 1.7 %shard_map.153 = (f32[256,512]{1,0:T(8,128)S(1)}, f32[256,512]{1,0:T(8,128)S(1)}, f32[2,16,512]{2,1,0:T(8,128)S(1)}, f32[2,16,512]{2,1,0:T(8,128)S(1)}, f32[1,128]{1,0:T(1,128)S(1)}) custom-call(f32[256,512]{1,0:T(8,128)S(1)} %get-tuple-element.52.pin_ref, f32[1,16,512]{2,1,0:T(8,128)S(1)} %collective-permute-done.16.xl_ref, ...), custom_call_target="tpu_custom_call" | custom-call | tf_op jit(solution)/shard_map/pallas_call | solution.py:348
  99.5 13.0 %all-to-all-start = ((f32[16,1,128]{2,1,0:T(1,128)}), f32[16,1,128]{2,1,0:T(1,128)S(1)}, u32[]{:S(2)}, u32[]{:S(2)}) async-start(f32[16,1,128]{2,1,0:T(1,128)} %broadcast_in_dim.46), calls=%async_computation | async-start | bytes 16384 | tf_op jit(solution)/shard_map/all_to_all | solution.py:350
  112.6 5.8 %collective-permute-start.20 = (f32[1,16,512]{2,1,0:T(8,128)S(1)}, f32[1,16,512]{2,1,0:T(8,128)S(1)}, u32[]{:S(2)}, u32[]{:S(2)}) collective-permute-start(f32[1,16,512]{2,1,0:T(8,128)S(1)} %get-tuple-element.78), channel_id=1, source_target_pairs={{0,16},{16,32},{32,48},{48,64},{64,80},{80,96},{96,112},{112,128},... | collective-permute-start | bytes 98312 | tf_op jit(solution)/shard_map/ppermute | solution.py:318
  119.5 2.8 %collective-permute-start.23 = (f32[1,16,512]{2,1,0:T(8,128)S(1)}, f32[1,16,512]{2,1,0:T(8,128)S(1)}, u32[]{:S(2)}, u32[]{:S(2)}) collective-permute-start(f32[1,16,512]{2,1,0:T(8,128)S(1)} %get-tuple-element.67), channel_id=1, source_target_pairs={{1,0},{2,1},{3,2},{4,3},{5,4},{6,5},{7,6},{8,7},{9,8},{10,9},{11,1... | collective-permute-start | bytes 98312 | tf_op jit(solution)/shard_map/ppermute | solution.py:328
  122.3 3.4 %collective-permute-start.22 = (f32[1,16,512]{2,1,0:T(8,128)S(1)}, f32[1,16,512]{2,1,0:T(8,128)S(1)}, u32[]{:S(2)}, u32[]{:S(2)}) collective-permute-start(f32[1,16,512]{2,1,0:T(8,128)S(1)} %get-tuple-element.68), channel_id=1, source_target_pairs={{0,1},{1,2},{2,3},{3,4},{4,5},{5,6},{6,7},{7,8},{8,9},{9,10},{10,1... | collective-permute-start | bytes 98312 | tf_op jit(solution)/shard_map/ppermute | solution.py:327
  125.8 30.7 %all_to_all.12 = f32[32,1,128]{2,1,0:T(1,128)S(1)} all-to-all(f32[32,1,128]{2,1,0:T(1,128)S(1)} %broadcast_in_dim.47), channel_id=1, replica_groups=mesh['gx'=32,'gy'=16] {'gx'}, dimensions={0} | all-to-all | bytes 32768 | tf_op jit(solution)/shard_map/all_to_all | solution.py:351
  156.5 2.1 %shard_map.154 = (f32[16,16,512]{2,1,0:T(8,128)}, f32[16,16,512]{2,1,0:T(8,128)}, f32[16,16,512]{2,1,0:T(8,128)}) custom-call(f32[128]{0:T(128)S(1)} %reduce_sum.19.dots_ref, f32[256,512]{1,0:T(8,128)S(1)} %get-tuple-element.59.pin_ref, f32[1,16,512]{2,1,0:T(8,128)S(1)} %collective-permute-done.20.xl_ref, f32[1,16,512]{2,1,0:T(8,128)S(1)} %collective-permute-done.21.xr_ref, ...), custom_call_target="tpu_custom_call" | custom-call | tf_op jit(solution)/shard_map/pallas_call | solution.py:354
  (91 shorter events, 32.1 us)
Async XLA Ops:
  9.0 7.0 %collective-permute-start.1 = (f32[2,16,512]{2,1,0:T(8,128)S(1)}, f32[2,16,512]{2,1,0:T(8,128)S(1)}, u32[]{:S(2)}, u32[]{:S(2)}) collective-permute-start(f32[2,16,512]{2,1,0:T(8,128)S(1)} %get-tuple-element.65), channel_id=1, source_target_pairs={{16,0},{32,16},{48,32},{64,48},{80,64},{96,80},{112,96},{128,112},... | collective-permute-start | bytes 196616 | tf_op jit(solution)/shard_map/ppermute | solution.py:319
  10.4 6.8 %collective-permute-start = (f32[2,16,512]{2,1,0:T(8,128)S(1)}, f32[2,16,512]{2,1,0:T(8,128)S(1)}, u32[]{:S(2)}, u32[]{:S(2)}) collective-permute-start(f32[2,16,512]{2,1,0:T(8,128)S(1)} %get-tuple-element.66), channel_id=1, source_target_pairs={{0,16},{16,32},{32,48},{48,64},{64,80},{80,96},{96,112},{112,128},... | collective-permute-start | bytes 196616 | tf_op jit(solution)/shard_map/ppermute | solution.py:318
  17.3 11.5 %collective-permute-start.3 = (f32[2,16,512]{2,1,0:T(8,128)S(1)}, f32[2,16,512]{2,1,0:T(8,128)S(1)}, u32[]{:S(2)}, u32[]{:S(2)}) collective-permute-start(f32[2,16,512]{2,1,0:T(8,128)S(1)} %get-tuple-element.63), channel_id=1, source_target_pairs={{1,0},{2,1},{3,2},{4,3},{5,4},{6,5},{7,6},{8,7},{9,8},{10,9},{11,1... | collective-permute-start | bytes 196616 | tf_op jit(solution)/shard_map/ppermute | solution.py:328
  30.9 5.9 %collective-permute-start.5 = (f32[1,16,512]{2,1,0:T(8,128)S(1)}, f32[1,16,512]{2,1,0:T(8,128)S(1)}, u32[]{:S(2)}, u32[]{:S(2)}) collective-permute-start(f32[1,16,512]{2,1,0:T(8,128)S(1)} %get-tuple-element.85), channel_id=1, source_target_pairs={{16,0},{32,16},{48,32},{64,48},{80,64},{96,80},{112,96},{128,112},... | collective-permute-start | bytes 98312 | tf_op jit(solution)/shard_map/ppermute | solution.py:319
  32.2 5.6 %collective-permute-start.4 = (f32[1,16,512]{2,1,0:T(8,128)S(1)}, f32[1,16,512]{2,1,0:T(8,128)S(1)}, u32[]{:S(2)}, u32[]{:S(2)}) collective-permute-start(f32[1,16,512]{2,1,0:T(8,128)S(1)} %get-tuple-element.86), channel_id=1, source_target_pairs={{0,16},{16,32},{32,48},{48,64},{64,80},{80,96},{96,112},{112,128},... | collective-permute-start | bytes 98312 | tf_op jit(solution)/shard_map/ppermute | solution.py:318
  37.9 7.0 %collective-permute-start.7 = (f32[1,16,512]{2,1,0:T(8,128)S(1)}, f32[1,16,512]{2,1,0:T(8,128)S(1)}, u32[]{:S(2)}, u32[]{:S(2)}) collective-permute-start(f32[1,16,512]{2,1,0:T(8,128)S(1)} %get-tuple-element.75), channel_id=1, source_target_pairs={{1,0},{2,1},{3,2},{4,3},{5,4},{6,5},{7,6},{8,7},{9,8},{10,9},{11,1... | collective-permute-start | bytes 98312 | tf_op jit(solution)/shard_map/ppermute | solution.py:328
  40.8 5.1 %collective-permute-start.6 = (f32[1,16,512]{2,1,0:T(8,128)S(1)}, f32[1,16,512]{2,1,0:T(8,128)S(1)}, u32[]{:S(2)}, u32[]{:S(2)}) collective-permute-start(f32[1,16,512]{2,1,0:T(8,128)S(1)} %get-tuple-element.76), channel_id=1, source_target_pairs={{0,1},{1,2},{2,3},{3,4},{4,5},{5,6},{6,7},{7,8},{8,9},{9,10},{10,1... | collective-permute-start | bytes 98312 | tf_op jit(solution)/shard_map/ppermute | solution.py:327
  47.6 5.9 %collective-permute-start.9 = (f32[1,16,512]{2,1,0:T(8,128)S(1)}, f32[1,16,512]{2,1,0:T(8,128)S(1)}, u32[]{:S(2)}, u32[]{:S(2)}) collective-permute-start(f32[1,16,512]{2,1,0:T(8,128)S(1)} %get-tuple-element.83), channel_id=1, source_target_pairs={{16,0},{32,16},{48,32},{64,48},{80,64},{96,80},{112,96},{128,112},... | collective-permute-start | bytes 98312 | tf_op jit(solution)/shard_map/ppermute | solution.py:319
  48.9 5.6 %collective-permute-start.8 = (f32[1,16,512]{2,1,0:T(8,128)S(1)}, f32[1,16,512]{2,1,0:T(8,128)S(1)}, u32[]{:S(2)}, u32[]{:S(2)}) collective-permute-start(f32[1,16,512]{2,1,0:T(8,128)S(1)} %get-tuple-element.84), channel_id=1, source_target_pairs={{0,16},{16,32},{32,48},{48,64},{64,80},{80,96},{96,112},{112,128},... | collective-permute-start | bytes 98312 | tf_op jit(solution)/shard_map/ppermute | solution.py:318
  54.5 7.0 %collective-permute-start.11 = (f32[1,16,512]{2,1,0:T(8,128)S(1)}, f32[1,16,512]{2,1,0:T(8,128)S(1)}, u32[]{:S(2)}, u32[]{:S(2)}) collective-permute-start(f32[1,16,512]{2,1,0:T(8,128)S(1)} %get-tuple-element.73), channel_id=1, source_target_pairs={{1,0},{2,1},{3,2},{4,3},{5,4},{6,5},{7,6},{8,7},{9,8},{10,9},{11,1... | collective-permute-start | bytes 98312 | tf_op jit(solution)/shard_map/ppermute | solution.py:328
  56.5 6.1 %collective-permute-start.10 = (f32[1,16,512]{2,1,0:T(8,128)S(1)}, f32[1,16,512]{2,1,0:T(8,128)S(1)}, u32[]{:S(2)}, u32[]{:S(2)}) collective-permute-start(f32[1,16,512]{2,1,0:T(8,128)S(1)} %get-tuple-element.74), channel_id=1, source_target_pairs={{0,1},{1,2},{2,3},{3,4},{4,5},{5,6},{6,7},{7,8},{8,9},{9,10},{10,1... | collective-permute-start | bytes 98312 | tf_op jit(solution)/shard_map/ppermute | solution.py:327
  64.3 5.9 %collective-permute-start.13 = (f32[1,16,512]{2,1,0:T(8,128)S(1)}, f32[1,16,512]{2,1,0:T(8,128)S(1)}, u32[]{:S(2)}, u32[]{:S(2)}) collective-permute-start(f32[1,16,512]{2,1,0:T(8,128)S(1)} %get-tuple-element.81), channel_id=1, source_target_pairs={{16,0},{32,16},{48,32},{64,48},{80,64},{96,80},{112,96},{128,112},... | collective-permute-start | bytes 98312 | tf_op jit(solution)/shard_map/ppermute | solution.py:319
  65.6 5.6 %collective-permute-start.12 = (f32[1,16,512]{2,1,0:T(8,128)S(1)}, f32[1,16,512]{2,1,0:T(8,128)S(1)}, u32[]{:S(2)}, u32[]{:S(2)}) collective-permute-start(f32[1,16,512]{2,1,0:T(8,128)S(1)} %get-tuple-element.82), channel_id=1, source_target_pairs={{0,16},{16,32},{32,48},{48,64},{64,80},{80,96},{96,112},{112,128},... | collective-permute-start | bytes 98312 | tf_op jit(solution)/shard_map/ppermute | solution.py:318
  71.3 7.0 %collective-permute-start.15 = (f32[1,16,512]{2,1,0:T(8,128)S(1)}, f32[1,16,512]{2,1,0:T(8,128)S(1)}, u32[]{:S(2)}, u32[]{:S(2)}) collective-permute-start(f32[1,16,512]{2,1,0:T(8,128)S(1)} %get-tuple-element.71), channel_id=1, source_target_pairs={{1,0},{2,1},{3,2},{4,3},{5,4},{6,5},{7,6},{8,7},{9,8},{10,9},{11,1... | collective-permute-start | bytes 98312 | tf_op jit(solution)/shard_map/ppermute | solution.py:328
  73.2 6.1 %collective-permute-start.14 = (f32[1,16,512]{2,1,0:T(8,128)S(1)}, f32[1,16,512]{2,1,0:T(8,128)S(1)}, u32[]{:S(2)}, u32[]{:S(2)}) collective-permute-start(f32[1,16,512]{2,1,0:T(8,128)S(1)} %get-tuple-element.72), channel_id=1, source_target_pairs={{0,1},{1,2},{2,3},{3,4},{4,5},{5,6},{6,7},{7,8},{8,9},{9,10},{10,1... | collective-permute-start | bytes 98312 | tf_op jit(solution)/shard_map/ppermute | solution.py:327
  80.9 5.9 %collective-permute-start.17 = (f32[1,16,512]{2,1,0:T(8,128)S(1)}, f32[1,16,512]{2,1,0:T(8,128)S(1)}, u32[]{:S(2)}, u32[]{:S(2)}) collective-permute-start(f32[1,16,512]{2,1,0:T(8,128)S(1)} %get-tuple-element.79), channel_id=1, source_target_pairs={{16,0},{32,16},{48,32},{64,48},{80,64},{96,80},{112,96},{128,112},... | collective-permute-start | bytes 98312 | tf_op jit(solution)/shard_map/ppermute | solution.py:319
  82.2 5.6 %collective-permute-start.16 = (f32[1,16,512]{2,1,0:T(8,128)S(1)}, f32[1,16,512]{2,1,0:T(8,128)S(1)}, u32[]{:S(2)}, u32[]{:S(2)}) collective-permute-start(f32[1,16,512]{2,1,0:T(8,128)S(1)} %get-tuple-element.80), channel_id=1, source_target_pairs={{0,16},{16,32},{32,48},{48,64},{64,80},{80,96},{96,112},{112,128},... | collective-permute-start | bytes 98312 | tf_op jit(solution)/shard_map/ppermute | solution.py:318
  87.9 7.0 %collective-permute-start.19 = (f32[1,16,512]{2,1,0:T(8,128)S(1)}, f32[1,16,512]{2,1,0:T(8,128)S(1)}, u32[]{:S(2)}, u32[]{:S(2)}) collective-permute-start(f32[1,16,512]{2,1,0:T(8,128)S(1)} %get-tuple-element.69), channel_id=1, source_target_pairs={{1,0},{2,1},{3,2},{4,3},{5,4},{6,5},{7,6},{8,7},{9,8},{10,9},{11,1... | collective-permute-start | bytes 98312 | tf_op jit(solution)/shard_map/ppermute | solution.py:328
  89.8 6.1 %collective-permute-start.18 = (f32[1,16,512]{2,1,0:T(8,128)S(1)}, f32[1,16,512]{2,1,0:T(8,128)S(1)}, u32[]{:S(2)}, u32[]{:S(2)}) collective-permute-start(f32[1,16,512]{2,1,0:T(8,128)S(1)} %get-tuple-element.70), channel_id=1, source_target_pairs={{0,1},{1,2},{2,3},{3,4},{4,5},{5,6},{6,7},{7,8},{8,9},{9,10},{10,1... | collective-permute-start | bytes 98312 | tf_op jit(solution)/shard_map/ppermute | solution.py:327
  97.6 20.7 %collective-permute-start.21 = (f32[1,16,512]{2,1,0:T(8,128)S(1)}, f32[1,16,512]{2,1,0:T(8,128)S(1)}, u32[]{:S(2)}, u32[]{:S(2)}) collective-permute-start(f32[1,16,512]{2,1,0:T(8,128)S(1)} %get-tuple-element.77), channel_id=1, source_target_pairs={{16,0},{32,16},{48,32},{64,48},{80,64},{96,80},{112,96},{128,112},... | collective-permute-start | bytes 98312 | tf_op jit(solution)/shard_map/ppermute | solution.py:319
  99.5 26.2 %all-to-all-start = ((f32[16,1,128]{2,1,0:T(1,128)}), f32[16,1,128]{2,1,0:T(1,128)S(1)}, u32[]{:S(2)}, u32[]{:S(2)}) async-start(f32[16,1,128]{2,1,0:T(1,128)} %broadcast_in_dim.46), calls=%async_computation | async-start | bytes 16384 | tf_op jit(solution)/shard_map/all_to_all | solution.py:350
  112.6 6.8 %collective-permute-start.20 = (f32[1,16,512]{2,1,0:T(8,128)S(1)}, f32[1,16,512]{2,1,0:T(8,128)S(1)}, u32[]{:S(2)}, u32[]{:S(2)}) collective-permute-start(f32[1,16,512]{2,1,0:T(8,128)S(1)} %get-tuple-element.78), channel_id=1, source_target_pairs={{0,16},{16,32},{32,48},{48,64},{64,80},{80,96},{96,112},{112,128},... | collective-permute-start | bytes 98312 | tf_op jit(solution)/shard_map/ppermute | solution.py:318
  119.5 37.0 %collective-permute-start.23 = (f32[1,16,512]{2,1,0:T(8,128)S(1)}, f32[1,16,512]{2,1,0:T(8,128)S(1)}, u32[]{:S(2)}, u32[]{:S(2)}) collective-permute-start(f32[1,16,512]{2,1,0:T(8,128)S(1)} %get-tuple-element.67), channel_id=1, source_target_pairs={{1,0},{2,1},{3,2},{4,3},{5,4},{6,5},{7,6},{8,7},{9,8},{10,9},{11,1... | collective-permute-start | bytes 98312 | tf_op jit(solution)/shard_map/ppermute | solution.py:328
  122.3 34.2 %collective-permute-start.22 = (f32[1,16,512]{2,1,0:T(8,128)S(1)}, f32[1,16,512]{2,1,0:T(8,128)S(1)}, u32[]{:S(2)}, u32[]{:S(2)}) collective-permute-start(f32[1,16,512]{2,1,0:T(8,128)S(1)} %get-tuple-element.68), channel_id=1, source_target_pairs={{0,1},{1,2},{2,3},{3,4},{4,5},{5,6},{6,7},{7,8},{8,9},{9,10},{10,1... | collective-permute-start | bytes 98312 | tf_op jit(solution)/shard_map/ppermute | solution.py:327
  (14 other events, 65.6 us)

commit v2 on v1

--- a/solution.py
+++ b/solution.py
@@ -135,19 +135,20 @@
     return f + jnp.where(upper, nxt, jnp.where(lower, prv, 0.0))
 
 
-def emit_partial(f, p_ref, x_ref, y_ref):
+def emit_partial(f, edge_ref, p_ref, faces):
     p_ref[...] = join_z(f)
     p_ref[112:128, :] = p_ref[112:128, :] + p_ref[128:144, :]
     p_ref[128:144, :] = p_ref[112:128, :]
+    x_low, x_high, y_low, y_high = faces
     for x in range(16):
         r = 16 * x
         mid = p_ref[r + 7:r + 8, :] + p_ref[r + 8:r + 9, :]
         p_ref[r + 7:r + 8, :] = mid
         p_ref[r + 8:r + 9, :] = mid
-        y_ref[0, x:x + 1, :] = p_ref[r:r + 1, :]
-        y_ref[1, x:x + 1, :] = p_ref[r + 15:r + 16, :]
-    x_ref[0] = p_ref[0:16, :]
-    x_ref[1] = p_ref[240:256, :]
+        y_low[x:x + 1, :] = p_ref[r:r + 1, :]
+        y_high[x:x + 1, :] = p_ref[r + 15:r + 16, :]
+    x_low[...] = jnp.where(edge_ref[0] == 1, 0.0, p_ref[0:16, :])
+    x_high[...] = jnp.where(edge_ref[1] == 1, 0.0, p_ref[240:256, :])
 
 
 def take_sum(p_ref, recv, s_ref):
@@ -167,8 +168,17 @@
     return part[:, 0:128] + part[:, 128:256] + part[:, 256:384] + part[:, 384:512]
 
 
-def first_kernel(table_ref, load_ref, cond_ref, region_ref, sq_ref, sqz_ref, wr_ref, wz_ref,
-                 coef_ref, react_ref, pl_ref, pd_ref, x_ref, y_ref):
+def first_kernel(edge_ref, table_hbm, load_hbm, cond_hbm, flags_hbm, region_hbm, sq_hbm, sqz_hbm, wr_hbm, wz_hbm,
+                 coef_ref, react_ref, keep_ref, pl_ref, pd_ref, xl_ref, xh_ref, yl_ref, yh_ref,
+                 table_ref, load_ref, cond_ref, flags_ref, region_ref, sq_ref, sqz_ref, wr_ref, wz_ref, sems):
+    flags_tile = flags_hbm.at[:, :, pl.ds(0, 128)]
+    pairs = ((cond_hbm, cond_ref), (wr_hbm, wr_ref), (wz_hbm, wz_ref), (region_hbm, region_ref), (table_hbm, table_ref),
+             (sq_hbm, sq_ref), (sqz_hbm, sqz_ref), (load_hbm, load_ref), (flags_tile, flags_ref))
+    copies = [pltpu.make_async_copy(src, dst, sems.at[i]) for i, (src, dst) in enumerate(pairs)]
+    for copy in copies:
+        copy.start()
+    for copy in copies[:5]:
+        copy.wait()
     w_row = wr_ref[...]
     w_row = jnp.concatenate([w_row] * 4, axis=1)
     quad_z = wz_ref[...]
@@ -188,6 +198,9 @@
             for ey in range(2):
                 r = (ex * 8 + x) * 16 + ey * 8
                 react_ref[r:r + 8, :] = (w_row[r:r + 8] * quad_z) * kappa[ey:ey + 1, :]
+    for copy in copies[5:]:
+        copy.wait()
+    keep_ref[...] = (1 - flags_ref[...].reshape(ROWS, 128)).astype(F32)
     high, low = halves(coef)
     rows = []
     for e in range(2):
@@ -195,35 +208,36 @@
         pair = jnp.concatenate([high[part], low[part]], 0)
         rows.append(dot(sq_ref[0], pair) + dot(sq_ref[1], pair))
     diag = jnp.concatenate(rows, 0) + mul_z(high, low, sqz_ref[...]) + react_ref[...]
-    emit_partial(diag, pd_ref, x_ref.at[1], y_ref.at[1])
-    emit_partial(load_ref[...].reshape(ROWS, COLS), pl_ref, x_ref.at[0], y_ref.at[0])
-
-
-def second_kernel(pl_ref, pd_ref, xl_ref, xr_ref, yb_ref, ya_ref, flags_ref, coef_ref, react_ref,
+    faces = (xl_ref, xh_ref, yl_ref, yh_ref)
+    emit_partial(diag, edge_ref, pd_ref, [face.at[1] for face in faces])
+    emit_partial(load_ref[...].reshape(ROWS, COLS), edge_ref, pl_ref, [face.at[0] for face in faces])
+
+
+def second_kernel(edge_ref, pl_ref, pd_ref, xl_ref, xr_ref, yb_ref, ya_ref, keep_ref, coef_ref, react_ref,
                   grad_ref, back_ref, gz_ref, bz_ref,
-                  r_ref, dinv_ref, p_ref, x_ref, y_ref, s_ref):
+                  r_ref, dinv_ref, p_ref, lo_x, hi_x, lo_y, hi_y, s_ref):
     diag = take_sum(pd_ref, (xl_ref[1], xr_ref[1], yb_ref[1], ya_ref[1]), s_ref)
     dinv_ref[...] = 1.0 / diag
-    keep = (1 - flags_ref[...].reshape(ROWS, 128)).astype(F32)
+    keep = keep_ref[...]
     dinv_ref[:, 0:128] = keep * dinv_ref[:, 0:128]
     r = take_sum(pl_ref, (xl_ref[0], xr_ref[0], yb_ref[0], ya_ref[0]), s_ref)
     r_ref[...] = r
     r_ref[:, 0:128] = keep * r_ref[:, 0:128]
     a0 = dinv_ref[...] * r_ref[...] * (1.0 / CENTER)
     f = local_op(a0, coef_ref[...], react_ref[...], grad_ref, back_ref, gz_ref[...], bz_ref[...])
-    emit_partial(f, p_ref, x_ref, y_ref)
-
-
-def sweep1_kernel(pin_ref, xl_ref, xr_ref, yb_ref, ya_ref, r_ref, dinv_ref, coef_ref, react_ref,
+    emit_partial(f, edge_ref, p_ref, (lo_x, hi_x, lo_y, hi_y))
+
+
+def sweep1_kernel(edge_ref, pin_ref, xl_ref, xr_ref, yb_ref, ya_ref, r_ref, dinv_ref, coef_ref, react_ref,
                   grad_ref, back_ref, gz_ref, bz_ref,
-                  a1_ref, p_ref, x_ref, y_ref, s_ref):
-    image = take_sum(pin_ref, (xl_ref[0], xr_ref[0], yb_ref[0], ya_ref[0]), s_ref)
+                  a1_ref, p_ref, lo_x, hi_x, lo_y, hi_y, s_ref):
+    image = take_sum(pin_ref, (xl_ref[...], xr_ref[...], yb_ref[...], ya_ref[...]), s_ref)
     dinv, r = dinv_ref[...], r_ref[...]
     a0 = dinv * r * (1.0 / CENTER)
     a1 = (1.0 + MIX1) * a0 + GAIN1 * (dinv * (r - image))
     a1_ref[...] = a1
     f = local_op(a1, coef_ref[...], react_ref[...], grad_ref, back_ref, gz_ref[...], bz_ref[...])
-    emit_partial(f, p_ref, x_ref, y_ref)
+    emit_partial(f, edge_ref, p_ref, (lo_x, hi_x, lo_y, hi_y))
 
 
 def sweep2(image, a1, r, dinv):
@@ -231,46 +245,47 @@
     return a1 + (MIX2 * (a1 - a0) + GAIN2 * (dinv * (r - image)))
 
 
-def third_kernel(pin_ref, xl_ref, xr_ref, yb_ref, ya_ref, r_ref, dinv_ref, a1_ref, load_ref, coef_ref, react_ref,
+def third_kernel(edge_ref, pin_ref, xl_ref, xr_ref, yb_ref, ya_ref, r_ref, dinv_ref, a1_ref, load_ref, coef_ref, react_ref,
                  grad_ref, back_ref, gz_ref, bz_ref,
-                 z_ref, p_ref, x_ref, y_ref, dots_ref, s_ref):
-    image = take_sum(pin_ref, (xl_ref[0], xr_ref[0], yb_ref[0], ya_ref[0]), s_ref)
+                 z_ref, p_ref, lo_x, hi_x, lo_y, hi_y, dots_ref, s_ref):
+    image = take_sum(pin_ref, (xl_ref[...], xr_ref[...], yb_ref[...], ya_ref[...]), s_ref)
     z = sweep2(image, a1_ref[...], r_ref[...], dinv_ref[...])
     z_ref[...] = z
     dots_ref[0] = fold(load_ref[...].reshape(ROWS, COLS) * z)
     f = local_op(z, coef_ref[...], react_ref[...], grad_ref, back_ref, gz_ref[...], bz_ref[...])
     dots_ref[1] = fold(f * z)
-    emit_partial(f, p_ref, x_ref, y_ref)
-
-
-def fourth_kernel(pin_ref, xl_ref, xr_ref, yb_ref, ya_ref, dinv_ref, z_ref, coef_ref, react_ref,
+    emit_partial(f, edge_ref, p_ref, (lo_x, hi_x, lo_y, hi_y))
+
+
+def fourth_kernel(edge_ref, pin_ref, xl_ref, xr_ref, yb_ref, ya_ref, dinv_ref, z_ref, coef_ref, react_ref,
                   grad_ref, back_ref, gz_ref, bz_ref,
-                  im_ref, p_ref, x_ref, y_ref, dots_ref, s_ref):
-    image = take_sum(pin_ref, (xl_ref[0], xr_ref[0], yb_ref[0], ya_ref[0]), s_ref)
+                  im_ref, p_ref, lo_x, hi_x, lo_y, hi_y, dots_ref, s_ref):
+    image = take_sum(pin_ref, (xl_ref[...], xr_ref[...], yb_ref[...], ya_ref[...]), s_ref)
     dinv = dinv_ref[...]
     im = jnp.where(dinv != 0.0, image, 0.0)
     im_ref[...] = im
     b0 = dinv * im * (1.0 / CENTER)
     f = local_op(b0, coef_ref[...], react_ref[...], grad_ref, back_ref, gz_ref[...], bz_ref[...])
     dots_ref[...] = fold(f * z_ref[...])
-    emit_partial(f, p_ref, x_ref, y_ref)
-
-
-def fifth_kernel(pin_ref, xl_ref, xr_ref, yb_ref, ya_ref, im_ref, dinv_ref, z_ref, d34_ref, d5_ref, coef_ref, react_ref,
+    emit_partial(f, edge_ref, p_ref, (lo_x, hi_x, lo_y, hi_y))
+
+
+def fifth_kernel(edge_ref, pin_ref, xl_ref, xr_ref, yb_ref, ya_ref, im_ref, dinv_ref, z_ref, d34_ref, d5_ref, coef_ref, react_ref,
                  grad_ref, back_ref, gz_ref, bz_ref,
-                 b1_ref, p_ref, x_ref, y_ref, dots_ref, s_ref):
-    image = take_sum(pin_ref, (xl_ref[0], xr_ref[0], yb_ref[0], ya_ref[0]), s_ref)
+                 b1_ref, p_ref, lo_x, hi_x, lo_y, hi_y, dots_ref, s_ref):
+    image = take_sum(pin_ref, (xl_ref[...], xr_ref[...], yb_ref[...], ya_ref[...]), s_ref)
     dinv, im = dinv_ref[...], im_ref[...]
     b0 = dinv * im * (1.0 / CENTER)
     b1 = (1.0 + MIX1) * b0 + GAIN1 * (dinv * (im - image))
     b1_ref[...] = b1
     f = local_op(b1, coef_ref[...], react_ref[...], grad_ref, back_ref, gz_ref[...], bz_ref[...])
-    emit_partial(f, p_ref, x_ref, y_ref)
+    emit_partial(f, edge_ref, p_ref, (lo_x, hi_x, lo_y, hi_y))
     last = fold(f * ((1.0 + MIX2) * z_ref[...] - (CENTER * GAIN2) * b0))
     both = last + (CENTER * GAIN2 - MIX2) * d5_ref[...]
     lane = lax.broadcasted_iota(jnp.int32, (1, 128), 1)
-    dots_ref[...] = jnp.where(
+    sums = jnp.where(
         lane == 0, jnp.sum(d34_ref[0]), jnp.where(lane == 1, jnp.sum(d34_ref[1]), jnp.sum(both)))
+    dots_ref[...] = jnp.broadcast_to(sums, dots_ref.shape)
 
 
 def last_kernel(dots_ref, pin_ref, xl_ref, xr_ref, yb_ref, ya_ref, im_ref, dinv_ref, b1_ref, z_ref, r_ref,
@@ -278,7 +293,7 @@
     first, curv, quad = dots_ref[0], dots_ref[1], dots_ref[2]
     step = first / curv
     ratio = (first - 2.0 * step * curv + step * step * quad) / first
-    image = take_sum(pin_ref, (xl_ref[0], xr_ref[0], yb_ref[0], ya_ref[0]), s_ref)
+    image = take_sum(pin_ref, (xl_ref[...], xr_ref[...], yb_ref[...], ya_ref[...]), s_ref)
     im = im_ref[...]
     b2 = sweep2(image, b1_ref[...], im, dinv_ref[...])
     z = z_ref[...]
@@ -290,68 +305,80 @@
 
 VM = pl.BlockSpec(memory_space=pltpu.VMEM)
 SM = pl.BlockSpec(memory_space=pltpu.SMEM)
+HB = pl.BlockSpec(memory_space=pl.ANY)
 BIG = jax.ShapeDtypeStruct((ROWS, COLS), F32)
-FACES = jax.ShapeDtypeStruct((2, 16, COLS), F32)
-SCRATCH = [pltpu.VMEM((ROWS, COLS), F32)]
+FACE = jax.ShapeDtypeStruct((16, COLS), F32)
+PART = (BIG, FACE, FACE, FACE, FACE)
 PARAMS = pltpu.CompilerParams(vmem_limit_bytes=24 << 20)
 
 
-def call(kernel, outs, n_in, smem_first=False, scratch=True):
-    specs = [VM] * n_in
-    if smem_first:
-        specs[0] = SM
+def call(kernel, outs, specs, scratch):
     return pl.pallas_call(
         kernel, out_shape=outs, in_specs=specs, out_specs=jax.tree.map(lambda _: VM, outs),
-        scratch_shapes=SCRATCH if scratch else [], compiler_params=PARAMS)
+        scratch_shapes=scratch, compiler_params=PARAMS)
+
+
+def step_call(kernel, outs, n_in):
+    return call(kernel, outs, [SM] + [VM] * n_in, [pltpu.VMEM((ROWS, COLS), F32)])
 
 
 def per_device(load, conductivity, flags, region, kappa_table):
     k = {name: jnp.asarray(value) for name, value in constants().items()}
     mats = (k["grad"], k["back"], k["grad_z"], k["back_z"])
     n_x, n_y = lax.axis_size("gx"), lax.axis_size("gy")
-    up_x = [(i, i + 1) for i in range(n_x - 1)]
-    up_y = [(i, i + 1) for i in range(n_y - 1)]
+    at_x, at_y = lax.axis_index("gx"), lax.axis_index("gy")
+    edge = jnp.stack([at_x == 0, at_x == n_x - 1, at_y == 0, at_y == n_y - 1]).astype(jnp.int32)
+    up_x = [(i, (i + 1) % n_x) for i in range(n_x)]
+    up_y = [(i, (i + 1) % n_y) for i in range(n_y)]
     down_x = [(j, i) for i, j in up_x]
     down_y = [(j, i) for i, j in up_y]
 
-    def exchange(faces_x, faces_y):
-        left = lax.ppermute(faces_x[:, 1], "gx", up_x)
-        right = lax.ppermute(faces_x[:, 0], "gx", down_x)
-
-        def with_corners(side, row):
-            face = faces_y[:, side]
-            fields = face.shape[0]
-            inner = jnp.zeros((fields, 14, COLS), F32)
-            return face + jnp.concatenate([left[:, row:row + 1], inner, right[:, row:row + 1]], axis=1)
-
-        below = lax.ppermute(with_corners(1, 15), "gy", up_y)
-        above = lax.ppermute(with_corners(0, 0), "gy", down_y)
+    def exchange(faces):
+        x_low, x_high, y_low, y_high = faces
+        left = lax.ppermute(x_high, "gx", up_x)
+        right = lax.ppermute(x_low, "gx", down_x)
+
+        def with_corners(face, row, last):
+            inner = jnp.zeros(face.shape[:-2] + (14, COLS), F32)
+            ends = [left[..., row:row + 1, :], inner, right[..., row:row + 1, :]]
+            return jnp.where(last, 0.0, face + jnp.concatenate(ends, axis=-2))
+
+        below = lax.ppermute(with_corners(y_high, 15, at_y == n_y - 1), "gy", up_y)
+        above = lax.ppermute(with_corners(y_low, 0, at_y == 0), "gy", down_y)
         return left, right, below, above
 
-    two = jax.ShapeDtypeStruct((2, 2, 16, COLS), F32)
-    coef, react, part_l, part_d, fx, fy = call(first_kernel, (BIG, BIG, BIG, BIG, two, two), 8, True, False)(
-        kappa_table, load, conductivity, region, k["sq"], k["sq_z"], k["w_rows"], k["w_z"])
-    recv = exchange(fx, fy)
-    flags0 = lax.slice_in_dim(flags, 0, 128, axis=2)
-    r, dinv, part, fx, fy = call(second_kernel, (BIG, BIG, BIG, FACES, FACES), 13)(
-        part_l, part_d, *recv, flags0, coef, react, *mats)
-    recv = exchange(fx[None], fy[None])
-    a1, part, fx, fy = call(sweep1_kernel, (BIG, BIG, FACES, FACES), 13)(part, *recv, r, dinv, coef, react, *mats)
-    recv = exchange(fx[None], fy[None])
-    z, part, fx, fy, d34 = call(
-        third_kernel, (BIG, BIG, FACES, FACES, jax.ShapeDtypeStruct((2, 8, 128), F32)), 15)(
-        part, *recv, r, dinv, a1, load, coef, react, *mats)
-    recv = exchange(fx[None], fy[None])
-    im, part, fx, fy, d5 = call(fourth_kernel, (BIG, BIG, FACES, FACES, jax.ShapeDtypeStruct((8, 128), F32)), 13)(
-        part, *recv, dinv, z, coef, react, *mats)
-    recv = exchange(fx[None], fy[None])
-    b1, part, fx, fy, dots = call(fifth_kernel, (BIG, BIG, FACES, FACES, jax.ShapeDtypeStruct((1, 128), F32)), 16)(
-        part, *recv, im, dinv, z, d34, d5, coef, react, *mats)
-    total = lax.all_to_all(jnp.broadcast_to(dots, (n_y, 128)), "gy", 0, 0, tiled=True).sum(0)
+    two = jax.ShapeDtypeStruct((2, 16, COLS), F32)
+    keep_shape = jax.ShapeDtypeStruct((ROWS, 128), F32)
+    inputs = (kappa_table, load, conductivity, flags, region, k["sq"], k["sq_z"], k["w_rows"], k["w_z"])
+    buffers = [pltpu.VMEM(v.shape, v.dtype) for v in inputs]
+    buffers[0] = pltpu.SMEM(kappa_table.shape, F32)
+    buffers[3] = pltpu.VMEM((16, 16, 128), jnp.int32)
+    coef, react, keep, part_l, part_d, *faces = call(
+        first_kernel, (BIG, BIG, keep_shape, BIG, BIG, two, two, two, two), [SM] + [HB] * len(inputs),
+        buffers + [pltpu.SemaphoreType.DMA((len(inputs),))])(edge, *inputs)
+    recv = exchange(faces)
+    r, dinv, part, *faces = step_call(second_kernel, (BIG, BIG) + PART, 13)(
+        edge, part_l, part_d, *recv, keep, coef, react, *mats)
+    recv = exchange(faces)
+    a1, part, *faces = step_call(sweep1_kernel, (BIG,) + PART, 13)(
+        edge, part, *recv, r, dinv, coef, react, *mats)
+    recv = exchange(faces)
+    d34_shape = jax.ShapeDtypeStruct((2, 8, 128), F32)
+    z, part, *faces, d34 = step_call(third_kernel, (BIG,) + PART + (d34_shape,), 15)(
+        edge, part, *recv, r, dinv, a1, load, coef, react, *mats)
+    recv = exchange(faces)
+    d5_shape = jax.ShapeDtypeStruct((8, 128), F32)
+    im, part, *faces, d5 = step_call(fourth_kernel, (BIG,) + PART + (d5_shape,), 13)(
+        edge, part, *recv, dinv, z, coef, react, *mats)
+    recv = exchange(faces)
+    dots_shape = jax.ShapeDtypeStruct((n_y, 128), F32)
+    b1, part, *faces, dots = step_call(fifth_kernel, (BIG,) + PART + (dots_shape,), 16)(
+        edge, part, *recv, im, dinv, z, d34, d5, coef, react, *mats)
+    total = lax.all_to_all(dots, "gy", 0, 0, tiled=True).sum(0)
+    recv = exchange(faces)
     total = lax.all_to_all(jnp.broadcast_to(total, (n_x, 128)), "gx", 0, 0, tiled=True).sum(0)
-    recv = exchange(fx[None], fy[None])
     shape = jax.ShapeDtypeStruct((16, 16, COLS), F32)
-    return call(last_kernel, (shape, shape, shape), 11, True)(
+    return step_call(last_kernel, (shape, shape, shape), 10)(
         total, part, *recv, im, dinv, b1, z, r)
 
 

time: 160 us -> 146 us (0.912)
  blocking collectives: 30.7 us -> 15.5 us
  Pallas kernels: 12 us -> 16.4 us
  starting transfers between devices: 95.3 us -> 92.7 us
  waiting for transfers between devices: 10.5 us -> 12.9 us
  local copies, waits for them, and re-layouts: 8.47 us -> 6.54 us
    all_to_all x1, blocking collectives: 30.7 us -> 15.5 us  [per_device(): lax.all_to_all(jnp.broadcast_to(total, (n_x, 128)), 'gx', 0, 0, tiled=True)]
    pallas_call x7, Pallas kernels: 12 us -> 16.4 us  [the longest x1 2.87 us: per_device(): step_call(fifth_kernel, (BIG,) + PART + (dots_shape,), 16)]
    all_to_all x1, starting transfers between devices: 13 us -> 8.76 us  [per_device(): total = lax.all_to_all(dots, 'gy', 0, 0, tiled=True).sum(0)]
    ppermute x24, waiting for transfers between devices: 10.5 us -> 12.9 us  [the longest x6 6.1 us: exchange(): right = lax.ppermute(x_low, 'gx', down_x)]
    ppermute x24, starting transfers between devices: 82.3 us -> 84 us  [the longest x6 47.2 us: exchange(): right = lax.ppermute(x_low, 'gx', down_x)]
    unnamed x26 -> x28, local copies, waits for them, and re-layouts: 6.74 us -> 6.38 us
  transfers between devices with their start and end apart: 25 -> 25, of which waited for: 11 -> 15; matrix products, arithmetic and copies ran while one was open for 1% -> 0% of each run, Pallas kernels for 0% -> 0%
where the time goes in v2:
time: 146 us
  starting transfers between devices  92.7 us (63%)
  Pallas kernels  16.4 us (11%)
  blocking collectives  15.5 us (11%)
  waiting for transfers between devices  12.9 us (9%)
  local copies, waits for them, and re-layouts  6.54 us (4%)
    ppermute x6, starting transfers between devices, exchange(): right = lax.ppermute(x_low, 'gx', down_x)  47.2 us
    ppermute x6, starting transfers between devices, exchange(): above = lax.ppermute(with_corners(y_low, 0, at_y == 0), 'gy', down_y)  19.5 us
    all_to_all x1, blocking collectives, per_device(): lax.all_to_all(jnp.broadcast_to(total, (n_x, 128)), 'gx', 0, 0, tiled=True)  15.5 us
    ppermute x6, starting transfers between devices, exchange(): left = lax.ppermute(x_high, 'gx', up_x)  14.6 us
    all_to_all x1, starting transfers between devices, per_device(): total = lax.all_to_all(dots, 'gy', 0, 0, tiled=True).sum(0)  8.76 us
    unnamed x28, local copies, waits for them, and re-layouts  6.38 us
    ppermute x6, waiting for transfers between devices, exchange(): right = lax.ppermute(x_low, 'gx', down_x)  6.1 us
    ppermute x6, waiting for transfers between devices, exchange(): above = lax.ppermute(with_corners(y_low, 0, at_y == 0), 'gy', down_y)  5.35 us
  transfers between devices with their start and end apart: 25, of which 15 were waited for; matrix products, arithmetic and copies ran while one was open for 0% of the time, Pallas kernels for 0%

profile of v2, /device:TPU:1, one launch (start us, length us, event | category | flops | bytes accessed | tf_op | source)
XLA Modules:
  0.0 145.5 jit_solution(17830461918073240311)
XLA Ops:
  7.1 2.5 %shard_map.148 = (f32[256,512]{1,0:T(8,128)S(1)}, f32[256,512]{1,0:T(8,128)S(1)}, f32[256,128]{1,0:T(8,128)S(1)}, f32[256,512]{1,0:T(8,128)S(1)}, f32[256,512]{1...) custom-call(s32[4]{0:T(128)S(1)} %add_convert_fusion.edge_ref, ...), custom_call_target="tpu_custom_call" | custom-call | tf_op jit(solution)/shard_map/pallas_call | solution.py:356
  9.6 5.0 %collective-permute-start = (f32[2,16,512]{2,1,0:T(8,128)S(1)}, f32[2,16,512]{2,1,0:T(8,128)S(1)}, u32[]{:S(2)}, u32[]{:S(2)}) collective-permute-start(f32[2,16,512]{2,1,0:T(8,128)S(1)} %get-tuple-element.48), channel_id=1, source_target_pairs={{0,16},{16,32},{32,48},{48,64},{64,80},{80,96},{96,112},{112,128},... | collective-permute-start | bytes 196616 | tf_op jit(solution)/shard_map/ppermute | solution.py:338
  14.6 10.8 %collective-permute-start.1 = (f32[2,16,512]{2,1,0:T(8,128)S(1)}, f32[2,16,512]{2,1,0:T(8,128)S(1)}, u32[]{:S(2)}, u32[]{:S(2)}) collective-permute-start(f32[2,16,512]{2,1,0:T(8,128)S(1)} %get-tuple-element.49), channel_id=1, source_target_pairs={{16,0},{32,16},{48,32},{64,48},{80,64},{96,80},{112,96},{128,112},... | collective-permute-start | bytes 196616 | tf_op jit(solution)/shard_map/ppermute | solution.py:339
  29.6 1.9 %collective-permute-done.3.ya_ref = f32[2,16,512]{2,1,0:T(8,128)S(1)} collective-permute-done((f32[2,16,512]{2,1,0:T(8,128)S(1)}, f32[2,16,512]{2,1,0:T(8,128)S(1)}, u32[]{:S(2)}, u32[]{:S(2)}) %collective-permute-start.3) | collective-permute-done | bytes 65568 | tf_op jit(solution)/shard_map/ppermute | solution.py:347
  31.5 2.2 %shard_map.149 = (f32[256,512]{1,0:T(8,128)S(1)}, f32[256,512]{1,0:T(8,128)S(1)}, f32[256,512]{1,0:T(8,128)S(1)}, f32[16,512]{1,0:T(8,128)S(1)}, f32[16,512]{1,0...) custom-call(s32[4]{0:T(128)S(1)} %add_convert_fusion.edge_ref, f32[256,512]{1,0:T(8,128)S(1)} %get-tuple-element.46.pl_ref, ...), custom_call_target="tpu_custom_call" | custom-call | tf_op jit(solution)/shard_map/pallas_call | solution.py:360
  33.8 1.9 %collective-permute-start.4 = (f32[16,512]{1,0:T(8,128)S(1)}, f32[16,512]{1,0:T(8,128)S(1)}, u32[]{:S(2)}, u32[]{:S(2)}) collective-permute-start(f32[16,512]{1,0:T(8,128)S(1)} %get-tuple-element.56), channel_id=1, source_target_pairs={{0,16},{16,32},{32,48},{48,64},{64,80},{80,96},{96,112},{112,128},... | collective-permute-start | bytes 98312 | tf_op jit(solution)/shard_map/ppermute | solution.py:338
  35.7 7.3 %collective-permute-start.5 = (f32[16,512]{1,0:T(8,128)S(1)}, f32[16,512]{1,0:T(8,128)S(1)}, u32[]{:S(2)}, u32[]{:S(2)}) collective-permute-start(f32[16,512]{1,0:T(8,128)S(1)} %get-tuple-element.57), channel_id=1, source_target_pairs={{16,0},{32,16},{48,32},{64,48},{80,64},{96,80},{112,96},{128,112},... | collective-permute-start | bytes 98312 | tf_op jit(solution)/shard_map/ppermute | solution.py:339
  44.1 4.4 %collective-permute-start.7 = (f32[16,512]{1,0:T(8,128)S(1)}, f32[16,512]{1,0:T(8,128)S(1)}, u32[]{:S(2)}, u32[]{:S(2)}) collective-permute-start(f32[16,512]{1,0:T(8,128)S(1)} %get-tuple-element.121), channel_id=1, source_target_pairs={{1,0},{2,1},{3,2},{4,3},{5,4},{6,5},{7,6},{8,7},{9,8},{10,9},{11,1... | collective-permute-start | bytes 98312 | tf_op jit(solution)/shard_map/ppermute | solution.py:347
  49.7 2.2 %shard_map.150 = (f32[256,512]{1,0:T(8,128)S(1)}, f32[256,512]{1,0:T(8,128)S(1)}, f32[16,512]{1,0:T(8,128)S(1)}, f32[16,512]{1,0:T(8,128)S(1)}, f32[16,512]{1,0:T(8,128)S(1)}, /*index=5*/f32[16,512]{1,0:T(8,128)S(1)}) custom-call(s32[4]{0:T(128)S(1)} %add_convert_fusion.edge_ref, f32[256,512]{1,0:T(8,128)S(1)} %get-tuple-element.55.pin_ref, ...), custom_call_target="tpu_custom_call" | custom-call | tf_op jit(solution)/shard_map/pallas_call | solution.py:363
  51.9 1.9 %collective-permute-start.8 = (f32[16,512]{1,0:T(8,128)S(1)}, f32[16,512]{1,0:T(8,128)S(1)}, u32[]{:S(2)}, u32[]{:S(2)}) collective-permute-start(f32[16,512]{1,0:T(8,128)S(1)} %get-tuple-element.63), channel_id=1, source_target_pairs={{0,16},{16,32},{32,48},{48,64},{64,80},{80,96},{96,112},{112,128},... | collective-permute-start | bytes 98312 | tf_op jit(solution)/shard_map/ppermute | solution.py:338
  53.8 7.3 %collective-permute-start.9 = (f32[16,512]{1,0:T(8,128)S(1)}, f32[16,512]{1,0:T(8,128)S(1)}, u32[]{:S(2)}, u32[]{:S(2)}) collective-permute-start(f32[16,512]{1,0:T(8,128)S(1)} %get-tuple-element.64), channel_id=1, source_target_pairs={{16,0},{32,16},{48,32},{64,48},{80,64},{96,80},{112,96},{128,112},... | collective-permute-start | bytes 98312 | tf_op jit(solution)/shard_map/ppermute | solution.py:339
  62.2 4.2 %collective-permute-start.11 = (f32[16,512]{1,0:T(8,128)S(1)}, f32[16,512]{1,0:T(8,128)S(1)}, u32[]{:S(2)}, u32[]{:S(2)}) collective-permute-start(f32[16,512]{1,0:T(8,128)S(1)} %get-tuple-element.119), channel_id=1, source_target_pairs={{1,0},{2,1},{3,2},{4,3},{5,4},{6,5},{7,6},{8,7},{9,8},{10,9},{11,1... | collective-permute-start | bytes 98312 | tf_op jit(solution)/shard_map/ppermute | solution.py:347
  67.6 2.3 %shard_map.151 = (f32[256,512]{1,0:T(8,128)S(1)}, f32[256,512]{1,0:T(8,128)S(1)}, f32[16,512]{1,0:T(8,128)S(1)}, f32[16,512]{1,0:T(8,128)S(1)}, f32[16,512]{1,0:...) custom-call(s32[4]{0:T(128)S(1)} %add_convert_fusion.edge_ref, f32[256,512]{1,0:T(8,128)S(1)} %get-tuple-element.62.pin_ref, ...), custom_call_target="tpu_custom_call" | custom-call | tf_op jit(solution)/shard_map/pallas_call | solution.py:367
  71.8 7.3 %collective-permute-start.13 = (f32[16,512]{1,0:T(8,128)S(1)}, f32[16,512]{1,0:T(8,128)S(1)}, u32[]{:S(2)}, u32[]{:S(2)}) collective-permute-start(f32[16,512]{1,0:T(8,128)S(1)} %get-tuple-element.70), channel_id=1, source_target_pairs={{16,0},{32,16},{48,32},{64,48},{80,64},{96,80},{112,96},{128,112},... | collective-permute-start | bytes 98312 | tf_op jit(solution)/shard_map/ppermute | solution.py:339
  80.2 4.2 %collective-permute-start.15 = (f32[16,512]{1,0:T(8,128)S(1)}, f32[16,512]{1,0:T(8,128)S(1)}, u32[]{:S(2)}, u32[]{:S(2)}) collective-permute-start(f32[16,512]{1,0:T(8,128)S(1)} %get-tuple-element.117), channel_id=1, source_target_pairs={{1,0},{2,1},{3,2},{4,3},{5,4},{6,5},{7,6},{8,7},{9,8},{10,9},{11,1... | collective-permute-start | bytes 98312 | tf_op jit(solution)/shard_map/ppermute | solution.py:347
  85.6 2.2 %shard_map.152 = (f32[256,512]{1,0:T(8,128)S(1)}, f32[256,512]{1,0:T(8,128)S(1)}, f32[16,512]{1,0:T(8,128)S(1)}, f32[16,512]{1,0:T(8,128)S(1)}, f32[16,512]{1,0:...) custom-call(s32[4]{0:T(128)S(1)} %add_convert_fusion.edge_ref, f32[256,512]{1,0:T(8,128)S(1)} %get-tuple-element.68.pin_ref, ...), custom_call_target="tpu_custom_call" | custom-call | tf_op jit(solution)/shard_map/pallas_call | solution.py:371
  87.8 1.9 %collective-permute-start.16 = (f32[16,512]{1,0:T(8,128)S(1)}, f32[16,512]{1,0:T(8,128)S(1)}, u32[]{:S(2)}, u32[]{:S(2)}) collective-permute-start(f32[16,512]{1,0:T(8,128)S(1)} %get-tuple-element.75), channel_id=1, source_target_pairs={{0,16},{16,32},{32,48},{48,64},{64,80},{80,96},{96,112},{112,128},... | collective-permute-start | bytes 98312 | tf_op jit(solution)/shard_map/ppermute | solution.py:338
  89.7 7.3 %collective-permute-start.17 = (f32[16,512]{1,0:T(8,128)S(1)}, f32[16,512]{1,0:T(8,128)S(1)}, u32[]{:S(2)}, u32[]{:S(2)}) collective-permute-start(f32[16,512]{1,0:T(8,128)S(1)} %get-tuple-element.76), channel_id=1, source_target_pairs={{16,0},{32,16},{48,32},{64,48},{80,64},{96,80},{112,96},{128,112},... | collective-permute-start | bytes 98312 | tf_op jit(solution)/shard_map/ppermute | solution.py:339
  98.1 4.2 %collective-permute-start.19 = (f32[16,512]{1,0:T(8,128)S(1)}, f32[16,512]{1,0:T(8,128)S(1)}, u32[]{:S(2)}, u32[]{:S(2)}) collective-permute-start(f32[16,512]{1,0:T(8,128)S(1)} %get-tuple-element.115), channel_id=1, source_target_pairs={{1,0},{2,1},{3,2},{4,3},{5,4},{6,5},{7,6},{8,7},{9,8},{10,9},{11,1... | collective-permute-start | bytes 98312 | tf_op jit(solution)/shard_map/ppermute | solution.py:347
  103.5 2.9 %shard_map.153 = (f32[256,512]{1,0:T(8,128)S(1)}, f32[256,512]{1,0:T(8,128)S(1)}, f32[16,512]{1,0:T(8,128)S(1)}, f32[16,512]{1,0:T(8,128)S(1)}, f32[16,512]{1,0:...) custom-call(s32[4]{0:T(128)S(1)} %add_convert_fusion.edge_ref, f32[256,512]{1,0:T(8,128)S(1)} %get-tuple-element.74.pin_ref, ...), custom_call_target="tpu_custom_call" | custom-call | tf_op jit(solution)/shard_map/pallas_call | solution.py:375
  108.3 8.8 %all-to-all-start = ((f32[16,1,128]{2,1,0:T(1,128)}), f32[16,1,128]{2,1,0:T(1,128)S(1)}, u32[]{:S(2)}, u32[]{:S(2)}) async-start(f32[16,1,128]{2,1,0:T(1,128)} %bitcast.5), calls=%async_computation | async-start | bytes 16384 | tf_op jit(solution)/shard_map/all_to_all | solution.py:377
  117.1 7.3 %collective-permute-start.21 = (f32[16,512]{1,0:T(8,128)S(1)}, f32[16,512]{1,0:T(8,128)S(1)}, u32[]{:S(2)}, u32[]{:S(2)}) collective-permute-start(f32[16,512]{1,0:T(8,128)S(1)} %get-tuple-element.85), channel_id=1, source_target_pairs={{16,0},{32,16},{48,32},{64,48},{80,64},{96,80},{112,96},{128,112},... | collective-permute-start | bytes 98312 | tf_op jit(solution)/shard_map/ppermute | solution.py:339
  128.0 15.5 %all_to_all.15 = f32[32,1,128]{2,1,0:T(1,128)S(1)} all-to-all(f32[32,1,128]{2,1,0:T(1,128)S(1)} %broadcast_in_dim.23), channel_id=1, replica_groups=mesh['gx'=32,'gy'=16] {'gx'}, dimensions={0} | all-to-all | bytes 32768 | tf_op jit(solution)/shard_map/all_to_all | solution.py:379
  143.5 2.1 %shard_map.154 = (f32[16,16,512]{2,1,0:T(8,128)}, f32[16,16,512]{2,1,0:T(8,128)}, f32[16,16,512]{2,1,0:T(8,128)}) custom-call(f32[128]{0:T(128)S(1)} %reduce_sum.19.dots_ref, f32[256,512]{1,0:T(8,128)S(1)} %get-tuple-element.83.pin_ref, f32[16,512]{1,0:T(8,128)S(1)} %collective-permute-done.20.xl_ref, f32[16,512]{1,0:T(8,128)S(1)} %collective-permute-done.21.xr_ref, ...), custom_call_target="tpu_custom_call" | custom-call | tf_op jit(solution)/shard_map/pallas_call | solution.py:381
  (86 shorter events, 27.2 us)
Async XLA Ops:
  9.6 15.9 %collective-permute-start = (f32[2,16,512]{2,1,0:T(8,128)S(1)}, f32[2,16,512]{2,1,0:T(8,128)S(1)}, u32[]{:S(2)}, u32[]{:S(2)}) collective-permute-start(f32[2,16,512]{2,1,0:T(8,128)S(1)} %get-tuple-element.48), channel_id=1, source_target_pairs={{0,16},{16,32},{32,48},{48,64},{64,80},{80,96},{96,112},{112,128},... | collective-permute-start | bytes 196616 | tf_op jit(solution)/shard_map/ppermute | solution.py:338
  14.6 12.1 %collective-permute-start.1 = (f32[2,16,512]{2,1,0:T(8,128)S(1)}, f32[2,16,512]{2,1,0:T(8,128)S(1)}, u32[]{:S(2)}, u32[]{:S(2)}) collective-permute-start(f32[2,16,512]{2,1,0:T(8,128)S(1)} %get-tuple-element.49), channel_id=1, source_target_pairs={{16,0},{32,16},{48,32},{64,48},{80,64},{96,80},{112,96},{128,112},... | collective-permute-start | bytes 196616 | tf_op jit(solution)/shard_map/ppermute | solution.py:339
  26.8 4.7 %collective-permute-start.3 = (f32[2,16,512]{2,1,0:T(8,128)S(1)}, f32[2,16,512]{2,1,0:T(8,128)S(1)}, u32[]{:S(2)}, u32[]{:S(2)}) collective-permute-start(f32[2,16,512]{2,1,0:T(8,128)S(1)} %get-tuple-element.123), channel_id=1, source_target_pairs={{1,0},{2,1},{3,2},{4,3},{5,4},{6,5},{7,6},{8,7},{9,8},{10,9},{11,1... | collective-permute-start | bytes 196616 | tf_op jit(solution)/shard_map/ppermute | solution.py:347
  28.3 3.1 %collective-permute-start.2 = (f32[2,16,512]{2,1,0:T(8,128)S(1)}, f32[2,16,512]{2,1,0:T(8,128)S(1)}, u32[]{:S(2)}, u32[]{:S(2)}) collective-permute-start(f32[2,16,512]{2,1,0:T(8,128)S(1)} %get-tuple-element.124), channel_id=1, source_target_pairs={{0,1},{1,2},{2,3},{3,4},{4,5},{5,6},{6,7},{7,8},{8,9},{9,10},{10,1... | collective-permute-start | bytes 196616 | tf_op jit(solution)/shard_map/ppermute | solution.py:346
  33.8 9.3 %collective-permute-start.4 = (f32[16,512]{1,0:T(8,128)S(1)}, f32[16,512]{1,0:T(8,128)S(1)}, u32[]{:S(2)}, u32[]{:S(2)}) collective-permute-start(f32[16,512]{1,0:T(8,128)S(1)} %get-tuple-element.56), channel_id=1, source_target_pairs={{0,16},{16,32},{32,48},{48,64},{64,80},{80,96},{96,112},{112,128},... | collective-permute-start | bytes 98312 | tf_op jit(solution)/shard_map/ppermute | solution.py:338
  35.7 8.3 %collective-permute-start.5 = (f32[16,512]{1,0:T(8,128)S(1)}, f32[16,512]{1,0:T(8,128)S(1)}, u32[]{:S(2)}, u32[]{:S(2)}) collective-permute-start(f32[16,512]{1,0:T(8,128)S(1)} %get-tuple-element.57), channel_id=1, source_target_pairs={{16,0},{32,16},{48,32},{64,48},{80,64},{96,80},{112,96},{128,112},... | collective-permute-start | bytes 98312 | tf_op jit(solution)/shard_map/ppermute | solution.py:339
  44.1 5.2 %collective-permute-start.7 = (f32[16,512]{1,0:T(8,128)S(1)}, f32[16,512]{1,0:T(8,128)S(1)}, u32[]{:S(2)}, u32[]{:S(2)}) collective-permute-start(f32[16,512]{1,0:T(8,128)S(1)} %get-tuple-element.121), channel_id=1, source_target_pairs={{1,0},{2,1},{3,2},{4,3},{5,4},{6,5},{7,6},{8,7},{9,8},{10,9},{11,1... | collective-permute-start | bytes 98312 | tf_op jit(solution)/shard_map/ppermute | solution.py:347
  48.5 1.2 collective-permute-start.6
  51.9 9.2 %collective-permute-start.8 = (f32[16,512]{1,0:T(8,128)S(1)}, f32[16,512]{1,0:T(8,128)S(1)}, u32[]{:S(2)}, u32[]{:S(2)}) collective-permute-start(f32[16,512]{1,0:T(8,128)S(1)} %get-tuple-element.63), channel_id=1, source_target_pairs={{0,16},{16,32},{32,48},{48,64},{64,80},{80,96},{96,112},{112,128},... | collective-permute-start | bytes 98312 | tf_op jit(solution)/shard_map/ppermute | solution.py:338
  53.8 8.3 %collective-permute-start.9 = (f32[16,512]{1,0:T(8,128)S(1)}, f32[16,512]{1,0:T(8,128)S(1)}, u32[]{:S(2)}, u32[]{:S(2)}) collective-permute-start(f32[16,512]{1,0:T(8,128)S(1)} %get-tuple-element.64), channel_id=1, source_target_pairs={{16,0},{32,16},{48,32},{64,48},{80,64},{96,80},{112,96},{128,112},... | collective-permute-start | bytes 98312 | tf_op jit(solution)/shard_map/ppermute | solution.py:339
  62.2 5.1 %collective-permute-start.11 = (f32[16,512]{1,0:T(8,128)S(1)}, f32[16,512]{1,0:T(8,128)S(1)}, u32[]{:S(2)}, u32[]{:S(2)}) collective-permute-start(f32[16,512]{1,0:T(8,128)S(1)} %get-tuple-element.119), channel_id=1, source_target_pairs={{1,0},{2,1},{3,2},{4,3},{5,4},{6,5},{7,6},{8,7},{9,8},{10,9},{11,1... | collective-permute-start | bytes 98312 | tf_op jit(solution)/shard_map/ppermute | solution.py:347
  66.4 1.2 collective-permute-start.10
  69.9 9.2 %collective-permute-start.12 = (f32[16,512]{1,0:T(8,128)S(1)}, f32[16,512]{1,0:T(8,128)S(1)}, u32[]{:S(2)}, u32[]{:S(2)}) collective-permute-start(f32[16,512]{1,0:T(8,128)S(1)} %get-tuple-element.69), channel_id=1, source_target_pairs={{0,16},{16,32},{32,48},{48,64},{64,80},{80,96},{96,112},{112,128},... | collective-permute-start | bytes 98312 | tf_op jit(solution)/shard_map/ppermute | solution.py:338
  71.8 8.3 %collective-permute-start.13 = (f32[16,512]{1,0:T(8,128)S(1)}, f32[16,512]{1,0:T(8,128)S(1)}, u32[]{:S(2)}, u32[]{:S(2)}) collective-permute-start(f32[16,512]{1,0:T(8,128)S(1)} %get-tuple-element.70), channel_id=1, source_target_pairs={{16,0},{32,16},{48,32},{64,48},{80,64},{96,80},{112,96},{128,112},... | collective-permute-start | bytes 98312 | tf_op jit(solution)/shard_map/ppermute | solution.py:339
  80.2 5.1 %collective-permute-start.15 = (f32[16,512]{1,0:T(8,128)S(1)}, f32[16,512]{1,0:T(8,128)S(1)}, u32[]{:S(2)}, u32[]{:S(2)}) collective-permute-start(f32[16,512]{1,0:T(8,128)S(1)} %get-tuple-element.117), channel_id=1, source_target_pairs={{1,0},{2,1},{3,2},{4,3},{5,4},{6,5},{7,6},{8,7},{9,8},{10,9},{11,1... | collective-permute-start | bytes 98312 | tf_op jit(solution)/shard_map/ppermute | solution.py:347
  84.4 1.2 collective-permute-start.14
  87.8 9.2 %collective-permute-start.16 = (f32[16,512]{1,0:T(8,128)S(1)}, f32[16,512]{1,0:T(8,128)S(1)}, u32[]{:S(2)}, u32[]{:S(2)}) collective-permute-start(f32[16,512]{1,0:T(8,128)S(1)} %get-tuple-element.75), channel_id=1, source_target_pairs={{0,16},{16,32},{32,48},{48,64},{64,80},{80,96},{96,112},{112,128},... | collective-permute-start | bytes 98312 | tf_op jit(solution)/shard_map/ppermute | solution.py:338
  89.7 8.3 %collective-permute-start.17 = (f32[16,512]{1,0:T(8,128)S(1)}, f32[16,512]{1,0:T(8,128)S(1)}, u32[]{:S(2)}, u32[]{:S(2)}) collective-permute-start(f32[16,512]{1,0:T(8,128)S(1)} %get-tuple-element.76), channel_id=1, source_target_pairs={{16,0},{32,16},{48,32},{64,48},{80,64},{96,80},{112,96},{128,112},... | collective-permute-start | bytes 98312 | tf_op jit(solution)/shard_map/ppermute | solution.py:339
  98.1 5.1 %collective-permute-start.19 = (f32[16,512]{1,0:T(8,128)S(1)}, f32[16,512]{1,0:T(8,128)S(1)}, u32[]{:S(2)}, u32[]{:S(2)}) collective-permute-start(f32[16,512]{1,0:T(8,128)S(1)} %get-tuple-element.115), channel_id=1, source_target_pairs={{1,0},{2,1},{3,2},{4,3},{5,4},{6,5},{7,6},{8,7},{9,8},{10,9},{11,1... | collective-permute-start | bytes 98312 | tf_op jit(solution)/shard_map/ppermute | solution.py:347
  106.4 18.0 %collective-permute-start.20 = (f32[16,512]{1,0:T(8,128)S(1)}, f32[16,512]{1,0:T(8,128)S(1)}, u32[]{:S(2)}, u32[]{:S(2)}) collective-permute-start(f32[16,512]{1,0:T(8,128)S(1)} %get-tuple-element.84), channel_id=1, source_target_pairs={{0,16},{16,32},{32,48},{48,64},{64,80},{80,96},{96,112},{112,128},... | collective-permute-start | bytes 98312 | tf_op jit(solution)/shard_map/ppermute | solution.py:338
  108.3 19.6 %all-to-all-start = ((f32[16,1,128]{2,1,0:T(1,128)}), f32[16,1,128]{2,1,0:T(1,128)S(1)}, u32[]{:S(2)}, u32[]{:S(2)}) async-start(f32[16,1,128]{2,1,0:T(1,128)} %bitcast.5), calls=%async_computation | async-start | bytes 16384 | tf_op jit(solution)/shard_map/all_to_all | solution.py:377
  117.1 8.3 %collective-permute-start.21 = (f32[16,512]{1,0:T(8,128)S(1)}, f32[16,512]{1,0:T(8,128)S(1)}, u32[]{:S(2)}, u32[]{:S(2)}) collective-permute-start(f32[16,512]{1,0:T(8,128)S(1)} %get-tuple-element.85), channel_id=1, source_target_pairs={{16,0},{32,16},{48,32},{64,48},{80,64},{96,80},{112,96},{128,112},... | collective-permute-start | bytes 98312 | tf_op jit(solution)/shard_map/ppermute | solution.py:339
  125.4 18.0 %collective-permute-start.23 = (f32[16,512]{1,0:T(8,128)S(1)}, f32[16,512]{1,0:T(8,128)S(1)}, u32[]{:S(2)}, u32[]{:S(2)}) collective-permute-start(f32[16,512]{1,0:T(8,128)S(1)} %get-tuple-element.113), channel_id=1, source_target_pairs={{1,0},{2,1},{3,2},{4,3},{5,4},{6,5},{7,6},{8,7},{9,8},{10,9},{11,1... | collective-permute-start | bytes 98312 | tf_op jit(solution)/shard_map/ppermute | solution.py:347
  126.4 17.1 %collective-permute-start.22 = (f32[16,512]{1,0:T(8,128)S(1)}, f32[16,512]{1,0:T(8,128)S(1)}, u32[]{:S(2)}, u32[]{:S(2)}) collective-permute-start(f32[16,512]{1,0:T(8,128)S(1)} %get-tuple-element.114), channel_id=1, source_target_pairs={{0,1},{1,2},{2,3},{3,4},{4,5},{5,6},{6,7},{7,8},{8,9},{9,10},{10,1... | collective-permute-start | bytes 98312 | tf_op jit(solution)/shard_map/ppermute | solution.py:346
  (15 other events, 121.9 us)

commit v3 on v2

--- a/solution.py
+++ b/solution.py
@@ -135,7 +135,7 @@
     return f + jnp.where(upper, nxt, jnp.where(lower, prv, 0.0))
 
 
-def emit_partial(f, edge_ref, p_ref, faces):
+def emit_partial(f, inside_ref, p_ref, faces):
     p_ref[...] = join_z(f)
     p_ref[112:128, :] = p_ref[112:128, :] + p_ref[128:144, :]
     p_ref[128:144, :] = p_ref[112:128, :]
@@ -147,8 +147,8 @@
         p_ref[r + 8:r + 9, :] = mid
         y_low[x:x + 1, :] = p_ref[r:r + 1, :]
         y_high[x:x + 1, :] = p_ref[r + 15:r + 16, :]
-    x_low[...] = jnp.where(edge_ref[0] == 1, 0.0, p_ref[0:16, :])
-    x_high[...] = jnp.where(edge_ref[1] == 1, 0.0, p_ref[240:256, :])
+    x_low[...] = inside_ref[0:1, :] * p_ref[0:16, :]
+    x_high[...] = inside_ref[1:2, :] * p_ref[240:256, :]
 
 
 def take_sum(p_ref, recv, s_ref):
@@ -168,7 +168,7 @@
     return part[:, 0:128] + part[:, 128:256] + part[:, 256:384] + part[:, 384:512]
 
 
-def first_kernel(edge_ref, table_hbm, load_hbm, cond_hbm, flags_hbm, region_hbm, sq_hbm, sqz_hbm, wr_hbm, wz_hbm,
+def first_kernel(inside_ref, table_hbm, load_hbm, cond_hbm, flags_hbm, region_hbm, sq_hbm, sqz_hbm, wr_hbm, wz_hbm,
                  coef_ref, react_ref, keep_ref, pl_ref, pd_ref, xl_ref, xh_ref, yl_ref, yh_ref,
                  table_ref, load_ref, cond_ref, flags_ref, region_ref, sq_ref, sqz_ref, wr_ref, wz_ref, sems):
     flags_tile = flags_hbm.at[:, :, pl.ds(0, 128)]
@@ -209,11 +209,11 @@
         rows.append(dot(sq_ref[0], pair) + dot(sq_ref[1], pair))
     diag = jnp.concatenate(rows, 0) + mul_z(high, low, sqz_ref[...]) + react_ref[...]
     faces = (xl_ref, xh_ref, yl_ref, yh_ref)
-    emit_partial(diag, edge_ref, pd_ref, [face.at[1] for face in faces])
-    emit_partial(load_ref[...].reshape(ROWS, COLS), edge_ref, pl_ref, [face.at[0] for face in faces])
-
-
-def second_kernel(edge_ref, pl_ref, pd_ref, xl_ref, xr_ref, yb_ref, ya_ref, keep_ref, coef_ref, react_ref,
+    emit_partial(diag, inside_ref, pd_ref, [face.at[1] for face in faces])
+    emit_partial(load_ref[...].reshape(ROWS, COLS), inside_ref, pl_ref, [face.at[0] for face in faces])
+
+
+def second_kernel(inside_ref, pl_ref, pd_ref, xl_ref, xr_ref, yb_ref, ya_ref, keep_ref, coef_ref, react_ref,
                   grad_ref, back_ref, gz_ref, bz_ref,
                   r_ref, dinv_ref, p_ref, lo_x, hi_x, lo_y, hi_y, s_ref):
     diag = take_sum(pd_ref, (xl_ref[1], xr_ref[1], yb_ref[1], ya_ref[1]), s_ref)
@@ -225,10 +225,10 @@
     r_ref[:, 0:128] = keep * r_ref[:, 0:128]
     a0 = dinv_ref[...] * r_ref[...] * (1.0 / CENTER)
     f = local_op(a0, coef_ref[...], react_ref[...], grad_ref, back_ref, gz_ref[...], bz_ref[...])
-    emit_partial(f, edge_ref, p_ref, (lo_x, hi_x, lo_y, hi_y))
-
-
-def sweep1_kernel(edge_ref, pin_ref, xl_ref, xr_ref, yb_ref, ya_ref, r_ref, dinv_ref, coef_ref, react_ref,
+    emit_partial(f, inside_ref, p_ref, (lo_x, hi_x, lo_y, hi_y))
+
+
+def sweep1_kernel(inside_ref, pin_ref, xl_ref, xr_ref, yb_ref, ya_ref, r_ref, dinv_ref, coef_ref, react_ref,
                   grad_ref, back_ref, gz_ref, bz_ref,
                   a1_ref, p_ref, lo_x, hi_x, lo_y, hi_y, s_ref):
     image = take_sum(pin_ref, (xl_ref[...], xr_ref[...], yb_ref[...], ya_ref[...]), s_ref)
@@ -237,7 +237,7 @@
     a1 = (1.0 + MIX1) * a0 + GAIN1 * (dinv * (r - image))
     a1_ref[...] = a1
     f = local_op(a1, coef_ref[...], react_ref[...], grad_ref, back_ref, gz_ref[...], bz_ref[...])
-    emit_partial(f, edge_ref, p_ref, (lo_x, hi_x, lo_y, hi_y))
+    emit_partial(f, inside_ref, p_ref, (lo_x, hi_x, lo_y, hi_y))
 
 
 def sweep2(image, a1, r, dinv):
@@ -245,7 +245,7 @@
     return a1 + (MIX2 * (a1 - a0) + GAIN2 * (dinv * (r - image)))
 
 
-def third_kernel(edge_ref, pin_ref, xl_ref, xr_ref, yb_ref, ya_ref, r_ref, dinv_ref, a1_ref, load_ref, coef_ref, react_ref,
+def third_kernel(inside_ref, pin_ref, xl_ref, xr_ref, yb_ref, ya_ref, r_ref, dinv_ref, a1_ref, load_ref, coef_ref, react_ref,
                  grad_ref, back_ref, gz_ref, bz_ref,
                  z_ref, p_ref, lo_x, hi_x, lo_y, hi_y, dots_ref, s_ref):
     image = take_sum(pin_ref, (xl_ref[...], xr_ref[...], yb_ref[...], ya_ref[...]), s_ref)
@@ -254,10 +254,10 @@
     dots_ref[0] = fold(load_ref[...].reshape(ROWS, COLS) * z)
     f = local_op(z, coef_ref[...], react_ref[...], grad_ref, back_ref, gz_ref[...], bz_ref[...])
     dots_ref[1] = fold(f * z)
-    emit_partial(f, edge_ref, p_ref, (lo_x, hi_x, lo_y, hi_y))
-
-
-def fourth_kernel(edge_ref, pin_ref, xl_ref, xr_ref, yb_ref, ya_ref, dinv_ref, z_ref, coef_ref, react_ref,
+    emit_partial(f, inside_ref, p_ref, (lo_x, hi_x, lo_y, hi_y))
+
+
+def fourth_kernel(inside_ref, pin_ref, xl_ref, xr_ref, yb_ref, ya_ref, dinv_ref, z_ref, coef_ref, react_ref,
                   grad_ref, back_ref, gz_ref, bz_ref,
                   im_ref, p_ref, lo_x, hi_x, lo_y, hi_y, dots_ref, s_ref):
     image = take_sum(pin_ref, (xl_ref[...], xr_ref[...], yb_ref[...], ya_ref[...]), s_ref)
@@ -267,10 +267,10 @@
     b0 = dinv * im * (1.0 / CENTER)
     f = local_op(b0, coef_ref[...], react_ref[...], grad_ref, back_ref, gz_ref[...], bz_ref[...])
     dots_ref[...] = fold(f * z_ref[...])
-    emit_partial(f, edge_ref, p_ref, (lo_x, hi_x, lo_y, hi_y))
-
-
-def fifth_kernel(edge_ref, pin_ref, xl_ref, xr_ref, yb_ref, ya_ref, im_ref, dinv_ref, z_ref, d34_ref, d5_ref, coef_ref, react_ref,
+    emit_partial(f, inside_ref, p_ref, (lo_x, hi_x, lo_y, hi_y))
+
+
+def fifth_kernel(inside_ref, pin_ref, xl_ref, xr_ref, yb_ref, ya_ref, im_ref, dinv_ref, z_ref, d34_ref, d5_ref, coef_ref, react_ref,
                  grad_ref, back_ref, gz_ref, bz_ref,
                  b1_ref, p_ref, lo_x, hi_x, lo_y, hi_y, dots_ref, s_ref):
     image = take_sum(pin_ref, (xl_ref[...], xr_ref[...], yb_ref[...], ya_ref[...]), s_ref)
@@ -279,7 +279,7 @@
     b1 = (1.0 + MIX1) * b0 + GAIN1 * (dinv * (im - image))
     b1_ref[...] = b1
     f = local_op(b1, coef_ref[...], react_ref[...], grad_ref, back_ref, gz_ref[...], bz_ref[...])
-    emit_partial(f, edge_ref, p_ref, (lo_x, hi_x, lo_y, hi_y))
+    emit_partial(f, inside_ref, p_ref, (lo_x, hi_x, lo_y, hi_y))
     last = fold(f * ((1.0 + MIX2) * z_ref[...] - (CENTER * GAIN2) * b0))
     both = last + (CENTER * GAIN2 - MIX2) * d5_ref[...]
     lane = lax.broadcasted_iota(jnp.int32, (1, 128), 1)
@@ -318,8 +318,8 @@
         scratch_shapes=scratch, compiler_params=PARAMS)
 
 
-def step_call(kernel, outs, n_in):
-    return call(kernel, outs, [SM] + [VM] * n_in, [pltpu.VMEM((ROWS, COLS), F32)])
+def step_call(kernel, outs, n_in, first=VM):
+    return call(kernel, outs, [first] + [VM] * n_in, [pltpu.VMEM((ROWS, COLS), F32)])
 
 
 def per_device(load, conductivity, flags, region, kappa_table):
@@ -327,7 +327,8 @@
     mats = (k["grad"], k["back"], k["grad_z"], k["back_z"])
     n_x, n_y = lax.axis_size("gx"), lax.axis_size("gy")
     at_x, at_y = lax.axis_index("gx"), lax.axis_index("gy")
-    edge = jnp.stack([at_x == 0, at_x == n_x - 1, at_y == 0, at_y == n_y - 1]).astype(jnp.int32)
+    inside = jnp.stack([at_x != 0, at_x != n_x - 1]).astype(F32)
+    inside = jnp.broadcast_to(inside[:, None], (2, COLS))
     up_x = [(i, (i + 1) % n_x) for i in range(n_x)]
     up_y = [(i, (i + 1) % n_y) for i in range(n_y)]
     down_x = [(j, i) for i, j in up_x]
@@ -350,35 +351,36 @@
     two = jax.ShapeDtypeStruct((2, 16, COLS), F32)
     keep_shape = jax.ShapeDtypeStruct((ROWS, 128), F32)
     inputs = (kappa_table, load, conductivity, flags, region, k["sq"], k["sq_z"], k["w_rows"], k["w_z"])
+    inputs = tuple(pltpu.with_memory_space_constraint(v, pltpu.HBM) for v in inputs)
     buffers = [pltpu.VMEM(v.shape, v.dtype) for v in inputs]
     buffers[0] = pltpu.SMEM(kappa_table.shape, F32)
     buffers[3] = pltpu.VMEM((16, 16, 128), jnp.int32)
     coef, react, keep, part_l, part_d, *faces = call(
-        first_kernel, (BIG, BIG, keep_shape, BIG, BIG, two, two, two, two), [SM] + [HB] * len(inputs),
-        buffers + [pltpu.SemaphoreType.DMA((len(inputs),))])(edge, *inputs)
+        first_kernel, (BIG, BIG, keep_shape, BIG, BIG, two, two, two, two), [VM] + [HB] * len(inputs),
+        buffers + [pltpu.SemaphoreType.DMA((len(inputs),))])(inside, *inputs)
     recv = exchange(faces)
     r, dinv, part, *faces = step_call(second_kernel, (BIG, BIG) + PART, 13)(
-        edge, part_l, part_d, *recv, keep, coef, react, *mats)
+        inside, part_l, part_d, *recv, keep, coef, react, *mats)
     recv = exchange(faces)
     a1, part, *faces = step_call(sweep1_kernel, (BIG,) + PART, 13)(
-        edge, part, *recv, r, dinv, coef, react, *mats)
+        inside, part, *recv, r, dinv, coef, react, *mats)
     recv = exchange(faces)
     d34_shape = jax.ShapeDtypeStruct((2, 8, 128), F32)
     z, part, *faces, d34 = step_call(third_kernel, (BIG,) + PART + (d34_shape,), 15)(
-        edge, part, *recv, r, dinv, a1, load, coef, react, *mats)
+        inside, part, *recv, r, dinv, a1, load, coef, react, *mats)
     recv = exchange(faces)
     d5_shape = jax.ShapeDtypeStruct((8, 128), F32)
     im, part, *faces, d5 = step_call(fourth_kernel, (BIG,) + PART + (d5_shape,), 13)(
-        edge, part, *recv, dinv, z, coef, react, *mats)
+        inside, part, *recv, dinv, z, coef, react, *mats)
     recv = exchange(faces)
     dots_shape = jax.ShapeDtypeStruct((n_y, 128), F32)
     b1, part, *faces, dots = step_call(fifth_kernel, (BIG,) + PART + (dots_shape,), 16)(
-        edge, part, *recv, im, dinv, z, d34, d5, coef, react, *mats)
+        inside, part, *recv, im, dinv, z, d34, d5, coef, react, *mats)
     total = lax.all_to_all(dots, "gy", 0, 0, tiled=True).sum(0)
     recv = exchange(faces)
     total = lax.all_to_all(jnp.broadcast_to(total, (n_x, 128)), "gx", 0, 0, tiled=True).sum(0)
     shape = jax.ShapeDtypeStruct((16, 16, COLS), F32)
-    return step_call(last_kernel, (shape, shape, shape), 10)(
+    return step_call(last_kernel, (shape, shape, shape), 10, SM)(
         total, part, *recv, im, dinv, b1, z, r)
 
 

time: 146 us -> 144 us (0.986)
  Pallas kernels: 16.4 us -> 13.3 us
    unnamed x28 -> x26, local copies, waits for them, and re-layouts: 6.38 us -> 6.55 us
where the time goes in v3:
time: 144 us; the launch traced here: 143 us
  starting transfers between devices  92.7 us (64%)
  blocking collectives  15.5 us (11%)
  Pallas kernels  13.3 us (9%)
  waiting for transfers between devices  12.9 us (9%)
  local copies, waits for them, and re-layouts  6.79 us (5%)
    ppermute x6, starting transfers between devices, exchange(): right = lax.ppermute(x_low, 'gx', down_x)  47.2 us
    ppermute x6, starting transfers between devices, exchange(): above = lax.ppermute(with_corners(y_low, 0, at_y == 0), 'gy', down_y)  19.5 us
    all_to_all x1, blocking collectives, per_device(): lax.all_to_all(jnp.broadcast_to(total, (n_x, 128)), 'gx', 0, 0, tiled=True)  15.5 us
    ppermute x6, starting transfers between devices, exchange(): left = lax.ppermute(x_high, 'gx', up_x)  14.5 us
    all_to_all x1, starting transfers between devices, per_device(): total = lax.all_to_all(dots, 'gy', 0, 0, tiled=True).sum(0)  8.76 us
    unnamed x26, local copies, waits for them, and re-layouts  6.55 us
    ppermute x6, waiting for transfers between devices, exchange(): right = lax.ppermute(x_low, 'gx', down_x)  6.09 us
    ppermute x6, waiting for transfers between devices, exchange(): above = lax.ppermute(with_corners(y_low, 0, at_y == 0), 'gy', down_y)  5.35 us
  transfers between devices with their start and end apart: 25, of which 15 were waited for; matrix products, arithmetic and copies ran while one was open for 0% of the time, Pallas kernels for 0%

profile of v3, /device:TPU:1, one launch (start us, length us, event | category | flops | bytes accessed | tf_op | source)
XLA Modules:
  0.0 142.7 jit_solution(2579723283655430337)
XLA Ops:
  0.8 2.3 %shard_map.148 = (f32[256,512]{1,0:T(8,128)S(1)}, f32[256,512]{1,0:T(8,128)S(1)}, f32[256,128]{1,0:T(8,128)S(1)}, f32[256,512]{1,0:T(8,128)S(1)}, f32[256,512]{1...) custom-call(f32[2,512]{1,0:T(2,128)S(1)} %broadcast_in_dim.27.inside, ...), custom_call_target="tpu_custom_call" | custom-call | tf_op jit(solution)/shard_map/pallas_call | solution.py:358
  3.9 5.0 %collective-permute-start = (f32[2,16,512]{2,1,0:T(8,128)S(1)}, f32[2,16,512]{2,1,0:T(8,128)S(1)}, u32[]{:S(2)}, u32[]{:S(2)}) collective-permute-start(f32[2,16,512]{2,1,0:T(8,128)S(1)} %get-tuple-element.48), channel_id=1, source_target_pairs={{0,16},{16,32},{32,48},{48,64},{64,80},{80,96},{96,112},{112,128},... | collective-permute-start | bytes 196616 | tf_op jit(solution)/shard_map/ppermute | solution.py:339
  8.9 10.8 %collective-permute-start.1 = (f32[2,16,512]{2,1,0:T(8,128)S(1)}, f32[2,16,512]{2,1,0:T(8,128)S(1)}, u32[]{:S(2)}, u32[]{:S(2)}) collective-permute-start(f32[2,16,512]{2,1,0:T(8,128)S(1)} %get-tuple-element.49), channel_id=1, source_target_pairs={{16,0},{32,16},{48,32},{64,48},{80,64},{96,80},{112,96},{128,112},... | collective-permute-start | bytes 196616 | tf_op jit(solution)/shard_map/ppermute | solution.py:340
  23.8 1.9 %collective-permute-done.3.ya_ref = f32[2,16,512]{2,1,0:T(8,128)S(1)} collective-permute-done((f32[2,16,512]{2,1,0:T(8,128)S(1)}, f32[2,16,512]{2,1,0:T(8,128)S(1)}, u32[]{:S(2)}, u32[]{:S(2)}) %collective-permute-start.3) | collective-permute-done | bytes 65568 | tf_op jit(solution)/shard_map/ppermute | solution.py:348
  26.8 1.7 %shard_map.149 = (f32[256,512]{1,0:T(8,128)S(1)}, f32[256,512]{1,0:T(8,128)S(1)}, f32[256,512]{1,0:T(8,128)S(1)}, f32[16,512]{1,0:T(8,128)S(1)}, f32[16,512]{1,0...) custom-call(f32[2,512]{1,0:T(2,128)S(1)} %broadcast_in_dim.27.inside_ref, ...), custom_call_target="tpu_custom_call" | custom-call | tf_op jit(solution)/shard_map/pallas_call | solution.py:362
  28.5 1.9 %collective-permute-start.4 = (f32[16,512]{1,0:T(8,128)S(1)}, f32[16,512]{1,0:T(8,128)S(1)}, u32[]{:S(2)}, u32[]{:S(2)}) collective-permute-start(f32[16,512]{1,0:T(8,128)S(1)} %get-tuple-element.56), channel_id=1, source_target_pairs={{0,16},{16,32},{32,48},{48,64},{64,80},{80,96},{96,112},{112,128},... | collective-permute-start | bytes 98312 | tf_op jit(solution)/shard_map/ppermute | solution.py:339
  30.4 7.3 %collective-permute-start.5 = (f32[16,512]{1,0:T(8,128)S(1)}, f32[16,512]{1,0:T(8,128)S(1)}, u32[]{:S(2)}, u32[]{:S(2)}) collective-permute-start(f32[16,512]{1,0:T(8,128)S(1)} %get-tuple-element.57), channel_id=1, source_target_pairs={{16,0},{32,16},{48,32},{64,48},{80,64},{96,80},{112,96},{128,112},... | collective-permute-start | bytes 98312 | tf_op jit(solution)/shard_map/ppermute | solution.py:340
  38.9 4.4 %collective-permute-start.7 = (f32[16,512]{1,0:T(8,128)S(1)}, f32[16,512]{1,0:T(8,128)S(1)}, u32[]{:S(2)}, u32[]{:S(2)}) collective-permute-start(f32[16,512]{1,0:T(8,128)S(1)} %get-tuple-element.121), channel_id=1, source_target_pairs={{1,0},{2,1},{3,2},{4,3},{5,4},{6,5},{7,6},{8,7},{9,8},{10,9},{11,1... | collective-permute-start | bytes 98312 | tf_op jit(solution)/shard_map/ppermute | solution.py:348
  46.1 1.9 %collective-permute-start.8 = (f32[16,512]{1,0:T(8,128)S(1)}, f32[16,512]{1,0:T(8,128)S(1)}, u32[]{:S(2)}, u32[]{:S(2)}) collective-permute-start(f32[16,512]{1,0:T(8,128)S(1)} %get-tuple-element.63), channel_id=1, source_target_pairs={{0,16},{16,32},{32,48},{48,64},{64,80},{80,96},{96,112},{112,128},... | collective-permute-start | bytes 98312 | tf_op jit(solution)/shard_map/ppermute | solution.py:339
  48.0 7.3 %collective-permute-start.9 = (f32[16,512]{1,0:T(8,128)S(1)}, f32[16,512]{1,0:T(8,128)S(1)}, u32[]{:S(2)}, u32[]{:S(2)}) collective-permute-start(f32[16,512]{1,0:T(8,128)S(1)} %get-tuple-element.64), channel_id=1, source_target_pairs={{16,0},{32,16},{48,32},{64,48},{80,64},{96,80},{112,96},{128,112},... | collective-permute-start | bytes 98312 | tf_op jit(solution)/shard_map/ppermute | solution.py:340
  56.4 4.2 %collective-permute-start.11 = (f32[16,512]{1,0:T(8,128)S(1)}, f32[16,512]{1,0:T(8,128)S(1)}, u32[]{:S(2)}, u32[]{:S(2)}) collective-permute-start(f32[16,512]{1,0:T(8,128)S(1)} %get-tuple-element.119), channel_id=1, source_target_pairs={{1,0},{2,1},{3,2},{4,3},{5,4},{6,5},{7,6},{8,7},{9,8},{10,9},{11,1... | collective-permute-start | bytes 98312 | tf_op jit(solution)/shard_map/ppermute | solution.py:348
  61.8 1.7 %shard_map.151 = (f32[256,512]{1,0:T(8,128)S(1)}, f32[256,512]{1,0:T(8,128)S(1)}, f32[16,512]{1,0:T(8,128)S(1)}, f32[16,512]{1,0:T(8,128)S(1)}, f32[16,512]{1,0:...) custom-call(f32[2,512]{1,0:T(2,128)S(1)} %broadcast_in_dim.27.inside_ref, ...), custom_call_target="tpu_custom_call" | custom-call | tf_op jit(solution)/shard_map/pallas_call | solution.py:369
  63.5 1.9 %collective-permute-start.12 = (f32[16,512]{1,0:T(8,128)S(1)}, f32[16,512]{1,0:T(8,128)S(1)}, u32[]{:S(2)}, u32[]{:S(2)}) collective-permute-start(f32[16,512]{1,0:T(8,128)S(1)} %get-tuple-element.69), channel_id=1, source_target_pairs={{0,16},{16,32},{32,48},{48,64},{64,80},{80,96},{96,112},{112,128},... | collective-permute-start | bytes 98312 | tf_op jit(solution)/shard_map/ppermute | solution.py:339
  65.4 7.3 %collective-permute-start.13 = (f32[16,512]{1,0:T(8,128)S(1)}, f32[16,512]{1,0:T(8,128)S(1)}, u32[]{:S(2)}, u32[]{:S(2)}) collective-permute-start(f32[16,512]{1,0:T(8,128)S(1)} %get-tuple-element.70), channel_id=1, source_target_pairs={{16,0},{32,16},{48,32},{64,48},{80,64},{96,80},{112,96},{128,112},... | collective-permute-start | bytes 98312 | tf_op jit(solution)/shard_map/ppermute | solution.py:340
  73.8 4.2 %collective-permute-start.15 = (f32[16,512]{1,0:T(8,128)S(1)}, f32[16,512]{1,0:T(8,128)S(1)}, u32[]{:S(2)}, u32[]{:S(2)}) collective-permute-start(f32[16,512]{1,0:T(8,128)S(1)} %get-tuple-element.117), channel_id=1, source_target_pairs={{1,0},{2,1},{3,2},{4,3},{5,4},{6,5},{7,6},{8,7},{9,8},{10,9},{11,1... | collective-permute-start | bytes 98312 | tf_op jit(solution)/shard_map/ppermute | solution.py:348
  80.9 1.9 %collective-permute-start.16 = (f32[16,512]{1,0:T(8,128)S(1)}, f32[16,512]{1,0:T(8,128)S(1)}, u32[]{:S(2)}, u32[]{:S(2)}) collective-permute-start(f32[16,512]{1,0:T(8,128)S(1)} %get-tuple-element.75), channel_id=1, source_target_pairs={{0,16},{16,32},{32,48},{48,64},{64,80},{80,96},{96,112},{112,128},... | collective-permute-start | bytes 98312 | tf_op jit(solution)/shard_map/ppermute | solution.py:339
  82.8 7.3 %collective-permute-start.17 = (f32[16,512]{1,0:T(8,128)S(1)}, f32[16,512]{1,0:T(8,128)S(1)}, u32[]{:S(2)}, u32[]{:S(2)}) collective-permute-start(f32[16,512]{1,0:T(8,128)S(1)} %get-tuple-element.76), channel_id=1, source_target_pairs={{16,0},{32,16},{48,32},{64,48},{80,64},{96,80},{112,96},{128,112},... | collective-permute-start | bytes 98312 | tf_op jit(solution)/shard_map/ppermute | solution.py:340
  91.1 4.2 %collective-permute-start.19 = (f32[16,512]{1,0:T(8,128)S(1)}, f32[16,512]{1,0:T(8,128)S(1)}, u32[]{:S(2)}, u32[]{:S(2)}) collective-permute-start(f32[16,512]{1,0:T(8,128)S(1)} %get-tuple-element.115), channel_id=1, source_target_pairs={{1,0},{2,1},{3,2},{4,3},{5,4},{6,5},{7,6},{8,7},{9,8},{10,9},{11,1... | collective-permute-start | bytes 98312 | tf_op jit(solution)/shard_map/ppermute | solution.py:348
  96.6 2.3 %shard_map.153 = (f32[256,512]{1,0:T(8,128)S(1)}, f32[256,512]{1,0:T(8,128)S(1)}, f32[16,512]{1,0:T(8,128)S(1)}, f32[16,512]{1,0:T(8,128)S(1)}, f32[16,512]{1,0:...) custom-call(f32[2,512]{1,0:T(2,128)S(1)} %broadcast_in_dim.27.inside_ref, ...), custom_call_target="tpu_custom_call" | custom-call | tf_op jit(solution)/shard_map/pallas_call | solution.py:377
  100.5 1.9 %collective-permute-start.20 = (f32[16,512]{1,0:T(8,128)S(1)}, f32[16,512]{1,0:T(8,128)S(1)}, u32[]{:S(2)}, u32[]{:S(2)}) collective-permute-start(f32[16,512]{1,0:T(8,128)S(1)} %get-tuple-element.84), channel_id=1, source_target_pairs={{0,16},{16,32},{32,48},{48,64},{64,80},{80,96},{96,112},{112,128},... | collective-permute-start | bytes 98312 | tf_op jit(solution)/shard_map/ppermute | solution.py:339
  102.4 8.8 %all-to-all-start = ((f32[16,1,128]{2,1,0:T(1,128)}), f32[16,1,128]{2,1,0:T(1,128)S(1)}, u32[]{:S(2)}, u32[]{:S(2)}) async-start(f32[16,1,128]{2,1,0:T(1,128)} %bitcast.3), calls=%async_computation | async-start | bytes 16384 | tf_op jit(solution)/shard_map/all_to_all | solution.py:379
  111.1 7.3 %collective-permute-start.21 = (f32[16,512]{1,0:T(8,128)S(1)}, f32[16,512]{1,0:T(8,128)S(1)}, u32[]{:S(2)}, u32[]{:S(2)}) collective-permute-start(f32[16,512]{1,0:T(8,128)S(1)} %get-tuple-element.85), channel_id=1, source_target_pairs={{16,0},{32,16},{48,32},{64,48},{80,64},{96,80},{112,96},{128,112},... | collective-permute-start | bytes 98312 | tf_op jit(solution)/shard_map/ppermute | solution.py:340
  122.1 15.5 %all_to_all.15 = f32[32,1,128]{2,1,0:T(1,128)S(1)} all-to-all(f32[32,1,128]{2,1,0:T(1,128)S(1)} %broadcast_in_dim.30), channel_id=1, replica_groups=mesh['gx'=32,'gy'=16] {'gx'}, dimensions={0} | all-to-all | bytes 32768 | tf_op jit(solution)/shard_map/all_to_all | solution.py:381
  140.7 2.1 %shard_map.154 = (f32[16,16,512]{2,1,0:T(8,128)}, f32[16,16,512]{2,1,0:T(8,128)}, f32[16,16,512]{2,1,0:T(8,128)}) custom-call(f32[128]{0:T(128)S(1)} %reduce_sum.19.dots_ref, f32[256,512]{1,0:T(8,128)S(1)} %copy-done.10, f32[16,512]{1,0:T(8,128)S(1)} %collective-permute-done.20.xl_ref, f32[16,512]{1,0:T(8,128)S(1)} %collective-permute-done.21.xr_ref, ...), custom_call_target="tpu_custom_call" | custom-call | tf_op jit(solution)/shard_map/pallas_call | solution.py:383
  (85 shorter events, 26.8 us)
Async XLA Ops:
  3.9 15.8 %collective-permute-start = (f32[2,16,512]{2,1,0:T(8,128)S(1)}, f32[2,16,512]{2,1,0:T(8,128)S(1)}, u32[]{:S(2)}, u32[]{:S(2)}) collective-permute-start(f32[2,16,512]{2,1,0:T(8,128)S(1)} %get-tuple-element.48), channel_id=1, source_target_pairs={{0,16},{16,32},{32,48},{48,64},{64,80},{80,96},{96,112},{112,128},... | collective-permute-start | bytes 196616 | tf_op jit(solution)/shard_map/ppermute | solution.py:339
  8.9 12.1 %collective-permute-start.1 = (f32[2,16,512]{2,1,0:T(8,128)S(1)}, f32[2,16,512]{2,1,0:T(8,128)S(1)}, u32[]{:S(2)}, u32[]{:S(2)}) collective-permute-start(f32[2,16,512]{2,1,0:T(8,128)S(1)} %get-tuple-element.49), channel_id=1, source_target_pairs={{16,0},{32,16},{48,32},{64,48},{80,64},{96,80},{112,96},{128,112},... | collective-permute-start | bytes 196616 | tf_op jit(solution)/shard_map/ppermute | solution.py:340
  21.1 4.7 %collective-permute-start.3 = (f32[2,16,512]{2,1,0:T(8,128)S(1)}, f32[2,16,512]{2,1,0:T(8,128)S(1)}, u32[]{:S(2)}, u32[]{:S(2)}) collective-permute-start(f32[2,16,512]{2,1,0:T(8,128)S(1)} %get-tuple-element.123), channel_id=1, source_target_pairs={{1,0},{2,1},{3,2},{4,3},{5,4},{6,5},{7,6},{8,7},{9,8},{10,9},{11,1... | collective-permute-start | bytes 196616 | tf_op jit(solution)/shard_map/ppermute | solution.py:348
  22.6 3.1 %collective-permute-start.2 = (f32[2,16,512]{2,1,0:T(8,128)S(1)}, f32[2,16,512]{2,1,0:T(8,128)S(1)}, u32[]{:S(2)}, u32[]{:S(2)}) collective-permute-start(f32[2,16,512]{2,1,0:T(8,128)S(1)} %get-tuple-element.124), channel_id=1, source_target_pairs={{0,1},{1,2},{2,3},{3,4},{4,5},{5,6},{6,7},{7,8},{8,9},{9,10},{10,1... | collective-permute-start | bytes 196616 | tf_op jit(solution)/shard_map/ppermute | solution.py:347
  28.5 9.3 %collective-permute-start.4 = (f32[16,512]{1,0:T(8,128)S(1)}, f32[16,512]{1,0:T(8,128)S(1)}, u32[]{:S(2)}, u32[]{:S(2)}) collective-permute-start(f32[16,512]{1,0:T(8,128)S(1)} %get-tuple-element.56), channel_id=1, source_target_pairs={{0,16},{16,32},{32,48},{48,64},{64,80},{80,96},{96,112},{112,128},... | collective-permute-start | bytes 98312 | tf_op jit(solution)/shard_map/ppermute | solution.py:339
  30.4 8.3 %collective-permute-start.5 = (f32[16,512]{1,0:T(8,128)S(1)}, f32[16,512]{1,0:T(8,128)S(1)}, u32[]{:S(2)}, u32[]{:S(2)}) collective-permute-start(f32[16,512]{1,0:T(8,128)S(1)} %get-tuple-element.57), channel_id=1, source_target_pairs={{16,0},{32,16},{48,32},{64,48},{80,64},{96,80},{112,96},{128,112},... | collective-permute-start | bytes 98312 | tf_op jit(solution)/shard_map/ppermute | solution.py:340
  38.9 5.2 %collective-permute-start.7 = (f32[16,512]{1,0:T(8,128)S(1)}, f32[16,512]{1,0:T(8,128)S(1)}, u32[]{:S(2)}, u32[]{:S(2)}) collective-permute-start(f32[16,512]{1,0:T(8,128)S(1)} %get-tuple-element.121), channel_id=1, source_target_pairs={{1,0},{2,1},{3,2},{4,3},{5,4},{6,5},{7,6},{8,7},{9,8},{10,9},{11,1... | collective-permute-start | bytes 98312 | tf_op jit(solution)/shard_map/ppermute | solution.py:348
  43.2 1.2 collective-permute-start.6
  46.1 9.2 %collective-permute-start.8 = (f32[16,512]{1,0:T(8,128)S(1)}, f32[16,512]{1,0:T(8,128)S(1)}, u32[]{:S(2)}, u32[]{:S(2)}) collective-permute-start(f32[16,512]{1,0:T(8,128)S(1)} %get-tuple-element.63), channel_id=1, source_target_pairs={{0,16},{16,32},{32,48},{48,64},{64,80},{80,96},{96,112},{112,128},... | collective-permute-start | bytes 98312 | tf_op jit(solution)/shard_map/ppermute | solution.py:339
  48.0 8.3 %collective-permute-start.9 = (f32[16,512]{1,0:T(8,128)S(1)}, f32[16,512]{1,0:T(8,128)S(1)}, u32[]{:S(2)}, u32[]{:S(2)}) collective-permute-start(f32[16,512]{1,0:T(8,128)S(1)} %get-tuple-element.64), channel_id=1, source_target_pairs={{16,0},{32,16},{48,32},{64,48},{80,64},{96,80},{112,96},{128,112},... | collective-permute-start | bytes 98312 | tf_op jit(solution)/shard_map/ppermute | solution.py:340
  56.4 5.1 %collective-permute-start.11 = (f32[16,512]{1,0:T(8,128)S(1)}, f32[16,512]{1,0:T(8,128)S(1)}, u32[]{:S(2)}, u32[]{:S(2)}) collective-permute-start(f32[16,512]{1,0:T(8,128)S(1)} %get-tuple-element.119), channel_id=1, source_target_pairs={{1,0},{2,1},{3,2},{4,3},{5,4},{6,5},{7,6},{8,7},{9,8},{10,9},{11,1... | collective-permute-start | bytes 98312 | tf_op jit(solution)/shard_map/ppermute | solution.py:348
  60.6 1.2 collective-permute-start.10
  63.5 9.2 %collective-permute-start.12 = (f32[16,512]{1,0:T(8,128)S(1)}, f32[16,512]{1,0:T(8,128)S(1)}, u32[]{:S(2)}, u32[]{:S(2)}) collective-permute-start(f32[16,512]{1,0:T(8,128)S(1)} %get-tuple-element.69), channel_id=1, source_target_pairs={{0,16},{16,32},{32,48},{48,64},{64,80},{80,96},{96,112},{112,128},... | collective-permute-start | bytes 98312 | tf_op jit(solution)/shard_map/ppermute | solution.py:339
  65.4 8.3 %collective-permute-start.13 = (f32[16,512]{1,0:T(8,128)S(1)}, f32[16,512]{1,0:T(8,128)S(1)}, u32[]{:S(2)}, u32[]{:S(2)}) collective-permute-start(f32[16,512]{1,0:T(8,128)S(1)} %get-tuple-element.70), channel_id=1, source_target_pairs={{16,0},{32,16},{48,32},{64,48},{80,64},{96,80},{112,96},{128,112},... | collective-permute-start | bytes 98312 | tf_op jit(solution)/shard_map/ppermute | solution.py:340
  73.8 5.1 %collective-permute-start.15 = (f32[16,512]{1,0:T(8,128)S(1)}, f32[16,512]{1,0:T(8,128)S(1)}, u32[]{:S(2)}, u32[]{:S(2)}) collective-permute-start(f32[16,512]{1,0:T(8,128)S(1)} %get-tuple-element.117), channel_id=1, source_target_pairs={{1,0},{2,1},{3,2},{4,3},{5,4},{6,5},{7,6},{8,7},{9,8},{10,9},{11,1... | collective-permute-start | bytes 98312 | tf_op jit(solution)/shard_map/ppermute | solution.py:348
  78.0 1.2 collective-permute-start.14
  80.9 9.2 %collective-permute-start.16 = (f32[16,512]{1,0:T(8,128)S(1)}, f32[16,512]{1,0:T(8,128)S(1)}, u32[]{:S(2)}, u32[]{:S(2)}) collective-permute-start(f32[16,512]{1,0:T(8,128)S(1)} %get-tuple-element.75), channel_id=1, source_target_pairs={{0,16},{16,32},{32,48},{48,64},{64,80},{80,96},{96,112},{112,128},... | collective-permute-start | bytes 98312 | tf_op jit(solution)/shard_map/ppermute | solution.py:339
  82.8 8.3 %collective-permute-start.17 = (f32[16,512]{1,0:T(8,128)S(1)}, f32[16,512]{1,0:T(8,128)S(1)}, u32[]{:S(2)}, u32[]{:S(2)}) collective-permute-start(f32[16,512]{1,0:T(8,128)S(1)} %get-tuple-element.76), channel_id=1, source_target_pairs={{16,0},{32,16},{48,32},{64,48},{80,64},{96,80},{112,96},{128,112},... | collective-permute-start | bytes 98312 | tf_op jit(solution)/shard_map/ppermute | solution.py:340
  91.1 5.1 %collective-permute-start.19 = (f32[16,512]{1,0:T(8,128)S(1)}, f32[16,512]{1,0:T(8,128)S(1)}, u32[]{:S(2)}, u32[]{:S(2)}) collective-permute-start(f32[16,512]{1,0:T(8,128)S(1)} %get-tuple-element.115), channel_id=1, source_target_pairs={{1,0},{2,1},{3,2},{4,3},{5,4},{6,5},{7,6},{8,7},{9,8},{10,9},{11,1... | collective-permute-start | bytes 98312 | tf_op jit(solution)/shard_map/ppermute | solution.py:348
  100.5 18.0 %collective-permute-start.20 = (f32[16,512]{1,0:T(8,128)S(1)}, f32[16,512]{1,0:T(8,128)S(1)}, u32[]{:S(2)}, u32[]{:S(2)}) collective-permute-start(f32[16,512]{1,0:T(8,128)S(1)} %get-tuple-element.84), channel_id=1, source_target_pairs={{0,16},{16,32},{32,48},{48,64},{64,80},{80,96},{96,112},{112,128},... | collective-permute-start | bytes 98312 | tf_op jit(solution)/shard_map/ppermute | solution.py:339
  102.4 19.6 %all-to-all-start = ((f32[16,1,128]{2,1,0:T(1,128)}), f32[16,1,128]{2,1,0:T(1,128)S(1)}, u32[]{:S(2)}, u32[]{:S(2)}) async-start(f32[16,1,128]{2,1,0:T(1,128)} %bitcast.3), calls=%async_computation | async-start | bytes 16384 | tf_op jit(solution)/shard_map/all_to_all | solution.py:379
  111.1 8.3 %collective-permute-start.21 = (f32[16,512]{1,0:T(8,128)S(1)}, f32[16,512]{1,0:T(8,128)S(1)}, u32[]{:S(2)}, u32[]{:S(2)}) collective-permute-start(f32[16,512]{1,0:T(8,128)S(1)} %get-tuple-element.85), channel_id=1, source_target_pairs={{16,0},{32,16},{48,32},{64,48},{80,64},{96,80},{112,96},{128,112},... | collective-permute-start | bytes 98312 | tf_op jit(solution)/shard_map/ppermute | solution.py:340
  119.5 18.0 %collective-permute-start.23 = (f32[16,512]{1,0:T(8,128)S(1)}, f32[16,512]{1,0:T(8,128)S(1)}, u32[]{:S(2)}, u32[]{:S(2)}) collective-permute-start(f32[16,512]{1,0:T(8,128)S(1)} %get-tuple-element.113), channel_id=1, source_target_pairs={{1,0},{2,1},{3,2},{4,3},{5,4},{6,5},{7,6},{8,7},{9,8},{10,9},{11,1... | collective-permute-start | bytes 98312 | tf_op jit(solution)/shard_map/ppermute | solution.py:348
  120.5 17.1 %collective-permute-start.22 = (f32[16,512]{1,0:T(8,128)S(1)}, f32[16,512]{1,0:T(8,128)S(1)}, u32[]{:S(2)}, u32[]{:S(2)}) collective-permute-start(f32[16,512]{1,0:T(8,128)S(1)} %get-tuple-element.114), channel_id=1, source_target_pairs={{0,1},{1,2},{2,3},{3,4},{4,5},{5,6},{6,7},{7,8},{8,9},{9,10},{10,1... | collective-permute-start | bytes 98312 | tf_op jit(solution)/shard_map/ppermute | solution.py:347
  (14 other events, 139.9 us)

commit v4 on v2

--- a/solution.py
+++ b/solution.py
@@ -85,11 +85,17 @@
     grad_z = right_pair(d_z.T)
     back_z = right_pair(d_z)
     sq_z = right_pair(q_z)
+    lines = np.zeros((8, 64))
+    for face in range(4):
+        lines[2 * face, 16 * face:16 * face + 8] = table[:, 0]
+        lines[2 * face + 1, 16 * face + 8:16 * face + 16] = table[:, 7]
+    grad_f = left_pair(np.kron(np.eye(8), table))
+    back_f = left_pair(lines)
     w_xy = (weights[:, None] * weights[None, :]).astype(np.float32)
     w_xy = np.tile(w_xy, (2, 2)).reshape(ROWS, 1)
     w_rows = np.ascontiguousarray(np.broadcast_to(w_xy, (ROWS, 128)))
     w_z = np.tile(weights, COLS // 8).reshape(1, COLS).astype(np.float32)
-    return dict(grad=grad, back=back, sq=sq, grad_z=grad_z, back_z=back_z, sq_z=sq_z, w_rows=w_rows, w_z=w_z)
+    return dict(grad=grad, back=back, sq=sq, grad_z=grad_z, back_z=back_z, grad_f=grad_f, back_f=back_f, sq_z=sq_z, w_rows=w_rows, w_z=w_z)
 
 
 def dot(a, b):
@@ -135,20 +141,74 @@
     return f + jnp.where(upper, nxt, jnp.where(lower, prv, 0.0))
 
 
-def emit_partial(f, edge_ref, p_ref, faces):
+def corner_lines(v_ref, cf, cz, rz, fv_ref, grad_f, back_f, grad_z, back_z):
+    for x in range(16):
+        r = 16 * x
+        fv_ref[x:x + 1, :] = v_ref[r + 15:r + 16, :]
+        fv_ref[16 + x:17 + x, :] = v_ref[r:r + 1, :]
+    fv_ref[32:48, :] = v_ref[240:256, :]
+    fv_ref[48:64, :] = v_ref[0:16, :]
+    pair = jnp.concatenate(halves(fv_ref[...]), 0)
+    flux = (dot(grad_f[0], pair) + dot(grad_f[1], pair)) * cf
+    pair = jnp.concatenate(halves(flux), 0)
+    ends = dot(back_f[0], pair) + dot(back_f[1], pair)
+    for row, r in enumerate((255, 15, 240, 0, 255, 15, 240, 0)):
+        fv_ref[row:row + 1, :] = v_ref[r:r + 1, :]
+    at = fv_ref[0:8, :]
+    flux_z = mul_z(*halves(at), grad_z) * cz
+    return join_z(jnp.concatenate([ends, mul_z(*halves(flux_z), back_z) + rz * at], 0))
+
+
+def join_rows(f, p_ref):
     p_ref[...] = join_z(f)
     p_ref[112:128, :] = p_ref[112:128, :] + p_ref[128:144, :]
     p_ref[128:144, :] = p_ref[112:128, :]
-    x_low, x_high, y_low, y_high = faces
     for x in range(16):
         r = 16 * x
         mid = p_ref[r + 7:r + 8, :] + p_ref[r + 8:r + 9, :]
         p_ref[r + 7:r + 8, :] = mid
         p_ref[r + 8:r + 9, :] = mid
-        y_low[x:x + 1, :] = p_ref[r:r + 1, :]
-        y_high[x:x + 1, :] = p_ref[r + 15:r + 16, :]
-    x_low[...] = jnp.where(edge_ref[0] == 1, 0.0, p_ref[0:16, :])
-    x_high[...] = jnp.where(edge_ref[1] == 1, 0.0, p_ref[240:256, :])
+
+
+def put_y(p_ref, low, high, base):
+    for x in range(16):
+        r = 16 * x
+        low[base + x:base + x + 1, :] = p_ref[r:r + 1, :]
+        high[base + x:base + x + 1, :] = p_ref[r + 15:r + 16, :]
+
+
+def add_row(ref, row, line):
+    ref[row:row + 1, :] = ref[row:row + 1, :] + line
+
+
+def emit_partial(f, lines, ctl_ref, p_ref, faces, st_ref):
+    even, odd, low_y, high_y = faces
+    join_rows(f, p_ref)
+    st_ref[0:16, :] = p_ref[0:16, :]
+    st_ref[16:32, :] = p_ref[240:256, :]
+    put_y(p_ref, low_y, high_y, 0)
+    ln = [lines[i:i + 1] for i in range(12)]
+    add_row(st_ref, 15, ln[0])
+    add_row(st_ref, 31, ln[1])
+    add_row(st_ref, 0, ln[2])
+    add_row(st_ref, 16, ln[3])
+    add_row(low_y, 15, ln[4])
+    add_row(high_y, 15, ln[5])
+    add_row(low_y, 0, ln[6])
+    add_row(high_y, 0, ln[7])
+    for i, r in enumerate((255, 15, 240, 0)):
+        add_row(p_ref, r, ln[8 + i])
+    is_odd = ctl_ref[0:1, :] > 0.5
+    low, high = st_ref[0:16, :], st_ref[16:32, :]
+    even[...] = jnp.where(is_odd, low, high)
+    odd[...] = jnp.where(is_odd, high, low)
+    low_y[...] = ctl_ref[1:2, :] * low_y[...]
+    high_y[...] = ctl_ref[2:3, :] * high_y[...]
+
+
+def pick(ctl_ref, even, odd):
+    is_odd = ctl_ref[0:1, :] > 0.5
+    return jnp.where(is_odd, even, odd), jnp.where(is_odd, odd, even)
 
 
 def take_sum(p_ref, recv, s_ref):
@@ -168,9 +228,9 @@
     return part[:, 0:128] + part[:, 128:256] + part[:, 256:384] + part[:, 384:512]
 
 
-def first_kernel(edge_ref, table_hbm, load_hbm, cond_hbm, flags_hbm, region_hbm, sq_hbm, sqz_hbm, wr_hbm, wz_hbm,
-                 coef_ref, react_ref, keep_ref, pl_ref, pd_ref, xl_ref, xh_ref, yl_ref, yh_ref,
-                 table_ref, load_ref, cond_ref, flags_ref, region_ref, sq_ref, sqz_ref, wr_ref, wz_ref, sems):
+def first_kernel(ctl_ref, table_hbm, load_hbm, cond_hbm, flags_hbm, region_hbm, sq_hbm, sqz_hbm, wr_hbm, wz_hbm,
+                 coef_ref, react_ref, keep_ref, pl_ref, pd_ref, even_ref, odd_ref, yl_ref, yh_ref,
+                 table_ref, load_ref, cond_ref, flags_ref, region_ref, sq_ref, sqz_ref, wr_ref, wz_ref, sems, st_ref):
     flags_tile = flags_hbm.at[:, :, pl.ds(0, 128)]
     pairs = ((cond_hbm, cond_ref), (wr_hbm, wr_ref), (wz_hbm, wz_ref), (region_hbm, region_ref), (table_hbm, table_ref),
              (sq_hbm, sq_ref), (sqz_hbm, sqz_ref), (load_hbm, load_ref), (flags_tile, flags_ref))
@@ -208,36 +268,80 @@
         pair = jnp.concatenate([high[part], low[part]], 0)
         rows.append(dot(sq_ref[0], pair) + dot(sq_ref[1], pair))
     diag = jnp.concatenate(rows, 0) + mul_z(high, low, sqz_ref[...]) + react_ref[...]
-    faces = (xl_ref, xh_ref, yl_ref, yh_ref)
-    emit_partial(diag, edge_ref, pd_ref, [face.at[1] for face in faces])
-    emit_partial(load_ref[...].reshape(ROWS, COLS), edge_ref, pl_ref, [face.at[0] for face in faces])
-
-
-def second_kernel(edge_ref, pl_ref, pd_ref, xl_ref, xr_ref, yb_ref, ya_ref, keep_ref, coef_ref, react_ref,
-                  grad_ref, back_ref, gz_ref, bz_ref,
-                  r_ref, dinv_ref, p_ref, lo_x, hi_x, lo_y, hi_y, s_ref):
-    diag = take_sum(pd_ref, (xl_ref[1], xr_ref[1], yb_ref[1], ya_ref[1]), s_ref)
+    join_rows(load_ref[...].reshape(ROWS, COLS), pl_ref)
+    join_rows(diag, pd_ref)
+    for i, src in enumerate((pl_ref, pd_ref, coef_ref)):
+        st_ref[0, 16 * i:16 * i + 16, :] = src[0:16, :]
+        st_ref[1, 16 * i:16 * i + 16, :] = src[240:256, :]
+        put_y(src, yl_ref, yh_ref, 16 * i)
+    zeros = jnp.zeros((8, COLS), F32)
+    for side, r in enumerate((0, 240)):
+        st_ref[side, 48:56, :] = zeros
+        st_ref[side, 48:49, :] = react_ref[r:r + 1, :]
+        st_ref[side, 49:50, :] = react_ref[r + 15:r + 16, :]
+    yl_ref[48:56, :] = zeros
+    yh_ref[48:56, :] = zeros
+    is_odd = ctl_ref[0:1, :] > 0.5
+    even_ref[...] = jnp.where(is_odd, st_ref[0], st_ref[1])
+    odd_ref[...] = jnp.where(is_odd, st_ref[1], st_ref[0])
+
+
+def corner_kernel(ctl_ref, even_ref, odd_ref, lin_ref, hin_ref, low_ref, high_ref, x_ref):
+    x_ref[0], x_ref[1] = pick(ctl_ref, even_ref[...], odd_ref[...])
+    for src, out, row in ((lin_ref, low_ref, 0), (hin_ref, high_ref, 15)):
+        out[...] = src[...]
+        for base in (0, 16):
+            add_row(out, base, x_ref[0, base + row:base + row + 1, :])
+            add_row(out, base + 15, x_ref[1, base + row:base + row + 1, :])
+        line = 48 if row == 0 else 49
+        out[48:49, :] = x_ref[0, 32 + row:33 + row, :]
+        out[49:50, :] = x_ref[1, 32 + row:33 + row, :]
+        out[50:51, :] = x_ref[0, line:line + 1, :]
+        out[51:52, :] = x_ref[1, line:line + 1, :]
+    low_ref[...] = ctl_ref[1:2, :] * low_ref[...]
+    high_ref[...] = ctl_ref[2:3, :] * high_ref[...]
+
+
+def second_kernel(ctl_ref, pl_ref, pd_ref, xe_ref, xo_ref, yb_ref, ya_ref, keep_ref, coef_ref, react_ref,
+                  grad_ref, back_ref, gz_ref, bz_ref, gf_ref, bf_ref,
+                  r_ref, dinv_ref, cf_ref, cz_ref, rz_ref, p_ref, even, odd, low_y, high_y, s_ref, fv_ref, st_ref):
+    left, right = pick(ctl_ref, xe_ref[...], xo_ref[...])
+    below, above = yb_ref[...], ya_ref[...]
+    diag = take_sum(pd_ref, (left[16:32], right[16:32], below[16:32], above[16:32]), s_ref)
     dinv_ref[...] = 1.0 / diag
     keep = keep_ref[...]
     dinv_ref[:, 0:128] = keep * dinv_ref[:, 0:128]
-    r = take_sum(pl_ref, (xl_ref[0], xr_ref[0], yb_ref[0], ya_ref[0]), s_ref)
+    r = take_sum(pl_ref, (left[0:16], right[0:16], below[0:16], above[0:16]), s_ref)
     r_ref[...] = r
     r_ref[:, 0:128] = keep * r_ref[:, 0:128]
+    cf_ref[0:16, :] = above[32:48]
+    cf_ref[16:32, :] = below[32:48]
+    cf_ref[32:48, :] = right[32:48]
+    cf_ref[48:64, :] = left[32:48]
+    for out, base in ((cz_ref, 48), (rz_ref, 50)):
+        out[0:1, :] = above[base + 1:base + 2]
+        out[1:2, :] = above[base:base + 1]
+        out[2:3, :] = below[base + 1:base + 2]
+        out[3:4, :] = below[base:base + 1]
+        out[4:8, :] = jnp.zeros((4, COLS), F32)
     a0 = dinv_ref[...] * r_ref[...] * (1.0 / CENTER)
+    s_ref[...] = a0
+    lines = corner_lines(s_ref, cf_ref[...], cz_ref[...], rz_ref[...], fv_ref, gf_ref, bf_ref, gz_ref[...], bz_ref[...])
     f = local_op(a0, coef_ref[...], react_ref[...], grad_ref, back_ref, gz_ref[...], bz_ref[...])
-    emit_partial(f, edge_ref, p_ref, (lo_x, hi_x, lo_y, hi_y))
-
-
-def sweep1_kernel(edge_ref, pin_ref, xl_ref, xr_ref, yb_ref, ya_ref, r_ref, dinv_ref, coef_ref, react_ref,
-                  grad_ref, back_ref, gz_ref, bz_ref,
-                  a1_ref, p_ref, lo_x, hi_x, lo_y, hi_y, s_ref):
-    image = take_sum(pin_ref, (xl_ref[...], xr_ref[...], yb_ref[...], ya_ref[...]), s_ref)
+    emit_partial(f, lines, ctl_ref, p_ref, (even, odd, low_y, high_y), st_ref)
+
+
+def sweep1_kernel(ctl_ref, pin_ref, xe_ref, xo_ref, yb_ref, ya_ref, r_ref, dinv_ref, coef_ref, react_ref,
+                  cf_ref, cz_ref, rz_ref, grad_ref, back_ref, gz_ref, bz_ref, gf_ref, bf_ref,
+                  a1_ref, p_ref, even, odd, low_y, high_y, s_ref, fv_ref, st_ref):
+    image = take_sum(pin_ref, (*pick(ctl_ref, xe_ref[...], xo_ref[...]), yb_ref[...], ya_ref[...]), s_ref)
     dinv, r = dinv_ref[...], r_ref[...]
     a0 = dinv * r * (1.0 / CENTER)
     a1 = (1.0 + MIX1) * a0 + GAIN1 * (dinv * (r - image))
     a1_ref[...] = a1
+    lines = corner_lines(a1_ref, cf_ref[...], cz_ref[...], rz_ref[...], fv_ref, gf_ref, bf_ref, gz_ref[...], bz_ref[...])
     f = local_op(a1, coef_ref[...], react_ref[...], grad_ref, back_ref, gz_ref[...], bz_ref[...])
-    emit_partial(f, edge_ref, p_ref, (lo_x, hi_x, lo_y, hi_y))
+    emit_partial(f, lines, ctl_ref, p_ref, (even, odd, low_y, high_y), st_ref)
 
 
 def sweep2(image, a1, r, dinv):
@@ -245,41 +349,45 @@
     return a1 + (MIX2 * (a1 - a0) + GAIN2 * (dinv * (r - image)))
 
 
-def third_kernel(edge_ref, pin_ref, xl_ref, xr_ref, yb_ref, ya_ref, r_ref, dinv_ref, a1_ref, load_ref, coef_ref, react_ref,
-                 grad_ref, back_ref, gz_ref, bz_ref,
-                 z_ref, p_ref, lo_x, hi_x, lo_y, hi_y, dots_ref, s_ref):
-    image = take_sum(pin_ref, (xl_ref[...], xr_ref[...], yb_ref[...], ya_ref[...]), s_ref)
+def third_kernel(ctl_ref, pin_ref, xe_ref, xo_ref, yb_ref, ya_ref, r_ref, dinv_ref, a1_ref, load_ref, coef_ref, react_ref,
+                 cf_ref, cz_ref, rz_ref, grad_ref, back_ref, gz_ref, bz_ref, gf_ref, bf_ref,
+                 z_ref, p_ref, even, odd, low_y, high_y, dots_ref, s_ref, fv_ref, st_ref):
+    image = take_sum(pin_ref, (*pick(ctl_ref, xe_ref[...], xo_ref[...]), yb_ref[...], ya_ref[...]), s_ref)
     z = sweep2(image, a1_ref[...], r_ref[...], dinv_ref[...])
     z_ref[...] = z
     dots_ref[0] = fold(load_ref[...].reshape(ROWS, COLS) * z)
+    lines = corner_lines(z_ref, cf_ref[...], cz_ref[...], rz_ref[...], fv_ref, gf_ref, bf_ref, gz_ref[...], bz_ref[...])
     f = local_op(z, coef_ref[...], react_ref[...], grad_ref, back_ref, gz_ref[...], bz_ref[...])
     dots_ref[1] = fold(f * z)
-    emit_partial(f, edge_ref, p_ref, (lo_x, hi_x, lo_y, hi_y))
-
-
-def fourth_kernel(edge_ref, pin_ref, xl_ref, xr_ref, yb_ref, ya_ref, dinv_ref, z_ref, coef_ref, react_ref,
-                  grad_ref, back_ref, gz_ref, bz_ref,
-                  im_ref, p_ref, lo_x, hi_x, lo_y, hi_y, dots_ref, s_ref):
-    image = take_sum(pin_ref, (xl_ref[...], xr_ref[...], yb_ref[...], ya_ref[...]), s_ref)
+    emit_partial(f, lines, ctl_ref, p_ref, (even, odd, low_y, high_y), st_ref)
+
+
+def fourth_kernel(ctl_ref, pin_ref, xe_ref, xo_ref, yb_ref, ya_ref, dinv_ref, z_ref, coef_ref, react_ref,
+                  cf_ref, cz_ref, rz_ref, grad_ref, back_ref, gz_ref, bz_ref, gf_ref, bf_ref,
+                  im_ref, p_ref, even, odd, low_y, high_y, dots_ref, s_ref, fv_ref, st_ref):
+    image = take_sum(pin_ref, (*pick(ctl_ref, xe_ref[...], xo_ref[...]), yb_ref[...], ya_ref[...]), s_ref)
     dinv = dinv_ref[...]
     im = jnp.where(dinv != 0.0, image, 0.0)
     im_ref[...] = im
     b0 = dinv * im * (1.0 / CENTER)
+    s_ref[...] = b0
+    lines = corner_lines(s_ref, cf_ref[...], cz_ref[...], rz_ref[...], fv_ref, gf_ref, bf_ref, gz_ref[...], bz_ref[...])
     f = local_op(b0, coef_ref[...], react_ref[...], grad_ref, back_ref, gz_ref[...], bz_ref[...])
     dots_ref[...] = fold(f * z_ref[...])
-    emit_partial(f, edge_ref, p_ref, (lo_x, hi_x, lo_y, hi_y))
-
-
-def fifth_kernel(edge_ref, pin_ref, xl_ref, xr_ref, yb_ref, ya_ref, im_ref, dinv_ref, z_ref, d34_ref, d5_ref, coef_ref, react_ref,
-                 grad_ref, back_ref, gz_ref, bz_ref,
-                 b1_ref, p_ref, lo_x, hi_x, lo_y, hi_y, dots_ref, s_ref):
-    image = take_sum(pin_ref, (xl_ref[...], xr_ref[...], yb_ref[...], ya_ref[...]), s_ref)
+    emit_partial(f, lines, ctl_ref, p_ref, (even, odd, low_y, high_y), st_ref)
+
+
+def fifth_kernel(ctl_ref, pin_ref, xe_ref, xo_ref, yb_ref, ya_ref, im_ref, dinv_ref, z_ref, d34_ref, d5_ref, coef_ref, react_ref,
+                 cf_ref, cz_ref, rz_ref, grad_ref, back_ref, gz_ref, bz_ref, gf_ref, bf_ref,
+                 b1_ref, p_ref, even, odd, low_y, high_y, dots_ref, s_ref, fv_ref, st_ref):
+    image = take_sum(pin_ref, (*pick(ctl_ref, xe_ref[...], xo_ref[...]), yb_ref[...], ya_ref[...]), s_ref)
     dinv, im = dinv_ref[...], im_ref[...]
     b0 = dinv * im * (1.0 / CENTER)
     b1 = (1.0 + MIX1) * b0 + GAIN1 * (dinv * (im - image))
     b1_ref[...] = b1
+    lines = corner_lines(b1_ref, cf_ref[...], cz_ref[...], rz_ref[...], fv_ref, gf_ref, bf_ref, gz_ref[...], bz_ref[...])
     f = local_op(b1, coef_ref[...], react_ref[...], grad_ref, back_ref, gz_ref[...], bz_ref[...])
-    emit_partial(f, edge_ref, p_ref, (lo_x, hi_x, lo_y, hi_y))
+    emit_partial(f, lines, ctl_ref, p_ref, (even, odd, low_y, high_y), st_ref)
     last = fold(f * ((1.0 + MIX2) * z_ref[...] - (CENTER * GAIN2) * b0))
     both = last + (CENTER * GAIN2 - MIX2) * d5_ref[...]
     lane = lax.broadcasted_iota(jnp.int32, (1, 128), 1)
@@ -288,12 +396,12 @@
     dots_ref[...] = jnp.broadcast_to(sums, dots_ref.shape)
 
 
-def last_kernel(dots_ref, pin_ref, xl_ref, xr_ref, yb_ref, ya_ref, im_ref, dinv_ref, b1_ref, z_ref, r_ref,
+def last_kernel(dots_ref, ctl_ref, pin_ref, xe_ref, xo_ref, yb_ref, ya_ref, im_ref, dinv_ref, b1_ref, z_ref, r_ref,
                 sol_ref, res_ref, dir_ref, s_ref):
     first, curv, quad = dots_ref[0], dots_ref[1], dots_ref[2]
     step = first / curv
     ratio = (first - 2.0 * step * curv + step * step * quad) / first
-    image = take_sum(pin_ref, (xl_ref[...], xr_ref[...], yb_ref[...], ya_ref[...]), s_ref)
+    image = take_sum(pin_ref, (*pick(ctl_ref, xe_ref[...], xo_ref[...]), yb_ref[...], ya_ref[...]), s_ref)
     im = im_ref[...]
     b2 = sweep2(image, b1_ref[...], im, dinv_ref[...])
     z = z_ref[...]
@@ -309,6 +417,7 @@
 BIG = jax.ShapeDtypeStruct((ROWS, COLS), F32)
 FACE = jax.ShapeDtypeStruct((16, COLS), F32)
 PART = (BIG, FACE, FACE, FACE, FACE)
+MESSAGE = jax.ShapeDtypeStruct((56, COLS), F32)
 PARAMS = pltpu.CompilerParams(vmem_limit_bytes=24 << 20)
 
 
@@ -319,67 +428,73 @@
 
 
 def step_call(kernel, outs, n_in):
-    return call(kernel, outs, [SM] + [VM] * n_in, [pltpu.VMEM((ROWS, COLS), F32)])
+    scratch = [pltpu.VMEM((rows, COLS), F32) for rows in (ROWS, 64, 32)]
+    return call(kernel, outs, [VM] * (n_in + 1), scratch)
+
+
+def swaps(first, count):
+    pairs = [(i, i + 1) for i in range(first, count - 1, 2)]
+    return pairs + [(j, i) for i, j in pairs]
 
 
 def per_device(load, conductivity, flags, region, kappa_table):
     k = {name: jnp.asarray(value) for name, value in constants().items()}
-    mats = (k["grad"], k["back"], k["grad_z"], k["back_z"])
+    mats = (k["grad"], k["back"], k["grad_z"], k["back_z"], k["grad_f"], k["back_f"])
     n_x, n_y = lax.axis_size("gx"), lax.axis_size("gy")
     at_x, at_y = lax.axis_index("gx"), lax.axis_index("gy")
-    edge = jnp.stack([at_x == 0, at_x == n_x - 1, at_y == 0, at_y == n_y - 1]).astype(jnp.int32)
-    up_x = [(i, (i + 1) % n_x) for i in range(n_x)]
+    ctl = jnp.stack([at_x % 2 == 1, at_y != 0, at_y != n_y - 1, at_y < 0]).astype(F32)
+    ctl = jnp.broadcast_to(ctl[:, None], (4, COLS))
     up_y = [(i, (i + 1) % n_y) for i in range(n_y)]
-    down_x = [(j, i) for i, j in up_x]
     down_y = [(j, i) for i, j in up_y]
 
+    def along_x(even, odd):
+        return lax.ppermute(even, "gx", swaps(0, n_x)), lax.ppermute(odd, "gx", swaps(1, n_x))
+
+    def along_y(low, high):
+        return lax.ppermute(high, "gy", up_y), lax.ppermute(low, "gy", down_y)
+
     def exchange(faces):
-        x_low, x_high, y_low, y_high = faces
-        left = lax.ppermute(x_high, "gx", up_x)
-        right = lax.ppermute(x_low, "gx", down_x)
-
-        def with_corners(face, row, last):
-            inner = jnp.zeros(face.shape[:-2] + (14, COLS), F32)
-            ends = [left[..., row:row + 1, :], inner, right[..., row:row + 1, :]]
-            return jnp.where(last, 0.0, face + jnp.concatenate(ends, axis=-2))
-
-        below = lax.ppermute(with_corners(y_high, 15, at_y == n_y - 1), "gy", up_y)
-        above = lax.ppermute(with_corners(y_low, 0, at_y == 0), "gy", down_y)
-        return left, right, below, above
-
-    two = jax.ShapeDtypeStruct((2, 16, COLS), F32)
+        even, odd, low_y, high_y = faces
+        return (*along_x(even, odd), *along_y(low_y, high_y))
+
     keep_shape = jax.ShapeDtypeStruct((ROWS, 128), F32)
     inputs = (kappa_table, load, conductivity, flags, region, k["sq"], k["sq_z"], k["w_rows"], k["w_z"])
+    inputs = tuple(pltpu.with_memory_space_constraint(v, pltpu.HBM) for v in inputs)
     buffers = [pltpu.VMEM(v.shape, v.dtype) for v in inputs]
     buffers[0] = pltpu.SMEM(kappa_table.shape, F32)
     buffers[3] = pltpu.VMEM((16, 16, 128), jnp.int32)
-    coef, react, keep, part_l, part_d, *faces = call(
-        first_kernel, (BIG, BIG, keep_shape, BIG, BIG, two, two, two, two), [SM] + [HB] * len(inputs),
-        buffers + [pltpu.SemaphoreType.DMA((len(inputs),))])(edge, *inputs)
+    buffers += [pltpu.SemaphoreType.DMA((len(inputs),)), pltpu.VMEM((2, 56, COLS), F32)]
+    coef, react, keep, part_l, part_d, even, odd, low_y, high_y = call(
+        first_kernel, (BIG, BIG, keep_shape, BIG, BIG) + (MESSAGE,) * 4, [VM] + [HB] * len(inputs), buffers)(ctl, *inputs)
+    even, odd = along_x(even, odd)
+    low_y, high_y = call(corner_kernel, (MESSAGE, MESSAGE), [VM] * 5, [pltpu.VMEM((2, 56, COLS), F32)])(
+        ctl, even, odd, low_y, high_y)
+    recv = (even, odd, *along_y(low_y, high_y))
+    line = jax.ShapeDtypeStruct((8, COLS), F32)
+    r, dinv, cf, cz, rz, part, *faces = step_call(
+        second_kernel, (BIG, BIG, jax.ShapeDtypeStruct((64, COLS), F32), line, line) + PART, 15)(
+        ctl, part_l, part_d, *recv, keep, coef, react, *mats)
+    tail = (coef, react, cf, cz, rz, *mats)
     recv = exchange(faces)
-    r, dinv, part, *faces = step_call(second_kernel, (BIG, BIG) + PART, 13)(
-        edge, part_l, part_d, *recv, keep, coef, react, *mats)
-    recv = exchange(faces)
-    a1, part, *faces = step_call(sweep1_kernel, (BIG,) + PART, 13)(
-        edge, part, *recv, r, dinv, coef, react, *mats)
+    a1, part, *faces = step_call(sweep1_kernel, (BIG,) + PART, 18)(ctl, part, *recv, r, dinv, *tail)
     recv = exchange(faces)
     d34_shape = jax.ShapeDtypeStruct((2, 8, 128), F32)
-    z, part, *faces, d34 = step_call(third_kernel, (BIG,) + PART + (d34_shape,), 15)(
-        edge, part, *recv, r, dinv, a1, load, coef, react, *mats)
+    z, part, *faces, d34 = step_call(third_kernel, (BIG,) + PART + (d34_shape,), 20)(
+        ctl, part, *recv, r, dinv, a1, load, *tail)
     recv = exchange(faces)
     d5_shape = jax.ShapeDtypeStruct((8, 128), F32)
-    im, part, *faces, d5 = step_call(fourth_kernel, (BIG,) + PART + (d5_shape,), 13)(
-        edge, part, *recv, dinv, z, coef, react, *mats)
+    im, part, *faces, d5 = step_call(fourth_kernel, (BIG,) + PART + (d5_shape,), 18)(
+        ctl, part, *recv, dinv, z, *tail)
     recv = exchange(faces)
     dots_shape = jax.ShapeDtypeStruct((n_y, 128), F32)
-    b1, part, *faces, dots = step_call(fifth_kernel, (BIG,) + PART + (dots_shape,), 16)(
-        edge, part, *recv, im, dinv, z, d34, d5, coef, react, *mats)
+    b1, part, *faces, dots = step_call(fifth_kernel, (BIG,) + PART + (dots_shape,), 21)(
+        ctl, part, *recv, im, dinv, z, d34, d5, *tail)
     total = lax.all_to_all(dots, "gy", 0, 0, tiled=True).sum(0)
     recv = exchange(faces)
     total = lax.all_to_all(jnp.broadcast_to(total, (n_x, 128)), "gx", 0, 0, tiled=True).sum(0)
     shape = jax.ShapeDtypeStruct((16, 16, COLS), F32)
-    return step_call(last_kernel, (shape, shape, shape), 10)(
-        total, part, *recv, im, dinv, b1, z, r)
+    return call(last_kernel, (shape, shape, shape), [SM] + [VM] * 11, [pltpu.VMEM((ROWS, COLS), F32)])(
+        total, ctl, part, *recv, im, dinv, b1, z, r)
 
 
 def solution(mesh):

time: 146 us -> 118 us (0.81)
  starting transfers between devices: 92.7 us -> 70.6 us
  local copies, waits for them, and re-layouts: 6.54 us -> 0.77 us
  waiting for transfers between devices: 12.9 us -> 9.37 us
  blocking collectives: 15.5 us -> 17.8 us
    ppermute x24, starting transfers between devices: 84 us -> 60.5 us  [the longest x6 38 us: along_x(): lax.ppermute(even, 'gx', swaps(0, n_x))]
    unnamed x28 -> x14, local copies, waits for them, and re-layouts: 6.38 us -> 0.68 us
    ppermute x24, waiting for transfers between devices: 12.9 us -> 9.37 us  [the longest x12 7.85 us: along_y(): return (lax.ppermute(high, 'gy', up_y), lax.ppermute(low, 'gy', down_y))]
    all_to_all x1, blocking collectives: 15.5 us -> 17.8 us  [per_device(): lax.all_to_all(jnp.broadcast_to(total, (n_x, 128)), 'gx', 0, 0, tiled=True)]
    pallas_call x7 -> x8, Pallas kernels: 16.4 us -> 16.5 us  [the longest x1 2.99 us: per_device(): step_call(fifth_kernel, (BIG,) + PART + (dots_shape,), 21)]
  transfers between devices with their start and end apart: 25 -> 25, of which waited for: 15 -> 11; matrix products, arithmetic and copies ran while one was open for 0% -> 0% of each run, Pallas kernels for 0% -> 0%
where the time goes in v4:
time: 118 us; the launch traced here: 116 us
  starting transfers between devices  70.6 us (60%)
  blocking collectives  17.8 us (15%)
  Pallas kernels  16.5 us (14%)
  waiting for transfers between devices  9.37 us (8%)
    ppermute x6, starting transfers between devices, along_x(): lax.ppermute(even, 'gx', swaps(0, n_x))  38 us
    ppermute x12, starting transfers between devices, along_y(): return (lax.ppermute(high, 'gy', up_y), lax.ppermute(low, 'gy', down_y))  18.5 us
    all_to_all x1, blocking collectives, per_device(): lax.all_to_all(jnp.broadcast_to(total, (n_x, 128)), 'gx', 0, 0, tiled=True)  17.8 us
    all_to_all x1, starting transfers between devices, per_device(): total = lax.all_to_all(dots, 'gy', 0, 0, tiled=True).sum(0)  10.2 us
    ppermute x12, waiting for transfers between devices, along_y(): return (lax.ppermute(high, 'gy', up_y), lax.ppermute(low, 'gy', down_y))  7.85 us
    ppermute x6, starting transfers between devices, along_x(): lax.ppermute(odd, 'gx', swaps(1, n_x))  3.98 us
    pallas_call x1, Pallas kernels, per_device(): step_call(fifth_kernel, (BIG,) + PART + (dots_shape,), 21)  2.99 us
    pallas_call x1, Pallas kernels, per_device(): step_call(third_kernel, (BIG,) + PART + (d34_shape,), 20)  2.4 us
  transfers between devices with their start and end apart: 25, of which 11 were waited for; matrix products, arithmetic and copies ran while one was open for 0% of the time, Pallas kernels for 0%

profile of v4, /device:TPU:1, one launch (start us, length us, event | category | flops | bytes accessed | tf_op | source)
XLA Modules:
  0.0 116.1 jit_solution(16109320154600951239)
XLA Ops:
  0.8 2.3 %shard_map.166 = (f32[256,512]{1,0:T(8,128)S(1)}, f32[256,512]{1,0:T(8,128)S(1)}, f32[256,128]{1,0:T(8,128)S(1)}, f32[256,512]{1,0:T(8,128)S(1)}, f32[256,512]{1...) custom-call(f32[4,512]{1,0:T(4,128)S(1)} %broadcast_in_dim.4.ctl_ref, ...), custom_call_target="tpu_custom_call" | custom-call | tf_op jit(solution)/shard_map/pallas_call | solution.py:467
  3.1 5.0 %collective-permute-start = (f32[56,512]{1,0:T(8,128)S(1)}, f32[56,512]{1,0:T(8,128)S(1)}, u32[]{:S(2)}, u32[]{:S(2)}) collective-permute-start(f32[56,512]{1,0:T(8,128)S(1)} %get-tuple-element.53), channel_id=1, source_target_pairs={{0,16},{32,48},{64,80},{96,112},{128,144},{160,176},{192,208},{224... | collective-permute-start | bytes 344072 | tf_op jit(solution)/shard_map/ppermute | solution.py:451
  8.8 1.5 %collective-permute-done.even_ref.xe_ref = f32[56,512]{1,0:T(8,128)S(1)} collective-permute-done((f32[56,512]{1,0:T(8,128)S(1)}, f32[56,512]{1,0:T(8,128)S(1)}, u32[]{:S(2)}, u32[]{:S(2)}) %collective-permute-start) | collective-permute-done | bytes 114720 | tf_op jit(solution)/shard_map/ppermute | solution.py:451
  10.4 3.1 %collective-permute-start.2 = (f32[56,512]{1,0:T(8,128)S(1)}, f32[56,512]{1,0:T(8,128)S(1)}, u32[]{:S(2)}, u32[]{:S(2)}) collective-permute-start(f32[56,512]{1,0:T(8,128)S(1)} %get-tuple-element.57), channel_id=1, source_target_pairs={{0,1},{1,2},{2,3},{3,4},{4,5},{5,6},{6,7},{7,8},{8,9},{9,10},{10,1... | collective-permute-start | bytes 344072 | tf_op jit(solution)/shard_map/ppermute | solution.py:454
  13.5 3.5 %collective-permute-start.3 = (f32[56,512]{1,0:T(8,128)S(1)}, f32[56,512]{1,0:T(8,128)S(1)}, u32[]{:S(2)}, u32[]{:S(2)}) collective-permute-start(f32[56,512]{1,0:T(8,128)S(1)} %get-tuple-element.58), channel_id=1, source_target_pairs={{1,0},{2,1},{3,2},{4,3},{5,4},{6,5},{7,6},{8,7},{9,8},{10,9},{11,1... | collective-permute-start | bytes 344072 | tf_op jit(solution)/shard_map/ppermute | solution.py:454
  18.6 2.2 %shard_map.168 = (f32[256,512]{1,0:T(8,128)S(1)}, f32[256,512]{1,0:T(8,128)S(1)}, f32[64,512]{1,0:T(8,128)S(1)}, f32[8,512]{1,0:T(8,128)S(1)}, f32[8,512]{1,0:T(...) custom-call(f32[4,512]{1,0:T(4,128)S(1)} %broadcast_in_dim.4.ctl_ref, ...), custom_call_target="tpu_custom_call" | custom-call | tf_op jit(solution)/shard_map/pallas_call | solution.py:474
  20.8 7.8 %collective-permute-start.4 = (f32[16,512]{1,0:T(8,128)S(1)}, f32[16,512]{1,0:T(8,128)S(1)}, u32[]{:S(2)}, u32[]{:S(2)}) collective-permute-start(f32[16,512]{1,0:T(8,128)S(1)} %get-tuple-element.63), channel_id=1, source_target_pairs={{0,16},{32,48},{64,80},{96,112},{128,144},{160,176},{192,208},{224... | collective-permute-start | bytes 98312 | tf_op jit(solution)/shard_map/ppermute | solution.py:451
  29.6 2.2 %collective-permute-start.7 = (f32[16,512]{1,0:T(8,128)S(1)}, f32[16,512]{1,0:T(8,128)S(1)}, u32[]{:S(2)}, u32[]{:S(2)}) collective-permute-start(f32[16,512]{1,0:T(8,128)S(1)} %get-tuple-element.66), channel_id=1, source_target_pairs={{1,0},{2,1},{3,2},{4,3},{5,4},{6,5},{7,6},{8,7},{9,8},{10,9},{11,1... | collective-permute-start | bytes 98312 | tf_op jit(solution)/shard_map/ppermute | solution.py:454
  32.9 2.2 %shard_map.169 = (f32[256,512]{1,0:T(8,128)S(1)}, f32[256,512]{1,0:T(8,128)S(1)}, f32[16,512]{1,0:T(8,128)S(1)}, f32[16,512]{1,0:T(8,128)S(1)}, f32[16,512]{1,0:T(8,128)S(1)}, /*index=5*/f32[16,512]{1,0:T(8,128)S(1)}) custom-call(f32[4,512]{1,0:T(4,128)S(1)} %broadcast_in_dim.4.ctl_ref, f32[256,512]{1,0:T(8,128)S(1)} %get-tuple-element.62.pin_ref, ...), custom_call_target="tpu_custom_call" | custom-call | tf_op jit(solution)/shard_map/pallas_call | solution.py:479
  35.2 8.2 %collective-permute-start.8 = (f32[16,512]{1,0:T(8,128)S(1)}, f32[16,512]{1,0:T(8,128)S(1)}, u32[]{:S(2)}, u32[]{:S(2)}) collective-permute-start(f32[16,512]{1,0:T(8,128)S(1)} %get-tuple-element.73), channel_id=1, source_target_pairs={{0,16},{32,48},{64,80},{96,112},{128,144},{160,176},{192,208},{224... | collective-permute-start | bytes 98312 | tf_op jit(solution)/shard_map/ppermute | solution.py:451
  46.0 1.4 %collective-permute-done.11.ya_ref = f32[16,512]{1,0:T(8,128)S(1)} collective-permute-done((f32[16,512]{1,0:T(8,128)S(1)}, f32[16,512]{1,0:T(8,128)S(1)}, u32[]{:S(2)}, u32[]{:S(2)}) %collective-permute-start.11) | collective-permute-done | bytes 32800 | tf_op jit(solution)/shard_map/ppermute | solution.py:454
  47.4 2.4 %shard_map.170 = (f32[256,512]{1,0:T(8,128)S(1)}, f32[256,512]{1,0:T(8,128)S(1)}, f32[16,512]{1,0:T(8,128)S(1)}, f32[16,512]{1,0:T(8,128)S(1)}, f32[16,512]{1,0:...) custom-call(f32[4,512]{1,0:T(4,128)S(1)} %broadcast_in_dim.4.ctl_ref, ...), custom_call_target="tpu_custom_call" | custom-call | tf_op jit(solution)/shard_map/pallas_call | solution.py:482
  49.8 6.0 %collective-permute-start.12 = (f32[16,512]{1,0:T(8,128)S(1)}, f32[16,512]{1,0:T(8,128)S(1)}, u32[]{:S(2)}, u32[]{:S(2)}) collective-permute-start(f32[16,512]{1,0:T(8,128)S(1)} %get-tuple-element.79), channel_id=1, source_target_pairs={{0,16},{32,48},{64,80},{96,112},{128,144},{160,176},{192,208},{224... | collective-permute-start | bytes 98312 | tf_op jit(solution)/shard_map/ppermute | solution.py:451
  56.8 2.5 %collective-permute-start.15 = (f32[16,512]{1,0:T(8,128)S(1)}, f32[16,512]{1,0:T(8,128)S(1)}, u32[]{:S(2)}, u32[]{:S(2)}) collective-permute-start(f32[16,512]{1,0:T(8,128)S(1)} %get-tuple-element.82), channel_id=1, source_target_pairs={{1,0},{2,1},{3,2},{4,3},{5,4},{6,5},{7,6},{8,7},{9,8},{10,9},{11,1... | collective-permute-start | bytes 98312 | tf_op jit(solution)/shard_map/ppermute | solution.py:454
  60.0 1.3 %collective-permute-done.15.ya_ref = f32[16,512]{1,0:T(8,128)S(1)} collective-permute-done((f32[16,512]{1,0:T(8,128)S(1)}, f32[16,512]{1,0:T(8,128)S(1)}, u32[]{:S(2)}, u32[]{:S(2)}) %collective-permute-start.15) | collective-permute-done | bytes 32800 | tf_op jit(solution)/shard_map/ppermute | solution.py:454
  61.3 2.2 %shard_map.171 = (f32[256,512]{1,0:T(8,128)S(1)}, f32[256,512]{1,0:T(8,128)S(1)}, f32[16,512]{1,0:T(8,128)S(1)}, f32[16,512]{1,0:T(8,128)S(1)}, f32[16,512]{1,0:...) custom-call(f32[4,512]{1,0:T(4,128)S(1)} %broadcast_in_dim.4.ctl_ref, ...), custom_call_target="tpu_custom_call" | custom-call | tf_op jit(solution)/shard_map/pallas_call | solution.py:486
  63.5 6.7 %collective-permute-start.16 = (f32[16,512]{1,0:T(8,128)S(1)}, f32[16,512]{1,0:T(8,128)S(1)}, u32[]{:S(2)}, u32[]{:S(2)}) collective-permute-start(f32[16,512]{1,0:T(8,128)S(1)} %get-tuple-element.85), channel_id=1, source_target_pairs={{0,16},{32,48},{64,80},{96,112},{128,144},{160,176},{192,208},{224... | collective-permute-start | bytes 98312 | tf_op jit(solution)/shard_map/ppermute | solution.py:451
  71.1 3.1 %collective-permute-start.19 = (f32[16,512]{1,0:T(8,128)S(1)}, f32[16,512]{1,0:T(8,128)S(1)}, u32[]{:S(2)}, u32[]{:S(2)}) collective-permute-start(f32[16,512]{1,0:T(8,128)S(1)} %get-tuple-element.88), channel_id=1, source_target_pairs={{1,0},{2,1},{3,2},{4,3},{5,4},{6,5},{7,6},{8,7},{9,8},{10,9},{11,1... | collective-permute-start | bytes 98312 | tf_op jit(solution)/shard_map/ppermute | solution.py:454
  75.9 3.0 %shard_map.172 = (f32[256,512]{1,0:T(8,128)S(1)}, f32[256,512]{1,0:T(8,128)S(1)}, f32[16,512]{1,0:T(8,128)S(1)}, f32[16,512]{1,0:T(8,128)S(1)}, f32[16,512]{1,0:...) custom-call(f32[4,512]{1,0:T(4,128)S(1)} %broadcast_in_dim.4.ctl_ref, f32[256,512]{1,0:T(8,128)S(1)} %get-tuple-element.84.pin_ref, ...), custom_call_target="tpu_custom_call" | custom-call | tf_op jit(solution)/shard_map/pallas_call | solution.py:490
  78.9 10.2 %all-to-all-start = ((f32[16,1,128]{2,1,0:T(1,128)}), f32[16,1,128]{2,1,0:T(1,128)S(1)}, u32[]{:S(2)}, u32[]{:S(2)}) async-start(f32[16,1,128]{2,1,0:T(1,128)} %bitcast.5), calls=%async_computation | async-start | bytes 16384 | tf_op jit(solution)/shard_map/all_to_all | solution.py:492
  89.1 4.4 %collective-permute-start.20 = (f32[16,512]{1,0:T(8,128)S(1)}, f32[16,512]{1,0:T(8,128)S(1)}, u32[]{:S(2)}, u32[]{:S(2)}) collective-permute-start(f32[16,512]{1,0:T(8,128)S(1)} %get-tuple-element.94), channel_id=1, source_target_pairs={{0,16},{32,48},{64,80},{96,112},{128,144},{160,176},{192,208},{224... | collective-permute-start | bytes 98312 | tf_op jit(solution)/shard_map/ppermute | solution.py:451
  94.2 1.9 %collective-permute-start.22 = (f32[16,512]{1,0:T(8,128)S(1)}, f32[16,512]{1,0:T(8,128)S(1)}, u32[]{:S(2)}, u32[]{:S(2)}) collective-permute-start(f32[16,512]{1,0:T(8,128)S(1)} %get-tuple-element.96), channel_id=1, source_target_pairs={{0,1},{1,2},{2,3},{3,4},{4,5},{5,6},{6,7},{7,8},{8,9},{9,10},{10,1... | collective-permute-start | bytes 98312 | tf_op jit(solution)/shard_map/ppermute | solution.py:454
  96.1 17.8 %all_to_all.15 = f32[32,1,128]{2,1,0:T(1,128)S(1)} all-to-all(f32[32,1,128]{2,1,0:T(1,128)S(1)} %broadcast_in_dim.10), channel_id=1, replica_groups=mesh['gx'=32,'gy'=16] {'gx'}, dimensions={0} | all-to-all | bytes 32768 | tf_op jit(solution)/shard_map/all_to_all | solution.py:494
  114.0 2.1 %shard_map.173 = (f32[16,16,512]{2,1,0:T(8,128)}, f32[16,16,512]{2,1,0:T(8,128)}, f32[16,16,512]{2,1,0:T(8,128)}) custom-call(f32[128]{0:T(128)S(1)} %reduce_sum.19.dots_ref, f32[4,512]{1,0:T(4,128)S(1)} %broadcast_in_dim.4.ctl_ref, f32[256,512]{1,0:T(8,128)S(1)} %get-tuple-element.93.pin_ref, f32[16,512]{1,0:T(8,128)S(1)} %collective-permute-done.20.xe_ref, ...), custom_call_target="tpu_custom_call" | custom-call | tf_op jit(solution)/shard_map/pallas_call | solution.py:496
  (54 shorter events, 12.3 us)
Async XLA Ops:
  3.1 7.1 %collective-permute-start = (f32[56,512]{1,0:T(8,128)S(1)}, f32[56,512]{1,0:T(8,128)S(1)}, u32[]{:S(2)}, u32[]{:S(2)}) collective-permute-start(f32[56,512]{1,0:T(8,128)S(1)} %get-tuple-element.53), channel_id=1, source_target_pairs={{0,16},{32,48},{64,80},{96,112},{128,144},{160,176},{192,208},{224... | collective-permute-start | bytes 344072 | tf_op jit(solution)/shard_map/ppermute | solution.py:451
  8.1 2.2 %collective-permute-start.1 = (f32[56,512]{1,0:T(8,128)S(1)}, f32[56,512]{1,0:T(8,128)S(1)}, u32[]{:S(2)}, u32[]{:S(2)}) collective-permute-start(f32[56,512]{1,0:T(8,128)S(1)} %get-tuple-element.54), channel_id=1, source_target_pairs={{16,32},{48,64},{80,96},{112,128},{144,160},{176,192},{208,224},{2... | collective-permute-start | bytes 344072 | tf_op jit(solution)/shard_map/ppermute | solution.py:451
  10.4 7.4 %collective-permute-start.2 = (f32[56,512]{1,0:T(8,128)S(1)}, f32[56,512]{1,0:T(8,128)S(1)}, u32[]{:S(2)}, u32[]{:S(2)}) collective-permute-start(f32[56,512]{1,0:T(8,128)S(1)} %get-tuple-element.57), channel_id=1, source_target_pairs={{0,1},{1,2},{2,3},{3,4},{4,5},{5,6},{6,7},{7,8},{8,9},{9,10},{10,1... | collective-permute-start | bytes 344072 | tf_op jit(solution)/shard_map/ppermute | solution.py:454
  13.5 4.5 %collective-permute-start.3 = (f32[56,512]{1,0:T(8,128)S(1)}, f32[56,512]{1,0:T(8,128)S(1)}, u32[]{:S(2)}, u32[]{:S(2)}) collective-permute-start(f32[56,512]{1,0:T(8,128)S(1)} %get-tuple-element.58), channel_id=1, source_target_pairs={{1,0},{2,1},{3,2},{4,3},{5,4},{6,5},{7,6},{8,7},{9,8},{10,9},{11,1... | collective-permute-start | bytes 344072 | tf_op jit(solution)/shard_map/ppermute | solution.py:454
  20.8 11.0 %collective-permute-start.4 = (f32[16,512]{1,0:T(8,128)S(1)}, f32[16,512]{1,0:T(8,128)S(1)}, u32[]{:S(2)}, u32[]{:S(2)}) collective-permute-start(f32[16,512]{1,0:T(8,128)S(1)} %get-tuple-element.63), channel_id=1, source_target_pairs={{0,16},{32,48},{64,80},{96,112},{128,144},{160,176},{192,208},{224... | collective-permute-start | bytes 98312 | tf_op jit(solution)/shard_map/ppermute | solution.py:451
  28.6 3.2 %collective-permute-start.5 = (f32[16,512]{1,0:T(8,128)S(1)}, f32[16,512]{1,0:T(8,128)S(1)}, u32[]{:S(2)}, u32[]{:S(2)}) collective-permute-start(f32[16,512]{1,0:T(8,128)S(1)} %get-tuple-element.64), channel_id=1, source_target_pairs={{16,32},{48,64},{80,96},{112,128},{144,160},{176,192},{208,224},{2... | collective-permute-start | bytes 98312 | tf_op jit(solution)/shard_map/ppermute | solution.py:451
  29.3 3.2 %collective-permute-start.6 = (f32[16,512]{1,0:T(8,128)S(1)}, f32[16,512]{1,0:T(8,128)S(1)}, u32[]{:S(2)}, u32[]{:S(2)}) collective-permute-start(f32[16,512]{1,0:T(8,128)S(1)} %get-tuple-element.65), channel_id=1, source_target_pairs={{0,1},{1,2},{2,3},{3,4},{4,5},{5,6},{6,7},{7,8},{8,9},{9,10},{10,1... | collective-permute-start | bytes 98312 | tf_op jit(solution)/shard_map/ppermute | solution.py:454
  29.6 3.3 %collective-permute-start.7 = (f32[16,512]{1,0:T(8,128)S(1)}, f32[16,512]{1,0:T(8,128)S(1)}, u32[]{:S(2)}, u32[]{:S(2)}) collective-permute-start(f32[16,512]{1,0:T(8,128)S(1)} %get-tuple-element.66), channel_id=1, source_target_pairs={{1,0},{2,1},{3,2},{4,3},{5,4},{6,5},{7,6},{8,7},{9,8},{10,9},{11,1... | collective-permute-start | bytes 98312 | tf_op jit(solution)/shard_map/ppermute | solution.py:454
  35.2 10.2 %collective-permute-start.8 = (f32[16,512]{1,0:T(8,128)S(1)}, f32[16,512]{1,0:T(8,128)S(1)}, u32[]{:S(2)}, u32[]{:S(2)}) collective-permute-start(f32[16,512]{1,0:T(8,128)S(1)} %get-tuple-element.73), channel_id=1, source_target_pairs={{0,16},{32,48},{64,80},{96,112},{128,144},{160,176},{192,208},{224... | collective-permute-start | bytes 98312 | tf_op jit(solution)/shard_map/ppermute | solution.py:451
  44.1 2.0 %collective-permute-start.10 = (f32[16,512]{1,0:T(8,128)S(1)}, f32[16,512]{1,0:T(8,128)S(1)}, u32[]{:S(2)}, u32[]{:S(2)}) collective-permute-start(f32[16,512]{1,0:T(8,128)S(1)} %get-tuple-element.75), channel_id=1, source_target_pairs={{0,1},{1,2},{2,3},{3,4},{4,5},{5,6},{6,7},{7,8},{8,9},{9,10},{10,1... | collective-permute-start | bytes 98312 | tf_op jit(solution)/shard_map/ppermute | solution.py:454
  44.1 3.4 %collective-permute-start.11 = (f32[16,512]{1,0:T(8,128)S(1)}, f32[16,512]{1,0:T(8,128)S(1)}, u32[]{:S(2)}, u32[]{:S(2)}) collective-permute-start(f32[16,512]{1,0:T(8,128)S(1)} %get-tuple-element.76), channel_id=1, source_target_pairs={{1,0},{2,1},{3,2},{4,3},{5,4},{6,5},{7,6},{8,7},{9,8},{10,9},{11,1... | collective-permute-start | bytes 98312 | tf_op jit(solution)/shard_map/ppermute | solution.py:454
  49.8 9.4 %collective-permute-start.12 = (f32[16,512]{1,0:T(8,128)S(1)}, f32[16,512]{1,0:T(8,128)S(1)}, u32[]{:S(2)}, u32[]{:S(2)}) collective-permute-start(f32[16,512]{1,0:T(8,128)S(1)} %get-tuple-element.79), channel_id=1, source_target_pairs={{0,16},{32,48},{64,80},{96,112},{128,144},{160,176},{192,208},{224... | collective-permute-start | bytes 98312 | tf_op jit(solution)/shard_map/ppermute | solution.py:451
  55.8 3.5 %collective-permute-start.13 = (f32[16,512]{1,0:T(8,128)S(1)}, f32[16,512]{1,0:T(8,128)S(1)}, u32[]{:S(2)}, u32[]{:S(2)}) collective-permute-start(f32[16,512]{1,0:T(8,128)S(1)} %get-tuple-element.80), channel_id=1, source_target_pairs={{16,32},{48,64},{80,96},{112,128},{144,160},{176,192},{208,224},{2... | collective-permute-start | bytes 98312 | tf_op jit(solution)/shard_map/ppermute | solution.py:451
  56.5 3.5 %collective-permute-start.14 = (f32[16,512]{1,0:T(8,128)S(1)}, f32[16,512]{1,0:T(8,128)S(1)}, u32[]{:S(2)}, u32[]{:S(2)}) collective-permute-start(f32[16,512]{1,0:T(8,128)S(1)} %get-tuple-element.81), channel_id=1, source_target_pairs={{0,1},{1,2},{2,3},{3,4},{4,5},{5,6},{6,7},{7,8},{8,9},{9,10},{10,1... | collective-permute-start | bytes 98312 | tf_op jit(solution)/shard_map/ppermute | solution.py:454
  56.8 4.5 %collective-permute-start.15 = (f32[16,512]{1,0:T(8,128)S(1)}, f32[16,512]{1,0:T(8,128)S(1)}, u32[]{:S(2)}, u32[]{:S(2)}) collective-permute-start(f32[16,512]{1,0:T(8,128)S(1)} %get-tuple-element.82), channel_id=1, source_target_pairs={{1,0},{2,1},{3,2},{4,3},{5,4},{6,5},{7,6},{8,7},{9,8},{10,9},{11,1... | collective-permute-start | bytes 98312 | tf_op jit(solution)/shard_map/ppermute | solution.py:454
  63.5 10.8 %collective-permute-start.16 = (f32[16,512]{1,0:T(8,128)S(1)}, f32[16,512]{1,0:T(8,128)S(1)}, u32[]{:S(2)}, u32[]{:S(2)}) collective-permute-start(f32[16,512]{1,0:T(8,128)S(1)} %get-tuple-element.85), channel_id=1, source_target_pairs={{0,16},{32,48},{64,80},{96,112},{128,144},{160,176},{192,208},{224... | collective-permute-start | bytes 98312 | tf_op jit(solution)/shard_map/ppermute | solution.py:451
  70.2 4.1 %collective-permute-start.17 = (f32[16,512]{1,0:T(8,128)S(1)}, f32[16,512]{1,0:T(8,128)S(1)}, u32[]{:S(2)}, u32[]{:S(2)}) collective-permute-start(f32[16,512]{1,0:T(8,128)S(1)} %get-tuple-element.86), channel_id=1, source_target_pairs={{16,32},{48,64},{80,96},{112,128},{144,160},{176,192},{208,224},{2... | collective-permute-start | bytes 98312 | tf_op jit(solution)/shard_map/ppermute | solution.py:451
  70.8 4.1 %collective-permute-start.18 = (f32[16,512]{1,0:T(8,128)S(1)}, f32[16,512]{1,0:T(8,128)S(1)}, u32[]{:S(2)}, u32[]{:S(2)}) collective-permute-start(f32[16,512]{1,0:T(8,128)S(1)} %get-tuple-element.87), channel_id=1, source_target_pairs={{0,1},{1,2},{2,3},{3,4},{4,5},{5,6},{6,7},{7,8},{8,9},{9,10},{10,1... | collective-permute-start | bytes 98312 | tf_op jit(solution)/shard_map/ppermute | solution.py:454
  71.1 4.8 %collective-permute-start.19 = (f32[16,512]{1,0:T(8,128)S(1)}, f32[16,512]{1,0:T(8,128)S(1)}, u32[]{:S(2)}, u32[]{:S(2)}) collective-permute-start(f32[16,512]{1,0:T(8,128)S(1)} %get-tuple-element.88), channel_id=1, source_target_pairs={{1,0},{2,1},{3,2},{4,3},{5,4},{6,5},{7,6},{8,7},{9,8},{10,9},{11,1... | collective-permute-start | bytes 98312 | tf_op jit(solution)/shard_map/ppermute | solution.py:454
  78.9 17.1 %all-to-all-start = ((f32[16,1,128]{2,1,0:T(1,128)}), f32[16,1,128]{2,1,0:T(1,128)S(1)}, u32[]{:S(2)}, u32[]{:S(2)}) async-start(f32[16,1,128]{2,1,0:T(1,128)} %bitcast.5), calls=%async_computation | async-start | bytes 16384 | tf_op jit(solution)/shard_map/all_to_all | solution.py:492
  89.1 24.8 %collective-permute-start.20 = (f32[16,512]{1,0:T(8,128)S(1)}, f32[16,512]{1,0:T(8,128)S(1)}, u32[]{:S(2)}, u32[]{:S(2)}) collective-permute-start(f32[16,512]{1,0:T(8,128)S(1)} %get-tuple-element.94), channel_id=1, source_target_pairs={{0,16},{32,48},{64,80},{96,112},{128,144},{160,176},{192,208},{224... | collective-permute-start | bytes 98312 | tf_op jit(solution)/shard_map/ppermute | solution.py:451
  93.5 20.5 %collective-permute-start.21 = (f32[16,512]{1,0:T(8,128)S(1)}, f32[16,512]{1,0:T(8,128)S(1)}, u32[]{:S(2)}, u32[]{:S(2)}) collective-permute-start(f32[16,512]{1,0:T(8,128)S(1)} %get-tuple-element.95), channel_id=1, source_target_pairs={{16,32},{48,64},{80,96},{112,128},{144,160},{176,192},{208,224},{2... | collective-permute-start | bytes 98312 | tf_op jit(solution)/shard_map/ppermute | solution.py:451
  94.2 19.8 %collective-permute-start.22 = (f32[16,512]{1,0:T(8,128)S(1)}, f32[16,512]{1,0:T(8,128)S(1)}, u32[]{:S(2)}, u32[]{:S(2)}) collective-permute-start(f32[16,512]{1,0:T(8,128)S(1)} %get-tuple-element.96), channel_id=1, source_target_pairs={{0,1},{1,2},{2,3},{3,4},{4,5},{5,6},{6,7},{7,8},{8,9},{9,10},{10,1... | collective-permute-start | bytes 98312 | tf_op jit(solution)/shard_map/ppermute | solution.py:454
  96.1 17.9 %collective-permute-start.23 = (f32[16,512]{1,0:T(8,128)S(1)}, f32[16,512]{1,0:T(8,128)S(1)}, u32[]{:S(2)}, u32[]{:S(2)}) collective-permute-start(f32[16,512]{1,0:T(8,128)S(1)} %get-tuple-element.97), channel_id=1, source_target_pairs={{1,0},{2,1},{3,2},{4,3},{5,4},{6,5},{7,6},{8,7},{9,8},{10,9},{11,1... | collective-permute-start | bytes 98312 | tf_op jit(solution)/shard_map/ppermute | solution.py:454
  (8 other events, 81.5 us)

commit v5 on v4

--- a/solution.py
+++ b/solution.py
@@ -229,11 +229,13 @@
 
 
 def first_kernel(ctl_ref, table_hbm, load_hbm, cond_hbm, flags_hbm, region_hbm, sq_hbm, sqz_hbm, wr_hbm, wz_hbm,
-                 coef_ref, react_ref, keep_ref, pl_ref, pd_ref, even_ref, odd_ref, yl_ref, yh_ref,
+                 gf_hbm, bf_hbm,
+                 coef_ref, react_ref, keep_ref, pl_ref, pd_ref, even_ref, odd_ref, yl_ref, yh_ref, gf_ref, bf_ref,
                  table_ref, load_ref, cond_ref, flags_ref, region_ref, sq_ref, sqz_ref, wr_ref, wz_ref, sems, st_ref):
     flags_tile = flags_hbm.at[:, :, pl.ds(0, 128)]
     pairs = ((cond_hbm, cond_ref), (wr_hbm, wr_ref), (wz_hbm, wz_ref), (region_hbm, region_ref), (table_hbm, table_ref),
-             (sq_hbm, sq_ref), (sqz_hbm, sqz_ref), (load_hbm, load_ref), (flags_tile, flags_ref))
+             (sq_hbm, sq_ref), (sqz_hbm, sqz_ref), (load_hbm, load_ref), (flags_tile, flags_ref),
+             (gf_hbm, gf_ref), (bf_hbm, bf_ref))
     copies = [pltpu.make_async_copy(src, dst, sems.at[i]) for i, (src, dst) in enumerate(pairs)]
     for copy in copies:
         copy.start()
@@ -390,29 +392,42 @@
     emit_partial(f, lines, ctl_ref, p_ref, (even, odd, low_y, high_y), st_ref)
     last = fold(f * ((1.0 + MIX2) * z_ref[...] - (CENTER * GAIN2) * b0))
     both = last + (CENTER * GAIN2 - MIX2) * d5_ref[...]
+    rows = [part.sum(axis=0, keepdims=True) for part in (d34_ref[0], d34_ref[1], both)]
     lane = lax.broadcasted_iota(jnp.int32, (1, 128), 1)
-    sums = jnp.where(
-        lane == 0, jnp.sum(d34_ref[0]), jnp.where(lane == 1, jnp.sum(d34_ref[1]), jnp.sum(both)))
-    dots_ref[...] = jnp.broadcast_to(sums, dots_ref.shape)
+    packed = jnp.zeros((1, 128), F32)
+    for i, row in enumerate(rows):
+        row = row + pltpu.roll(row, 64, 1)
+        row = row + pltpu.roll(row, 32, 1)
+        packed = jnp.where(lane // 32 == i, row, packed)
+    dots_ref[...] = jnp.broadcast_to(packed, dots_ref.shape)
 
 
 def last_kernel(dots_ref, ctl_ref, pin_ref, xe_ref, xo_ref, yb_ref, ya_ref, im_ref, dinv_ref, b1_ref, z_ref, r_ref,
-                sol_ref, res_ref, dir_ref, s_ref):
-    first, curv, quad = dots_ref[0], dots_ref[1], dots_ref[2]
+                sol_hbm, res_hbm, dir_hbm, s_ref, sol_ref, res_ref, dir_ref, sems):
+    lane = lax.broadcasted_iota(jnp.int32, (8, 128), 1)
+    row = lax.broadcasted_iota(jnp.int32, (8, 128), 0)
+    sums = jnp.sum(dots_ref[...], axis=0, keepdims=True)
+    sums = jnp.sum(jnp.where(lane // 32 == row, sums, 0.0), axis=1, keepdims=True)
+    first, curv, quad = sums[0:1], sums[1:2], sums[2:3]
     step = first / curv
     ratio = (first - 2.0 * step * curv + step * step * quad) / first
+    shape = (16, 16, COLS)
+    copies = [pltpu.make_async_copy(src, dst, sems.at[i])
+              for i, (src, dst) in enumerate(((sol_ref, sol_hbm), (res_ref, res_hbm), (dir_ref, dir_hbm)))]
+    z, im = z_ref[...], im_ref[...]
+    sol_ref[...] = (step * z).reshape(shape)
+    copies[0].start()
+    res_ref[...] = (r_ref[...] - step * im).reshape(shape)
+    copies[1].start()
     image = take_sum(pin_ref, (*pick(ctl_ref, xe_ref[...], xo_ref[...]), yb_ref[...], ya_ref[...]), s_ref)
-    im = im_ref[...]
     b2 = sweep2(image, b1_ref[...], im, dinv_ref[...])
-    z = z_ref[...]
-    shape = (16, 16, COLS)
-    sol_ref[...] = (step * z).reshape(shape)
-    res_ref[...] = (r_ref[...] - step * im).reshape(shape)
     dir_ref[...] = ((z - step * b2) + ratio * z).reshape(shape)
+    copies[2].start()
+    for copy in copies:
+        copy.wait()
 
 
 VM = pl.BlockSpec(memory_space=pltpu.VMEM)
-SM = pl.BlockSpec(memory_space=pltpu.SMEM)
 HB = pl.BlockSpec(memory_space=pl.ANY)
 BIG = jax.ShapeDtypeStruct((ROWS, COLS), F32)
 FACE = jax.ShapeDtypeStruct((16, COLS), F32)
@@ -439,7 +454,6 @@
 
 def per_device(load, conductivity, flags, region, kappa_table):
     k = {name: jnp.asarray(value) for name, value in constants().items()}
-    mats = (k["grad"], k["back"], k["grad_z"], k["back_z"], k["grad_f"], k["back_f"])
     n_x, n_y = lax.axis_size("gx"), lax.axis_size("gy")
     at_x, at_y = lax.axis_index("gx"), lax.axis_index("gy")
     ctl = jnp.stack([at_x % 2 == 1, at_y != 0, at_y != n_y - 1, at_y < 0]).astype(F32)
@@ -458,14 +472,18 @@
         return (*along_x(even, odd), *along_y(low_y, high_y))
 
     keep_shape = jax.ShapeDtypeStruct((ROWS, 128), F32)
-    inputs = (kappa_table, load, conductivity, flags, region, k["sq"], k["sq_z"], k["w_rows"], k["w_z"])
+    inputs = (kappa_table, load, conductivity, flags, region, k["sq"], k["sq_z"], k["w_rows"], k["w_z"],
+              k["grad_f"], k["back_f"])
     inputs = tuple(pltpu.with_memory_space_constraint(v, pltpu.HBM) for v in inputs)
-    buffers = [pltpu.VMEM(v.shape, v.dtype) for v in inputs]
+    buffers = [pltpu.VMEM(v.shape, v.dtype) for v in inputs[:9]]
     buffers[0] = pltpu.SMEM(kappa_table.shape, F32)
     buffers[3] = pltpu.VMEM((16, 16, 128), jnp.int32)
     buffers += [pltpu.SemaphoreType.DMA((len(inputs),)), pltpu.VMEM((2, 56, COLS), F32)]
-    coef, react, keep, part_l, part_d, even, odd, low_y, high_y = call(
-        first_kernel, (BIG, BIG, keep_shape, BIG, BIG) + (MESSAGE,) * 4, [VM] + [HB] * len(inputs), buffers)(ctl, *inputs)
+    small = tuple(jax.ShapeDtypeStruct(v.shape, v.dtype) for v in inputs[9:])
+    coef, react, keep, part_l, part_d, even, odd, low_y, high_y, grad_f, back_f = call(
+        first_kernel, (BIG, BIG, keep_shape, BIG, BIG) + (MESSAGE,) * 4 + small, [VM] + [HB] * len(inputs),
+        buffers)(ctl, *inputs)
+    mats = (k["grad"], k["back"], k["grad_z"], k["back_z"], grad_f, back_f)
     even, odd = along_x(even, odd)
     low_y, high_y = call(corner_kernel, (MESSAGE, MESSAGE), [VM] * 5, [pltpu.VMEM((2, 56, COLS), F32)])(
         ctl, even, odd, low_y, high_y)
@@ -491,10 +509,12 @@
         ctl, part, *recv, im, dinv, z, d34, d5, *tail)
     total = lax.all_to_all(dots, "gy", 0, 0, tiled=True).sum(0)
     recv = exchange(faces)
-    total = lax.all_to_all(jnp.broadcast_to(total, (n_x, 128)), "gx", 0, 0, tiled=True).sum(0)
+    total = lax.all_to_all(jnp.broadcast_to(total, (n_x, 128)), "gx", 0, 0, tiled=True)
     shape = jax.ShapeDtypeStruct((16, 16, COLS), F32)
-    return call(last_kernel, (shape, shape, shape), [SM] + [VM] * 11, [pltpu.VMEM((ROWS, COLS), F32)])(
-        total, ctl, part, *recv, im, dinv, b1, z, r)
+    scratch = [pltpu.VMEM((ROWS, COLS), F32)] + [pltpu.VMEM((16, 16, COLS), F32)] * 3 + [pltpu.SemaphoreType.DMA((3,))]
+    return pl.pallas_call(
+        last_kernel, out_shape=(shape, shape, shape), in_specs=[VM] * 12, out_specs=(HB, HB, HB),
+        scratch_shapes=scratch, compiler_params=PARAMS)(total, ctl, part, *recv, im, dinv, b1, z, r)
 
 
 def solution(mesh):

time: 118 us -> 118 us (level)
  blocking collectives: 17.8 us -> 0 us
  starting transfers between devices: 70.6 us -> 80 us
  waiting for transfers between devices: 9.37 us -> 17.9 us
    all_to_all x1 -> x0, blocking collectives: 17.8 us -> none  [per_device(): lax.all_to_all(jnp.broadcast_to(total, (n_x, 128)), 'gx', 0, 0, tiled=True)]
    all_to_all x0 -> x1, starting transfers between devices: none -> 9.34 us  [per_device(): lax.all_to_all(jnp.broadcast_to(total, (n_x, 128)), 'gx', 0, 0, tiled=True)]
    all_to_all x0 -> x1, waiting for transfers between devices: none -> 8.52 us  [per_device(): lax.all_to_all(jnp.broadcast_to(total, (n_x, 128)), 'gx', 0, 0, tiled=True)]
  transfers between devices with their start and end apart: 25 -> 26, of which waited for: 11 -> 12; matrix products, arithmetic and copies ran while one was open for 0% -> 1% of each run, Pallas kernels for 0% -> 0%
where the time goes in v5:
time: 118 us; the launch traced here: 116 us
  starting transfers between devices  80 us (68%)
  waiting for transfers between devices  17.9 us (15%)
  Pallas kernels  16.1 us (14%)
    ppermute x6, starting transfers between devices, along_x(): lax.ppermute(even, 'gx', swaps(0, n_x))  38 us
    ppermute x12, starting transfers between devices, along_y(): return (lax.ppermute(high, 'gy', up_y), lax.ppermute(low, 'gy', down_y))  18.5 us
    all_to_all x1, starting transfers between devices, per_device(): total = lax.all_to_all(dots, 'gy', 0, 0, tiled=True).sum(0)  10.2 us
    all_to_all x1, starting transfers between devices, per_device(): lax.all_to_all(jnp.broadcast_to(total, (n_x, 128)), 'gx', 0, 0, tiled=True)  9.34 us
    all_to_all x1, waiting for transfers between devices, per_device(): lax.all_to_all(jnp.broadcast_to(total, (n_x, 128)), 'gx', 0, 0, tiled=True)  8.52 us
    ppermute x12, waiting for transfers between devices, along_y(): return (lax.ppermute(high, 'gy', up_y), lax.ppermute(low, 'gy', down_y))  7.89 us
    ppermute x6, starting transfers between devices, along_x(): lax.ppermute(odd, 'gx', swaps(1, n_x))  3.98 us
    pallas_call x1, Pallas kernels, per_device(): step_call(fifth_kernel, (BIG,) + PART + (dots_shape,), 21)  2.99 us
  transfers between devices with their start and end apart: 26, of which 12 were waited for; matrix products, arithmetic and copies ran while one was open for 1% of the time, Pallas kernels for 0%

profile of v5, /device:TPU:1, one launch (start us, length us, event | category | flops | bytes accessed | tf_op | source)
XLA Modules:
  0.0 115.7 jit_solution(15831658555517170729)
XLA Ops:
  0.8 2.3 %shard_map.166 = (f32[256,512]{1,0:T(8,128)S(1)}, f32[256,512]{1,0:T(8,128)S(1)}, f32[256,128]{1,0:T(8,128)S(1)}, f32[256,512]{1,0:T(8,128)S(1)}, f32[256,512]{1...) custom-call(f32[4,512]{1,0:T(4,128)S(1)} %broadcast_in_dim.4.ctl_ref, ...), custom_call_target="tpu_custom_call" | custom-call | tf_op jit(solution)/shard_map/pallas_call | solution.py:483
  3.1 5.0 %collective-permute-start = (f32[56,512]{1,0:T(8,128)S(1)}, f32[56,512]{1,0:T(8,128)S(1)}, u32[]{:S(2)}, u32[]{:S(2)}) collective-permute-start(f32[56,512]{1,0:T(8,128)S(1)} %get-tuple-element.55), channel_id=1, source_target_pairs={{0,16},{32,48},{64,80},{96,112},{128,144},{160,176},{192,208},{224... | collective-permute-start | bytes 344072 | tf_op jit(solution)/shard_map/ppermute | solution.py:465
  8.8 1.5 %collective-permute-done.even_ref.xe_ref = f32[56,512]{1,0:T(8,128)S(1)} collective-permute-done((f32[56,512]{1,0:T(8,128)S(1)}, f32[56,512]{1,0:T(8,128)S(1)}, u32[]{:S(2)}, u32[]{:S(2)}) %collective-permute-start) | collective-permute-done | bytes 114720 | tf_op jit(solution)/shard_map/ppermute | solution.py:465
  10.4 3.1 %collective-permute-start.2 = (f32[56,512]{1,0:T(8,128)S(1)}, f32[56,512]{1,0:T(8,128)S(1)}, u32[]{:S(2)}, u32[]{:S(2)}) collective-permute-start(f32[56,512]{1,0:T(8,128)S(1)} %get-tuple-element.59), channel_id=1, source_target_pairs={{0,1},{1,2},{2,3},{3,4},{4,5},{5,6},{6,7},{7,8},{8,9},{9,10},{10,1... | collective-permute-start | bytes 344072 | tf_op jit(solution)/shard_map/ppermute | solution.py:468
  13.5 3.5 %collective-permute-start.3 = (f32[56,512]{1,0:T(8,128)S(1)}, f32[56,512]{1,0:T(8,128)S(1)}, u32[]{:S(2)}, u32[]{:S(2)}) collective-permute-start(f32[56,512]{1,0:T(8,128)S(1)} %get-tuple-element.60), channel_id=1, source_target_pairs={{1,0},{2,1},{3,2},{4,3},{5,4},{6,5},{7,6},{8,7},{9,8},{10,9},{11,1... | collective-permute-start | bytes 344072 | tf_op jit(solution)/shard_map/ppermute | solution.py:468
  17.9 2.2 %shard_map.168 = (f32[256,512]{1,0:T(8,128)S(1)}, f32[256,512]{1,0:T(8,128)S(1)}, f32[64,512]{1,0:T(8,128)S(1)}, f32[8,512]{1,0:T(8,128)S(1)}, f32[8,512]{1,0:T(...) custom-call(f32[4,512]{1,0:T(4,128)S(1)} %broadcast_in_dim.4.ctl_ref, ...), custom_call_target="tpu_custom_call" | custom-call | tf_op jit(solution)/shard_map/pallas_call | solution.py:492
  20.2 7.8 %collective-permute-start.4 = (f32[16,512]{1,0:T(8,128)S(1)}, f32[16,512]{1,0:T(8,128)S(1)}, u32[]{:S(2)}, u32[]{:S(2)}) collective-permute-start(f32[16,512]{1,0:T(8,128)S(1)} %get-tuple-element.67), channel_id=1, source_target_pairs={{0,16},{32,48},{64,80},{96,112},{128,144},{160,176},{192,208},{224... | collective-permute-start | bytes 98312 | tf_op jit(solution)/shard_map/ppermute | solution.py:465
  29.0 2.2 %collective-permute-start.7 = (f32[16,512]{1,0:T(8,128)S(1)}, f32[16,512]{1,0:T(8,128)S(1)}, u32[]{:S(2)}, u32[]{:S(2)}) collective-permute-start(f32[16,512]{1,0:T(8,128)S(1)} %get-tuple-element.70), channel_id=1, source_target_pairs={{1,0},{2,1},{3,2},{4,3},{5,4},{6,5},{7,6},{8,7},{9,8},{10,9},{11,1... | collective-permute-start | bytes 98312 | tf_op jit(solution)/shard_map/ppermute | solution.py:468
  32.3 2.2 %shard_map.169 = (f32[256,512]{1,0:T(8,128)S(1)}, f32[256,512]{1,0:T(8,128)S(1)}, f32[16,512]{1,0:T(8,128)S(1)}, f32[16,512]{1,0:T(8,128)S(1)}, f32[16,512]{1,0:T(8,128)S(1)}, /*index=5*/f32[16,512]{1,0:T(8,128)S(1)}) custom-call(f32[4,512]{1,0:T(4,128)S(1)} %broadcast_in_dim.4.ctl_ref, f32[256,512]{1,0:T(8,128)S(1)} %get-tuple-element.66.pin_ref, ...), custom_call_target="tpu_custom_call" | custom-call | tf_op jit(solution)/shard_map/pallas_call | solution.py:497
  34.5 8.2 %collective-permute-start.8 = (f32[16,512]{1,0:T(8,128)S(1)}, f32[16,512]{1,0:T(8,128)S(1)}, u32[]{:S(2)}, u32[]{:S(2)}) collective-permute-start(f32[16,512]{1,0:T(8,128)S(1)} %get-tuple-element.77), channel_id=1, source_target_pairs={{0,16},{32,48},{64,80},{96,112},{128,144},{160,176},{192,208},{224... | collective-permute-start | bytes 98312 | tf_op jit(solution)/shard_map/ppermute | solution.py:465
  45.4 1.4 %collective-permute-done.11.ya_ref = f32[16,512]{1,0:T(8,128)S(1)} collective-permute-done((f32[16,512]{1,0:T(8,128)S(1)}, f32[16,512]{1,0:T(8,128)S(1)}, u32[]{:S(2)}, u32[]{:S(2)}) %collective-permute-start.11) | collective-permute-done | bytes 32800 | tf_op jit(solution)/shard_map/ppermute | solution.py:468
  46.8 2.4 %shard_map.170 = (f32[256,512]{1,0:T(8,128)S(1)}, f32[256,512]{1,0:T(8,128)S(1)}, f32[16,512]{1,0:T(8,128)S(1)}, f32[16,512]{1,0:T(8,128)S(1)}, f32[16,512]{1,0:...) custom-call(f32[4,512]{1,0:T(4,128)S(1)} %broadcast_in_dim.4.ctl_ref, ...), custom_call_target="tpu_custom_call" | custom-call | tf_op jit(solution)/shard_map/pallas_call | solution.py:500
  49.2 6.0 %collective-permute-start.12 = (f32[16,512]{1,0:T(8,128)S(1)}, f32[16,512]{1,0:T(8,128)S(1)}, u32[]{:S(2)}, u32[]{:S(2)}) collective-permute-start(f32[16,512]{1,0:T(8,128)S(1)} %get-tuple-element.83), channel_id=1, source_target_pairs={{0,16},{32,48},{64,80},{96,112},{128,144},{160,176},{192,208},{224... | collective-permute-start | bytes 98312 | tf_op jit(solution)/shard_map/ppermute | solution.py:465
  56.2 2.5 %collective-permute-start.15 = (f32[16,512]{1,0:T(8,128)S(1)}, f32[16,512]{1,0:T(8,128)S(1)}, u32[]{:S(2)}, u32[]{:S(2)}) collective-permute-start(f32[16,512]{1,0:T(8,128)S(1)} %get-tuple-element.86), channel_id=1, source_target_pairs={{1,0},{2,1},{3,2},{4,3},{5,4},{6,5},{7,6},{8,7},{9,8},{10,9},{11,1... | collective-permute-start | bytes 98312 | tf_op jit(solution)/shard_map/ppermute | solution.py:468
  60.6 2.2 %shard_map.171 = (f32[256,512]{1,0:T(8,128)S(1)}, f32[256,512]{1,0:T(8,128)S(1)}, f32[16,512]{1,0:T(8,128)S(1)}, f32[16,512]{1,0:T(8,128)S(1)}, f32[16,512]{1,0:...) custom-call(f32[4,512]{1,0:T(4,128)S(1)} %broadcast_in_dim.4.ctl_ref, ...), custom_call_target="tpu_custom_call" | custom-call | tf_op jit(solution)/shard_map/pallas_call | solution.py:504
  62.8 6.7 %collective-permute-start.16 = (f32[16,512]{1,0:T(8,128)S(1)}, f32[16,512]{1,0:T(8,128)S(1)}, u32[]{:S(2)}, u32[]{:S(2)}) collective-permute-start(f32[16,512]{1,0:T(8,128)S(1)} %get-tuple-element.89), channel_id=1, source_target_pairs={{0,16},{32,48},{64,80},{96,112},{128,144},{160,176},{192,208},{224... | collective-permute-start | bytes 98312 | tf_op jit(solution)/shard_map/ppermute | solution.py:465
  70.5 3.1 %collective-permute-start.19 = (f32[16,512]{1,0:T(8,128)S(1)}, f32[16,512]{1,0:T(8,128)S(1)}, u32[]{:S(2)}, u32[]{:S(2)}) collective-permute-start(f32[16,512]{1,0:T(8,128)S(1)} %get-tuple-element.92), channel_id=1, source_target_pairs={{1,0},{2,1},{3,2},{4,3},{5,4},{6,5},{7,6},{8,7},{9,8},{10,9},{11,1... | collective-permute-start | bytes 98312 | tf_op jit(solution)/shard_map/ppermute | solution.py:468
  75.3 3.0 %shard_map.172 = (f32[256,512]{1,0:T(8,128)S(1)}, f32[256,512]{1,0:T(8,128)S(1)}, f32[16,512]{1,0:T(8,128)S(1)}, f32[16,512]{1,0:T(8,128)S(1)}, f32[16,512]{1,0:...) custom-call(f32[4,512]{1,0:T(4,128)S(1)} %broadcast_in_dim.4.ctl_ref, f32[256,512]{1,0:T(8,128)S(1)} %get-tuple-element.88.pin_ref, ...), custom_call_target="tpu_custom_call" | custom-call | tf_op jit(solution)/shard_map/pallas_call | solution.py:508
  78.3 10.2 %all-to-all-start = ((f32[16,1,128]{2,1,0:T(1,128)}), f32[16,1,128]{2,1,0:T(1,128)S(1)}, u32[]{:S(2)}, u32[]{:S(2)}) async-start(f32[16,1,128]{2,1,0:T(1,128)} %bitcast.5), calls=%async_computation | async-start | bytes 16384 | tf_op jit(solution)/shard_map/all_to_all | solution.py:510
  88.5 4.4 %collective-permute-start.20 = (f32[16,512]{1,0:T(8,128)S(1)}, f32[16,512]{1,0:T(8,128)S(1)}, u32[]{:S(2)}, u32[]{:S(2)}) collective-permute-start(f32[16,512]{1,0:T(8,128)S(1)} %get-tuple-element.98), channel_id=1, source_target_pairs={{0,16},{32,48},{64,80},{96,112},{128,144},{160,176},{192,208},{224... | collective-permute-start | bytes 98312 | tf_op jit(solution)/shard_map/ppermute | solution.py:465
  93.6 1.9 %collective-permute-start.22 = (f32[16,512]{1,0:T(8,128)S(1)}, f32[16,512]{1,0:T(8,128)S(1)}, u32[]{:S(2)}, u32[]{:S(2)}) collective-permute-start(f32[16,512]{1,0:T(8,128)S(1)} %get-tuple-element.100), channel_id=1, source_target_pairs={{0,1},{1,2},{2,3},{3,4},{4,5},{5,6},{6,7},{7,8},{8,9},{9,10},{10,1... | collective-permute-start | bytes 98312 | tf_op jit(solution)/shard_map/ppermute | solution.py:468
  96.1 9.3 %all-to-all-start.1 = ((f32[32,1,128]{2,1,0:T(1,128)}), f32[32,1,128]{2,1,0:T(1,128)S(1)}, u32[]{:S(2)}, u32[]{:S(2)}) async-start(f32[32,1,128]{2,1,0:T(1,128)} %broadcast_in_dim.10), calls=%async_computation.1 | async-start | bytes 32768 | tf_op jit(solution)/shard_map/all_to_all | solution.py:512
  105.5 8.5 %all-to-all-done.1 = f32[32,1,128]{2,1,0:T(1,128)S(1)} async-done(((f32[32,1,128]{2,1,0:T(1,128)}), f32[32,1,128]{2,1,0:T(1,128)S(1)}, u32[]{:S(2)}, u32[]{:S(2)}) %all-to-all-start.1) | async-done | bytes 16416 | tf_op jit(solution)/shard_map/all_to_all | solution.py:512
  114.0 1.7 %shard_map.173 = (f32[16,16,512]{2,1,0:T(8,128)}, f32[16,16,512]{2,1,0:T(8,128)}, f32[16,16,512]{2,1,0:T(8,128)}) custom-call(f32[32,128]{1,0:T(8,128)S(1)} %bitcast.8, f32[4,512]{1,0:T(4,128)S(1)} %broadcast_in_dim.4.ctl_ref, f32[256,512]{1,0:T(8,128)S(1)} %get-tuple-element.97.pin_ref, f32[16,512]{1,0:T(8,128)S(1)} %collective-permute-done.20.xe_ref, ...), custom_call_target="tpu_custom_call" | custom-call | tf_op jit(solution)/shard_map/pallas_call | solution.py:515
  (50 shorter events, 13.5 us)
Async XLA Ops:
  3.1 7.1 %collective-permute-start = (f32[56,512]{1,0:T(8,128)S(1)}, f32[56,512]{1,0:T(8,128)S(1)}, u32[]{:S(2)}, u32[]{:S(2)}) collective-permute-start(f32[56,512]{1,0:T(8,128)S(1)} %get-tuple-element.55), channel_id=1, source_target_pairs={{0,16},{32,48},{64,80},{96,112},{128,144},{160,176},{192,208},{224... | collective-permute-start | bytes 344072 | tf_op jit(solution)/shard_map/ppermute | solution.py:465
  8.1 2.2 %collective-permute-start.1 = (f32[56,512]{1,0:T(8,128)S(1)}, f32[56,512]{1,0:T(8,128)S(1)}, u32[]{:S(2)}, u32[]{:S(2)}) collective-permute-start(f32[56,512]{1,0:T(8,128)S(1)} %get-tuple-element.56), channel_id=1, source_target_pairs={{16,32},{48,64},{80,96},{112,128},{144,160},{176,192},{208,224},{2... | collective-permute-start | bytes 344072 | tf_op jit(solution)/shard_map/ppermute | solution.py:465
  10.4 7.4 %collective-permute-start.2 = (f32[56,512]{1,0:T(8,128)S(1)}, f32[56,512]{1,0:T(8,128)S(1)}, u32[]{:S(2)}, u32[]{:S(2)}) collective-permute-start(f32[56,512]{1,0:T(8,128)S(1)} %get-tuple-element.59), channel_id=1, source_target_pairs={{0,1},{1,2},{2,3},{3,4},{4,5},{5,6},{6,7},{7,8},{8,9},{9,10},{10,1... | collective-permute-start | bytes 344072 | tf_op jit(solution)/shard_map/ppermute | solution.py:468
  13.5 4.5 %collective-permute-start.3 = (f32[56,512]{1,0:T(8,128)S(1)}, f32[56,512]{1,0:T(8,128)S(1)}, u32[]{:S(2)}, u32[]{:S(2)}) collective-permute-start(f32[56,512]{1,0:T(8,128)S(1)} %get-tuple-element.60), channel_id=1, source_target_pairs={{1,0},{2,1},{3,2},{4,3},{5,4},{6,5},{7,6},{8,7},{9,8},{10,9},{11,1... | collective-permute-start | bytes 344072 | tf_op jit(solution)/shard_map/ppermute | solution.py:468
  20.2 11.0 %collective-permute-start.4 = (f32[16,512]{1,0:T(8,128)S(1)}, f32[16,512]{1,0:T(8,128)S(1)}, u32[]{:S(2)}, u32[]{:S(2)}) collective-permute-start(f32[16,512]{1,0:T(8,128)S(1)} %get-tuple-element.67), channel_id=1, source_target_pairs={{0,16},{32,48},{64,80},{96,112},{128,144},{160,176},{192,208},{224... | collective-permute-start | bytes 98312 | tf_op jit(solution)/shard_map/ppermute | solution.py:465
  28.0 3.2 %collective-permute-start.5 = (f32[16,512]{1,0:T(8,128)S(1)}, f32[16,512]{1,0:T(8,128)S(1)}, u32[]{:S(2)}, u32[]{:S(2)}) collective-permute-start(f32[16,512]{1,0:T(8,128)S(1)} %get-tuple-element.68), channel_id=1, source_target_pairs={{16,32},{48,64},{80,96},{112,128},{144,160},{176,192},{208,224},{2... | collective-permute-start | bytes 98312 | tf_op jit(solution)/shard_map/ppermute | solution.py:465
  28.7 3.2 %collective-permute-start.6 = (f32[16,512]{1,0:T(8,128)S(1)}, f32[16,512]{1,0:T(8,128)S(1)}, u32[]{:S(2)}, u32[]{:S(2)}) collective-permute-start(f32[16,512]{1,0:T(8,128)S(1)} %get-tuple-element.69), channel_id=1, source_target_pairs={{0,1},{1,2},{2,3},{3,4},{4,5},{5,6},{6,7},{7,8},{8,9},{9,10},{10,1... | collective-permute-start | bytes 98312 | tf_op jit(solution)/shard_map/ppermute | solution.py:468
  29.0 3.3 %collective-permute-start.7 = (f32[16,512]{1,0:T(8,128)S(1)}, f32[16,512]{1,0:T(8,128)S(1)}, u32[]{:S(2)}, u32[]{:S(2)}) collective-permute-start(f32[16,512]{1,0:T(8,128)S(1)} %get-tuple-element.70), channel_id=1, source_target_pairs={{1,0},{2,1},{3,2},{4,3},{5,4},{6,5},{7,6},{8,7},{9,8},{10,9},{11,1... | collective-permute-start | bytes 98312 | tf_op jit(solution)/shard_map/ppermute | solution.py:468
  34.5 10.2 %collective-permute-start.8 = (f32[16,512]{1,0:T(8,128)S(1)}, f32[16,512]{1,0:T(8,128)S(1)}, u32[]{:S(2)}, u32[]{:S(2)}) collective-permute-start(f32[16,512]{1,0:T(8,128)S(1)} %get-tuple-element.77), channel_id=1, source_target_pairs={{0,16},{32,48},{64,80},{96,112},{128,144},{160,176},{192,208},{224... | collective-permute-start | bytes 98312 | tf_op jit(solution)/shard_map/ppermute | solution.py:465
  43.5 3.4 %collective-permute-start.11 = (f32[16,512]{1,0:T(8,128)S(1)}, f32[16,512]{1,0:T(8,128)S(1)}, u32[]{:S(2)}, u32[]{:S(2)}) collective-permute-start(f32[16,512]{1,0:T(8,128)S(1)} %get-tuple-element.80), channel_id=1, source_target_pairs={{1,0},{2,1},{3,2},{4,3},{5,4},{6,5},{7,6},{8,7},{9,8},{10,9},{11,1... | collective-permute-start | bytes 98312 | tf_op jit(solution)/shard_map/ppermute | solution.py:468
  49.2 9.4 %collective-permute-start.12 = (f32[16,512]{1,0:T(8,128)S(1)}, f32[16,512]{1,0:T(8,128)S(1)}, u32[]{:S(2)}, u32[]{:S(2)}) collective-permute-start(f32[16,512]{1,0:T(8,128)S(1)} %get-tuple-element.83), channel_id=1, source_target_pairs={{0,16},{32,48},{64,80},{96,112},{128,144},{160,176},{192,208},{224... | collective-permute-start | bytes 98312 | tf_op jit(solution)/shard_map/ppermute | solution.py:465
  55.2 3.4 %collective-permute-start.13 = (f32[16,512]{1,0:T(8,128)S(1)}, f32[16,512]{1,0:T(8,128)S(1)}, u32[]{:S(2)}, u32[]{:S(2)}) collective-permute-start(f32[16,512]{1,0:T(8,128)S(1)} %get-tuple-element.84), channel_id=1, source_target_pairs={{16,32},{48,64},{80,96},{112,128},{144,160},{176,192},{208,224},{2... | collective-permute-start | bytes 98312 | tf_op jit(solution)/shard_map/ppermute | solution.py:465
  55.9 3.4 %collective-permute-start.14 = (f32[16,512]{1,0:T(8,128)S(1)}, f32[16,512]{1,0:T(8,128)S(1)}, u32[]{:S(2)}, u32[]{:S(2)}) collective-permute-start(f32[16,512]{1,0:T(8,128)S(1)} %get-tuple-element.85), channel_id=1, source_target_pairs={{0,1},{1,2},{2,3},{3,4},{4,5},{5,6},{6,7},{7,8},{8,9},{9,10},{10,1... | collective-permute-start | bytes 98312 | tf_op jit(solution)/shard_map/ppermute | solution.py:468
  56.2 4.5 %collective-permute-start.15 = (f32[16,512]{1,0:T(8,128)S(1)}, f32[16,512]{1,0:T(8,128)S(1)}, u32[]{:S(2)}, u32[]{:S(2)}) collective-permute-start(f32[16,512]{1,0:T(8,128)S(1)} %get-tuple-element.86), channel_id=1, source_target_pairs={{1,0},{2,1},{3,2},{4,3},{5,4},{6,5},{7,6},{8,7},{9,8},{10,9},{11,1... | collective-permute-start | bytes 98312 | tf_op jit(solution)/shard_map/ppermute | solution.py:468
  62.8 10.8 %collective-permute-start.16 = (f32[16,512]{1,0:T(8,128)S(1)}, f32[16,512]{1,0:T(8,128)S(1)}, u32[]{:S(2)}, u32[]{:S(2)}) collective-permute-start(f32[16,512]{1,0:T(8,128)S(1)} %get-tuple-element.89), channel_id=1, source_target_pairs={{0,16},{32,48},{64,80},{96,112},{128,144},{160,176},{192,208},{224... | collective-permute-start | bytes 98312 | tf_op jit(solution)/shard_map/ppermute | solution.py:465
  69.5 4.1 %collective-permute-start.17 = (f32[16,512]{1,0:T(8,128)S(1)}, f32[16,512]{1,0:T(8,128)S(1)}, u32[]{:S(2)}, u32[]{:S(2)}) collective-permute-start(f32[16,512]{1,0:T(8,128)S(1)} %get-tuple-element.90), channel_id=1, source_target_pairs={{16,32},{48,64},{80,96},{112,128},{144,160},{176,192},{208,224},{2... | collective-permute-start | bytes 98312 | tf_op jit(solution)/shard_map/ppermute | solution.py:465
  70.2 4.1 %collective-permute-start.18 = (f32[16,512]{1,0:T(8,128)S(1)}, f32[16,512]{1,0:T(8,128)S(1)}, u32[]{:S(2)}, u32[]{:S(2)}) collective-permute-start(f32[16,512]{1,0:T(8,128)S(1)} %get-tuple-element.91), channel_id=1, source_target_pairs={{0,1},{1,2},{2,3},{3,4},{4,5},{5,6},{6,7},{7,8},{8,9},{9,10},{10,1... | collective-permute-start | bytes 98312 | tf_op jit(solution)/shard_map/ppermute | solution.py:468
  70.5 4.8 %collective-permute-start.19 = (f32[16,512]{1,0:T(8,128)S(1)}, f32[16,512]{1,0:T(8,128)S(1)}, u32[]{:S(2)}, u32[]{:S(2)}) collective-permute-start(f32[16,512]{1,0:T(8,128)S(1)} %get-tuple-element.92), channel_id=1, source_target_pairs={{1,0},{2,1},{3,2},{4,3},{5,4},{6,5},{7,6},{8,7},{9,8},{10,9},{11,1... | collective-permute-start | bytes 98312 | tf_op jit(solution)/shard_map/ppermute | solution.py:468
  78.3 17.1 %all-to-all-start = ((f32[16,1,128]{2,1,0:T(1,128)}), f32[16,1,128]{2,1,0:T(1,128)S(1)}, u32[]{:S(2)}, u32[]{:S(2)}) async-start(f32[16,1,128]{2,1,0:T(1,128)} %bitcast.5), calls=%async_computation | async-start | bytes 16384 | tf_op jit(solution)/shard_map/all_to_all | solution.py:510
  88.5 16.9 %collective-permute-start.20 = (f32[16,512]{1,0:T(8,128)S(1)}, f32[16,512]{1,0:T(8,128)S(1)}, u32[]{:S(2)}, u32[]{:S(2)}) collective-permute-start(f32[16,512]{1,0:T(8,128)S(1)} %get-tuple-element.98), channel_id=1, source_target_pairs={{0,16},{32,48},{64,80},{96,112},{128,144},{160,176},{192,208},{224... | collective-permute-start | bytes 98312 | tf_op jit(solution)/shard_map/ppermute | solution.py:465
  92.9 12.6 %collective-permute-start.21 = (f32[16,512]{1,0:T(8,128)S(1)}, f32[16,512]{1,0:T(8,128)S(1)}, u32[]{:S(2)}, u32[]{:S(2)}) collective-permute-start(f32[16,512]{1,0:T(8,128)S(1)} %get-tuple-element.99), channel_id=1, source_target_pairs={{16,32},{48,64},{80,96},{112,128},{144,160},{176,192},{208,224},{2... | collective-permute-start | bytes 98312 | tf_op jit(solution)/shard_map/ppermute | solution.py:465
  93.6 11.9 %collective-permute-start.22 = (f32[16,512]{1,0:T(8,128)S(1)}, f32[16,512]{1,0:T(8,128)S(1)}, u32[]{:S(2)}, u32[]{:S(2)}) collective-permute-start(f32[16,512]{1,0:T(8,128)S(1)} %get-tuple-element.100), channel_id=1, source_target_pairs={{0,1},{1,2},{2,3},{3,4},{4,5},{5,6},{6,7},{7,8},{8,9},{9,10},{10,1... | collective-permute-start | bytes 98312 | tf_op jit(solution)/shard_map/ppermute | solution.py:468
  95.5 10.0 %collective-permute-start.23 = (f32[16,512]{1,0:T(8,128)S(1)}, f32[16,512]{1,0:T(8,128)S(1)}, u32[]{:S(2)}, u32[]{:S(2)}) collective-permute-start(f32[16,512]{1,0:T(8,128)S(1)} %get-tuple-element.101), channel_id=1, source_target_pairs={{1,0},{2,1},{3,2},{4,3},{5,4},{6,5},{7,6},{8,7},{9,8},{10,9},{11,1... | collective-permute-start | bytes 98312 | tf_op jit(solution)/shard_map/ppermute | solution.py:468
  96.1 17.9 %all-to-all-start.1 = ((f32[32,1,128]{2,1,0:T(1,128)}), f32[32,1,128]{2,1,0:T(1,128)S(1)}, u32[]{:S(2)}, u32[]{:S(2)}) async-start(f32[32,1,128]{2,1,0:T(1,128)} %broadcast_in_dim.10), calls=%async_computation.1 | async-start | bytes 32768 | tf_op jit(solution)/shard_map/all_to_all | solution.py:512
  (7 other events, 75.1 us)

commit v6 on v5

--- a/solution.py
+++ b/solution.py
@@ -393,21 +393,17 @@
     last = fold(f * ((1.0 + MIX2) * z_ref[...] - (CENTER * GAIN2) * b0))
     both = last + (CENTER * GAIN2 - MIX2) * d5_ref[...]
     rows = [part.sum(axis=0, keepdims=True) for part in (d34_ref[0], d34_ref[1], both)]
-    lane = lax.broadcasted_iota(jnp.int32, (1, 128), 1)
-    packed = jnp.zeros((1, 128), F32)
-    for i, row in enumerate(rows):
-        row = row + pltpu.roll(row, 64, 1)
-        row = row + pltpu.roll(row, 32, 1)
-        packed = jnp.where(lane // 32 == i, row, packed)
-    dots_ref[...] = jnp.broadcast_to(packed, dots_ref.shape)
+    dots_ref[0] = jnp.concatenate(rows + [jnp.zeros((5, 128), F32)], 0)
+    for i in range(1, dots_ref.shape[0]):
+        dots_ref[i] = dots_ref[0]
 
 
 def last_kernel(dots_ref, ctl_ref, pin_ref, xe_ref, xo_ref, yb_ref, ya_ref, im_ref, dinv_ref, b1_ref, z_ref, r_ref,
                 sol_hbm, res_hbm, dir_hbm, s_ref, sol_ref, res_ref, dir_ref, sems):
-    lane = lax.broadcasted_iota(jnp.int32, (8, 128), 1)
-    row = lax.broadcasted_iota(jnp.int32, (8, 128), 0)
-    sums = jnp.sum(dots_ref[...], axis=0, keepdims=True)
-    sums = jnp.sum(jnp.where(lane // 32 == row, sums, 0.0), axis=1, keepdims=True)
+    sums = dots_ref[0]
+    for i in range(1, dots_ref.shape[0]):
+        sums = sums + dots_ref[i]
+    sums = jnp.sum(sums, axis=1, keepdims=True)
     first, curv, quad = sums[0:1], sums[1:2], sums[2:3]
     step = first / curv
     ratio = (first - 2.0 * step * curv + step * step * quad) / first
@@ -504,12 +500,13 @@
     im, part, *faces, d5 = step_call(fourth_kernel, (BIG,) + PART + (d5_shape,), 18)(
         ctl, part, *recv, dinv, z, *tail)
     recv = exchange(faces)
-    dots_shape = jax.ShapeDtypeStruct((n_y, 128), F32)
+    dots_shape = jax.ShapeDtypeStruct((n_y, 8, 128), F32)
     b1, part, *faces, dots = step_call(fifth_kernel, (BIG,) + PART + (dots_shape,), 21)(
         ctl, part, *recv, im, dinv, z, d34, d5, *tail)
     total = lax.all_to_all(dots, "gy", 0, 0, tiled=True).sum(0)
     recv = exchange(faces)
-    total = lax.all_to_all(jnp.broadcast_to(total, (n_x, 128)), "gx", 0, 0, tiled=True)
+    total, recv = lax.optimization_barrier((total, recv))
+    total = lax.all_to_all(jnp.broadcast_to(total, (n_x, 8, 128)), "gx", 0, 0, tiled=True)
     shape = jax.ShapeDtypeStruct((16, 16, COLS), F32)
     scratch = [pltpu.VMEM((ROWS, COLS), F32)] + [pltpu.VMEM((16, 16, COLS), F32)] * 3 + [pltpu.SemaphoreType.DMA((3,))]
     return pl.pallas_call(

time: 118 us -> 120 us (1.017)
  blocking collectives: 0 us -> 18.5 us
  starting transfers between devices: 80 us -> 70.7 us
  waiting for transfers between devices: 17.9 us -> 12.7 us
    all_to_all x0 -> x1, blocking collectives: none -> 18.5 us  [per_device(): lax.all_to_all(jnp.broadcast_to(total, (n_x, 8, 128)), 'gx', 0, 0, tiled=...]
    all_to_all x1 -> x0, starting transfers between devices: 9.34 us -> none  [per_device(): lax.all_to_all(jnp.broadcast_to(total, (n_x, 128)), 'gx', 0, 0, tiled=True)]
    all_to_all x1 -> x0, waiting for transfers between devices: 8.52 us -> none  [per_device(): lax.all_to_all(jnp.broadcast_to(total, (n_x, 128)), 'gx', 0, 0, tiled=True)]
    ppermute x12, waiting for transfers between devices: 7.89 us -> 10.3 us  [along_y(): return (lax.ppermute(high, 'gy', up_y), lax.ppermute(low, 'gy', down_y))]
  transfers between devices with their start and end apart: 26 -> 25, of which waited for: 12 -> 14; matrix products, arithmetic and copies ran while one was open for 1% -> 0% of each run, Pallas kernels for 0% -> 0%
where the time goes in v6:
time: 120 us; the launch traced here: 119 us
  starting transfers between devices  70.7 us (59%)
  blocking collectives  18.5 us (15%)
  Pallas kernels  15.9 us (13%)
  waiting for transfers between devices  12.7 us (11%)
    ppermute x6, starting transfers between devices, along_x(): lax.ppermute(even, 'gx', swaps(0, n_x))  38 us
    all_to_all x1, blocking collectives, per_device(): lax.all_to_all(jnp.broadcast_to(total, (n_x, 8, 128)), 'gx', 0, 0, tiled=...  18.5 us
    ppermute x12, starting transfers between devices, along_y(): return (lax.ppermute(high, 'gy', up_y), lax.ppermute(low, 'gy', down_y))  18.5 us
    ppermute x12, waiting for transfers between devices, along_y(): return (lax.ppermute(high, 'gy', up_y), lax.ppermute(low, 'gy', down_y))  10.3 us
    all_to_all x1, starting transfers between devices, per_device(): total = lax.all_to_all(dots, 'gy', 0, 0, tiled=True).sum(0)  10.2 us
    ppermute x6, starting transfers between devices, along_x(): lax.ppermute(odd, 'gx', swaps(1, n_x))  3.98 us
    pallas_call x1, Pallas kernels, per_device(): step_call(fifth_kernel, (BIG,) + PART + (dots_shape,), 21)  2.73 us
    pallas_call x1, Pallas kernels, per_device(): step_call(third_kernel, (BIG,) + PART + (d34_shape,), 20)  2.4 us
  transfers between devices with their start and end apart: 25, of which 14 were waited for; matrix products, arithmetic and copies ran while one was open for 0% of the time, Pallas kernels for 0%

profile of v6, /device:TPU:1, one launch (start us, length us, event | category | flops | bytes accessed | tf_op | source)
XLA Modules:
  0.0 118.8 jit_solution(983978254182743431)
XLA Ops:
  0.8 2.3 %shard_map.166 = (f32[256,512]{1,0:T(8,128)S(1)}, f32[256,512]{1,0:T(8,128)S(1)}, f32[256,128]{1,0:T(8,128)S(1)}, f32[256,512]{1,0:T(8,128)S(1)}, f32[256,512]{1...) custom-call(f32[4,512]{1,0:T(4,128)S(1)} %broadcast_in_dim.4.ctl_ref, ...), custom_call_target="tpu_custom_call" | custom-call | tf_op jit(solution)/shard_map/pallas_call | solution.py:479
  3.1 5.0 %collective-permute-start = (f32[56,512]{1,0:T(8,128)S(1)}, f32[56,512]{1,0:T(8,128)S(1)}, u32[]{:S(2)}, u32[]{:S(2)}) collective-permute-start(f32[56,512]{1,0:T(8,128)S(1)} %get-tuple-element.60), channel_id=1, source_target_pairs={{0,16},{32,48},{64,80},{96,112},{128,144},{160,176},{192,208},{224... | collective-permute-start | bytes 344072 | tf_op jit(solution)/shard_map/ppermute | solution.py:461
  8.8 1.5 %collective-permute-done.even_ref.xe_ref = f32[56,512]{1,0:T(8,128)S(1)} collective-permute-done((f32[56,512]{1,0:T(8,128)S(1)}, f32[56,512]{1,0:T(8,128)S(1)}, u32[]{:S(2)}, u32[]{:S(2)}) %collective-permute-start) | collective-permute-done | bytes 114720 | tf_op jit(solution)/shard_map/ppermute | solution.py:461
  10.4 3.1 %collective-permute-start.2 = (f32[56,512]{1,0:T(8,128)S(1)}, f32[56,512]{1,0:T(8,128)S(1)}, u32[]{:S(2)}, u32[]{:S(2)}) collective-permute-start(f32[56,512]{1,0:T(8,128)S(1)} %get-tuple-element.64), channel_id=1, source_target_pairs={{0,1},{1,2},{2,3},{3,4},{4,5},{5,6},{6,7},{7,8},{8,9},{9,10},{10,1... | collective-permute-start | bytes 344072 | tf_op jit(solution)/shard_map/ppermute | solution.py:464
  13.5 3.5 %collective-permute-start.3 = (f32[56,512]{1,0:T(8,128)S(1)}, f32[56,512]{1,0:T(8,128)S(1)}, u32[]{:S(2)}, u32[]{:S(2)}) collective-permute-start(f32[56,512]{1,0:T(8,128)S(1)} %get-tuple-element.65), channel_id=1, source_target_pairs={{1,0},{2,1},{3,2},{4,3},{5,4},{6,5},{7,6},{8,7},{9,8},{10,9},{11,1... | collective-permute-start | bytes 344072 | tf_op jit(solution)/shard_map/ppermute | solution.py:464
  17.9 2.2 %shard_map.168 = (f32[256,512]{1,0:T(8,128)S(1)}, f32[256,512]{1,0:T(8,128)S(1)}, f32[64,512]{1,0:T(8,128)S(1)}, f32[8,512]{1,0:T(8,128)S(1)}, f32[8,512]{1,0:T(...) custom-call(f32[4,512]{1,0:T(4,128)S(1)} %broadcast_in_dim.4.ctl_ref, ...), custom_call_target="tpu_custom_call" | custom-call | tf_op jit(solution)/shard_map/pallas_call | solution.py:488
  20.2 7.8 %collective-permute-start.4 = (f32[16,512]{1,0:T(8,128)S(1)}, f32[16,512]{1,0:T(8,128)S(1)}, u32[]{:S(2)}, u32[]{:S(2)}) collective-permute-start(f32[16,512]{1,0:T(8,128)S(1)} %get-tuple-element.72), channel_id=1, source_target_pairs={{0,16},{32,48},{64,80},{96,112},{128,144},{160,176},{192,208},{224... | collective-permute-start | bytes 98312 | tf_op jit(solution)/shard_map/ppermute | solution.py:461
  29.0 2.2 %collective-permute-start.7 = (f32[16,512]{1,0:T(8,128)S(1)}, f32[16,512]{1,0:T(8,128)S(1)}, u32[]{:S(2)}, u32[]{:S(2)}) collective-permute-start(f32[16,512]{1,0:T(8,128)S(1)} %get-tuple-element.75), channel_id=1, source_target_pairs={{1,0},{2,1},{3,2},{4,3},{5,4},{6,5},{7,6},{8,7},{9,8},{10,9},{11,1... | collective-permute-start | bytes 98312 | tf_op jit(solution)/shard_map/ppermute | solution.py:464
  32.3 2.2 %shard_map.169 = (f32[256,512]{1,0:T(8,128)S(1)}, f32[256,512]{1,0:T(8,128)S(1)}, f32[16,512]{1,0:T(8,128)S(1)}, f32[16,512]{1,0:T(8,128)S(1)}, f32[16,512]{1,0:T(8,128)S(1)}, /*index=5*/f32[16,512]{1,0:T(8,128)S(1)}) custom-call(f32[4,512]{1,0:T(4,128)S(1)} %broadcast_in_dim.4.ctl_ref, f32[256,512]{1,0:T(8,128)S(1)} %get-tuple-element.71.pin_ref, ...), custom_call_target="tpu_custom_call" | custom-call | tf_op jit(solution)/shard_map/pallas_call | solution.py:493
  34.5 8.2 %collective-permute-start.8 = (f32[16,512]{1,0:T(8,128)S(1)}, f32[16,512]{1,0:T(8,128)S(1)}, u32[]{:S(2)}, u32[]{:S(2)}) collective-permute-start(f32[16,512]{1,0:T(8,128)S(1)} %get-tuple-element.82), channel_id=1, source_target_pairs={{0,16},{32,48},{64,80},{96,112},{128,144},{160,176},{192,208},{224... | collective-permute-start | bytes 98312 | tf_op jit(solution)/shard_map/ppermute | solution.py:461
  45.4 1.4 %collective-permute-done.11.ya_ref = f32[16,512]{1,0:T(8,128)S(1)} collective-permute-done((f32[16,512]{1,0:T(8,128)S(1)}, f32[16,512]{1,0:T(8,128)S(1)}, u32[]{:S(2)}, u32[]{:S(2)}) %collective-permute-start.11) | collective-permute-done | bytes 32800 | tf_op jit(solution)/shard_map/ppermute | solution.py:464
  46.8 2.4 %shard_map.170 = (f32[256,512]{1,0:T(8,128)S(1)}, f32[256,512]{1,0:T(8,128)S(1)}, f32[16,512]{1,0:T(8,128)S(1)}, f32[16,512]{1,0:T(8,128)S(1)}, f32[16,512]{1,0:...) custom-call(f32[4,512]{1,0:T(4,128)S(1)} %broadcast_in_dim.4.ctl_ref, ...), custom_call_target="tpu_custom_call" | custom-call | tf_op jit(solution)/shard_map/pallas_call | solution.py:496
  49.2 6.0 %collective-permute-start.12 = (f32[16,512]{1,0:T(8,128)S(1)}, f32[16,512]{1,0:T(8,128)S(1)}, u32[]{:S(2)}, u32[]{:S(2)}) collective-permute-start(f32[16,512]{1,0:T(8,128)S(1)} %get-tuple-element.88), channel_id=1, source_target_pairs={{0,16},{32,48},{64,80},{96,112},{128,144},{160,176},{192,208},{224... | collective-permute-start | bytes 98312 | tf_op jit(solution)/shard_map/ppermute | solution.py:461
  56.2 2.5 %collective-permute-start.15 = (f32[16,512]{1,0:T(8,128)S(1)}, f32[16,512]{1,0:T(8,128)S(1)}, u32[]{:S(2)}, u32[]{:S(2)}) collective-permute-start(f32[16,512]{1,0:T(8,128)S(1)} %get-tuple-element.91), channel_id=1, source_target_pairs={{1,0},{2,1},{3,2},{4,3},{5,4},{6,5},{7,6},{8,7},{9,8},{10,9},{11,1... | collective-permute-start | bytes 98312 | tf_op jit(solution)/shard_map/ppermute | solution.py:464
  60.6 2.2 %shard_map.171 = (f32[256,512]{1,0:T(8,128)S(1)}, f32[256,512]{1,0:T(8,128)S(1)}, f32[16,512]{1,0:T(8,128)S(1)}, f32[16,512]{1,0:T(8,128)S(1)}, f32[16,512]{1,0:...) custom-call(f32[4,512]{1,0:T(4,128)S(1)} %broadcast_in_dim.4.ctl_ref, ...), custom_call_target="tpu_custom_call" | custom-call | tf_op jit(solution)/shard_map/pallas_call | solution.py:500
  62.8 6.7 %collective-permute-start.16 = (f32[16,512]{1,0:T(8,128)S(1)}, f32[16,512]{1,0:T(8,128)S(1)}, u32[]{:S(2)}, u32[]{:S(2)}) collective-permute-start(f32[16,512]{1,0:T(8,128)S(1)} %get-tuple-element.94), channel_id=1, source_target_pairs={{0,16},{32,48},{64,80},{96,112},{128,144},{160,176},{192,208},{224... | collective-permute-start | bytes 98312 | tf_op jit(solution)/shard_map/ppermute | solution.py:461
  70.5 3.1 %collective-permute-start.19 = (f32[16,512]{1,0:T(8,128)S(1)}, f32[16,512]{1,0:T(8,128)S(1)}, u32[]{:S(2)}, u32[]{:S(2)}) collective-permute-start(f32[16,512]{1,0:T(8,128)S(1)} %get-tuple-element.97), channel_id=1, source_target_pairs={{1,0},{2,1},{3,2},{4,3},{5,4},{6,5},{7,6},{8,7},{9,8},{10,9},{11,1... | collective-permute-start | bytes 98312 | tf_op jit(solution)/shard_map/ppermute | solution.py:464
  75.3 2.7 %shard_map.172 = (f32[256,512]{1,0:T(8,128)S(1)}, f32[256,512]{1,0:T(8,128)S(1)}, f32[16,512]{1,0:T(8,128)S(1)}, f32[16,512]{1,0:T(8,128)S(1)}, f32[16,512]{1,0:...) custom-call(f32[4,512]{1,0:T(4,128)S(1)} %broadcast_in_dim.4.ctl_ref, ...), custom_call_target="tpu_custom_call" | custom-call | tf_op jit(solution)/shard_map/pallas_call | solution.py:504
  78.1 10.2 %all-to-all-start = ((f32[16,8,128]{2,1,0:T(8,128)}), f32[16,8,128]{2,1,0:T(8,128)S(1)}, u32[]{:S(2)}, u32[]{:S(2)}) async-start(f32[16,8,128]{2,1,0:T(8,128)} %get-tuple-element.101), calls=%async_computation | async-start | bytes 131072 | tf_op jit(solution)/shard_map/all_to_all | solution.py:506
  88.3 4.3 %collective-permute-start.20 = (f32[16,512]{1,0:T(8,128)S(1)}, f32[16,512]{1,0:T(8,128)S(1)}, u32[]{:S(2)}, u32[]{:S(2)}) collective-permute-start(f32[16,512]{1,0:T(8,128)S(1)} %get-tuple-element.102), channel_id=1, source_target_pairs={{0,16},{32,48},{64,80},{96,112},{128,144},{160,176},{192,208},{224... | collective-permute-start | bytes 98312 | tf_op jit(solution)/shard_map/ppermute | solution.py:461
  93.3 1.9 %collective-permute-start.22 = (f32[16,512]{1,0:T(8,128)S(1)}, f32[16,512]{1,0:T(8,128)S(1)}, u32[]{:S(2)}, u32[]{:S(2)}) collective-permute-start(f32[16,512]{1,0:T(8,128)S(1)} %get-tuple-element.104), channel_id=1, source_target_pairs={{0,1},{1,2},{2,3},{3,4},{4,5},{5,6},{6,7},{7,8},{8,9},{9,10},{10,1... | collective-permute-start | bytes 98312 | tf_op jit(solution)/shard_map/ppermute | solution.py:464
  96.2 2.3 %collective-permute-done.23.ya_ref = f32[16,512]{1,0:T(8,128)S(1)} collective-permute-done((f32[16,512]{1,0:T(8,128)S(1)}, f32[16,512]{1,0:T(8,128)S(1)}, u32[]{:S(2)}, u32[]{:S(2)}) %collective-permute-start.23) | collective-permute-done | bytes 32800 | tf_op jit(solution)/shard_map/ppermute | solution.py:464
  98.6 18.5 %all_to_all.10.dots_ref = f32[32,8,128]{2,1,0:T(8,128)S(1)} all-to-all(f32[32,8,128]{2,1,0:T(8,128)S(1)} %broadcast_in_dim.10), channel_id=1, replica_groups=mesh['gx'=32,'gy'=16] {'gx'}, dimensions={0} | all-to-all | bytes 262144 | tf_op jit(solution)/shard_map/all_to_all | solution.py:509
  117.1 1.7 %shard_map.173 = (f32[16,16,512]{2,1,0:T(8,128)}, f32[16,16,512]{2,1,0:T(8,128)}, f32[16,16,512]{2,1,0:T(8,128)}) custom-call(f32[32,8,128]{2,1,0:T(8,128)S(1)} %all_to_all.10.dots_ref, f32[4,512]{1,0:T(4,128)S(1)} %broadcast_in_dim.4.ctl_ref, f32[256,512]{1,0:T(8,128)S(1)} %get-tuple-element.107.pin_ref, f32[16,512]{1,0:T(8,128)S(1)} %collective-permute-done.20.xe_ref, ...), custom_call_target="tpu_custom_call" | custom-call | tf_op jit(solution)/shard_map/pallas_call | solution.py:512
  (49 shorter events, 13.9 us)
Async XLA Ops:
  3.1 7.1 %collective-permute-start = (f32[56,512]{1,0:T(8,128)S(1)}, f32[56,512]{1,0:T(8,128)S(1)}, u32[]{:S(2)}, u32[]{:S(2)}) collective-permute-start(f32[56,512]{1,0:T(8,128)S(1)} %get-tuple-element.60), channel_id=1, source_target_pairs={{0,16},{32,48},{64,80},{96,112},{128,144},{160,176},{192,208},{224... | collective-permute-start | bytes 344072 | tf_op jit(solution)/shard_map/ppermute | solution.py:461
  8.1 2.2 %collective-permute-start.1 = (f32[56,512]{1,0:T(8,128)S(1)}, f32[56,512]{1,0:T(8,128)S(1)}, u32[]{:S(2)}, u32[]{:S(2)}) collective-permute-start(f32[56,512]{1,0:T(8,128)S(1)} %get-tuple-element.61), channel_id=1, source_target_pairs={{16,32},{48,64},{80,96},{112,128},{144,160},{176,192},{208,224},{2... | collective-permute-start | bytes 344072 | tf_op jit(solution)/shard_map/ppermute | solution.py:461
  10.4 7.4 %collective-permute-start.2 = (f32[56,512]{1,0:T(8,128)S(1)}, f32[56,512]{1,0:T(8,128)S(1)}, u32[]{:S(2)}, u32[]{:S(2)}) collective-permute-start(f32[56,512]{1,0:T(8,128)S(1)} %get-tuple-element.64), channel_id=1, source_target_pairs={{0,1},{1,2},{2,3},{3,4},{4,5},{5,6},{6,7},{7,8},{8,9},{9,10},{10,1... | collective-permute-start | bytes 344072 | tf_op jit(solution)/shard_map/ppermute | solution.py:464
  13.5 4.5 %collective-permute-start.3 = (f32[56,512]{1,0:T(8,128)S(1)}, f32[56,512]{1,0:T(8,128)S(1)}, u32[]{:S(2)}, u32[]{:S(2)}) collective-permute-start(f32[56,512]{1,0:T(8,128)S(1)} %get-tuple-element.65), channel_id=1, source_target_pairs={{1,0},{2,1},{3,2},{4,3},{5,4},{6,5},{7,6},{8,7},{9,8},{10,9},{11,1... | collective-permute-start | bytes 344072 | tf_op jit(solution)/shard_map/ppermute | solution.py:464
  20.2 11.0 %collective-permute-start.4 = (f32[16,512]{1,0:T(8,128)S(1)}, f32[16,512]{1,0:T(8,128)S(1)}, u32[]{:S(2)}, u32[]{:S(2)}) collective-permute-start(f32[16,512]{1,0:T(8,128)S(1)} %get-tuple-element.72), channel_id=1, source_target_pairs={{0,16},{32,48},{64,80},{96,112},{128,144},{160,176},{192,208},{224... | collective-permute-start | bytes 98312 | tf_op jit(solution)/shard_map/ppermute | solution.py:461
  28.0 3.2 %collective-permute-start.5 = (f32[16,512]{1,0:T(8,128)S(1)}, f32[16,512]{1,0:T(8,128)S(1)}, u32[]{:S(2)}, u32[]{:S(2)}) collective-permute-start(f32[16,512]{1,0:T(8,128)S(1)} %get-tuple-element.73), channel_id=1, source_target_pairs={{16,32},{48,64},{80,96},{112,128},{144,160},{176,192},{208,224},{2... | collective-permute-start | bytes 98312 | tf_op jit(solution)/shard_map/ppermute | solution.py:461
  28.7 3.2 %collective-permute-start.6 = (f32[16,512]{1,0:T(8,128)S(1)}, f32[16,512]{1,0:T(8,128)S(1)}, u32[]{:S(2)}, u32[]{:S(2)}) collective-permute-start(f32[16,512]{1,0:T(8,128)S(1)} %get-tuple-element.74), channel_id=1, source_target_pairs={{0,1},{1,2},{2,3},{3,4},{4,5},{5,6},{6,7},{7,8},{8,9},{9,10},{10,1... | collective-permute-start | bytes 98312 | tf_op jit(solution)/shard_map/ppermute | solution.py:464
  29.0 3.3 %collective-permute-start.7 = (f32[16,512]{1,0:T(8,128)S(1)}, f32[16,512]{1,0:T(8,128)S(1)}, u32[]{:S(2)}, u32[]{:S(2)}) collective-permute-start(f32[16,512]{1,0:T(8,128)S(1)} %get-tuple-element.75), channel_id=1, source_target_pairs={{1,0},{2,1},{3,2},{4,3},{5,4},{6,5},{7,6},{8,7},{9,8},{10,9},{11,1... | collective-permute-start | bytes 98312 | tf_op jit(solution)/shard_map/ppermute | solution.py:464
  34.5 10.2 %collective-permute-start.8 = (f32[16,512]{1,0:T(8,128)S(1)}, f32[16,512]{1,0:T(8,128)S(1)}, u32[]{:S(2)}, u32[]{:S(2)}) collective-permute-start(f32[16,512]{1,0:T(8,128)S(1)} %get-tuple-element.82), channel_id=1, source_target_pairs={{0,16},{32,48},{64,80},{96,112},{128,144},{160,176},{192,208},{224... | collective-permute-start | bytes 98312 | tf_op jit(solution)/shard_map/ppermute | solution.py:461
  43.4 2.0 %collective-permute-start.10 = (f32[16,512]{1,0:T(8,128)S(1)}, f32[16,512]{1,0:T(8,128)S(1)}, u32[]{:S(2)}, u32[]{:S(2)}) collective-permute-start(f32[16,512]{1,0:T(8,128)S(1)} %get-tuple-element.84), channel_id=1, source_target_pairs={{0,1},{1,2},{2,3},{3,4},{4,5},{5,6},{6,7},{7,8},{8,9},{9,10},{10,1... | collective-permute-start | bytes 98312 | tf_op jit(solution)/shard_map/ppermute | solution.py:464
  43.5 3.4 %collective-permute-start.11 = (f32[16,512]{1,0:T(8,128)S(1)}, f32[16,512]{1,0:T(8,128)S(1)}, u32[]{:S(2)}, u32[]{:S(2)}) collective-permute-start(f32[16,512]{1,0:T(8,128)S(1)} %get-tuple-element.85), channel_id=1, source_target_pairs={{1,0},{2,1},{3,2},{4,3},{5,4},{6,5},{7,6},{8,7},{9,8},{10,9},{11,1... | collective-permute-start | bytes 98312 | tf_op jit(solution)/shard_map/ppermute | solution.py:464
  49.2 9.4 %collective-permute-start.12 = (f32[16,512]{1,0:T(8,128)S(1)}, f32[16,512]{1,0:T(8,128)S(1)}, u32[]{:S(2)}, u32[]{:S(2)}) collective-permute-start(f32[16,512]{1,0:T(8,128)S(1)} %get-tuple-element.88), channel_id=1, source_target_pairs={{0,16},{32,48},{64,80},{96,112},{128,144},{160,176},{192,208},{224... | collective-permute-start | bytes 98312 | tf_op jit(solution)/shard_map/ppermute | solution.py:461
  55.2 3.4 %collective-permute-start.13 = (f32[16,512]{1,0:T(8,128)S(1)}, f32[16,512]{1,0:T(8,128)S(1)}, u32[]{:S(2)}, u32[]{:S(2)}) collective-permute-start(f32[16,512]{1,0:T(8,128)S(1)} %get-tuple-element.89), channel_id=1, source_target_pairs={{16,32},{48,64},{80,96},{112,128},{144,160},{176,192},{208,224},{2... | collective-permute-start | bytes 98312 | tf_op jit(solution)/shard_map/ppermute | solution.py:461
  55.9 3.4 %collective-permute-start.14 = (f32[16,512]{1,0:T(8,128)S(1)}, f32[16,512]{1,0:T(8,128)S(1)}, u32[]{:S(2)}, u32[]{:S(2)}) collective-permute-start(f32[16,512]{1,0:T(8,128)S(1)} %get-tuple-element.90), channel_id=1, source_target_pairs={{0,1},{1,2},{2,3},{3,4},{4,5},{5,6},{6,7},{7,8},{8,9},{9,10},{10,1... | collective-permute-start | bytes 98312 | tf_op jit(solution)/shard_map/ppermute | solution.py:464
  56.2 4.5 %collective-permute-start.15 = (f32[16,512]{1,0:T(8,128)S(1)}, f32[16,512]{1,0:T(8,128)S(1)}, u32[]{:S(2)}, u32[]{:S(2)}) collective-permute-start(f32[16,512]{1,0:T(8,128)S(1)} %get-tuple-element.91), channel_id=1, source_target_pairs={{1,0},{2,1},{3,2},{4,3},{5,4},{6,5},{7,6},{8,7},{9,8},{10,9},{11,1... | collective-permute-start | bytes 98312 | tf_op jit(solution)/shard_map/ppermute | solution.py:464
  62.8 10.8 %collective-permute-start.16 = (f32[16,512]{1,0:T(8,128)S(1)}, f32[16,512]{1,0:T(8,128)S(1)}, u32[]{:S(2)}, u32[]{:S(2)}) collective-permute-start(f32[16,512]{1,0:T(8,128)S(1)} %get-tuple-element.94), channel_id=1, source_target_pairs={{0,16},{32,48},{64,80},{96,112},{128,144},{160,176},{192,208},{224... | collective-permute-start | bytes 98312 | tf_op jit(solution)/shard_map/ppermute | solution.py:461
  69.5 4.1 %collective-permute-start.17 = (f32[16,512]{1,0:T(8,128)S(1)}, f32[16,512]{1,0:T(8,128)S(1)}, u32[]{:S(2)}, u32[]{:S(2)}) collective-permute-start(f32[16,512]{1,0:T(8,128)S(1)} %get-tuple-element.95), channel_id=1, source_target_pairs={{16,32},{48,64},{80,96},{112,128},{144,160},{176,192},{208,224},{2... | collective-permute-start | bytes 98312 | tf_op jit(solution)/shard_map/ppermute | solution.py:461
  70.2 4.1 %collective-permute-start.18 = (f32[16,512]{1,0:T(8,128)S(1)}, f32[16,512]{1,0:T(8,128)S(1)}, u32[]{:S(2)}, u32[]{:S(2)}) collective-permute-start(f32[16,512]{1,0:T(8,128)S(1)} %get-tuple-element.96), channel_id=1, source_target_pairs={{0,1},{1,2},{2,3},{3,4},{4,5},{5,6},{6,7},{7,8},{8,9},{9,10},{10,1... | collective-permute-start | bytes 98312 | tf_op jit(solution)/shard_map/ppermute | solution.py:464
  70.5 4.8 %collective-permute-start.19 = (f32[16,512]{1,0:T(8,128)S(1)}, f32[16,512]{1,0:T(8,128)S(1)}, u32[]{:S(2)}, u32[]{:S(2)}) collective-permute-start(f32[16,512]{1,0:T(8,128)S(1)} %get-tuple-element.97), channel_id=1, source_target_pairs={{1,0},{2,1},{3,2},{4,3},{5,4},{6,5},{7,6},{8,7},{9,8},{10,9},{11,1... | collective-permute-start | bytes 98312 | tf_op jit(solution)/shard_map/ppermute | solution.py:464
  78.1 18.0 %all-to-all-start = ((f32[16,8,128]{2,1,0:T(8,128)}), f32[16,8,128]{2,1,0:T(8,128)S(1)}, u32[]{:S(2)}, u32[]{:S(2)}) async-start(f32[16,8,128]{2,1,0:T(8,128)} %get-tuple-element.101), calls=%async_computation | async-start | bytes 131072 | tf_op jit(solution)/shard_map/all_to_all | solution.py:506
  88.3 7.8 %collective-permute-start.20 = (f32[16,512]{1,0:T(8,128)S(1)}, f32[16,512]{1,0:T(8,128)S(1)}, u32[]{:S(2)}, u32[]{:S(2)}) collective-permute-start(f32[16,512]{1,0:T(8,128)S(1)} %get-tuple-element.102), channel_id=1, source_target_pairs={{0,16},{32,48},{64,80},{96,112},{128,144},{160,176},{192,208},{224... | collective-permute-start | bytes 98312 | tf_op jit(solution)/shard_map/ppermute | solution.py:461
  92.6 3.5 %collective-permute-start.21 = (f32[16,512]{1,0:T(8,128)S(1)}, f32[16,512]{1,0:T(8,128)S(1)}, u32[]{:S(2)}, u32[]{:S(2)}) collective-permute-start(f32[16,512]{1,0:T(8,128)S(1)} %get-tuple-element.103), channel_id=1, source_target_pairs={{16,32},{48,64},{80,96},{112,128},{144,160},{176,192},{208,224},{2... | collective-permute-start | bytes 98312 | tf_op jit(solution)/shard_map/ppermute | solution.py:461
  93.3 2.9 %collective-permute-start.22 = (f32[16,512]{1,0:T(8,128)S(1)}, f32[16,512]{1,0:T(8,128)S(1)}, u32[]{:S(2)}, u32[]{:S(2)}) collective-permute-start(f32[16,512]{1,0:T(8,128)S(1)} %get-tuple-element.104), channel_id=1, source_target_pairs={{0,1},{1,2},{2,3},{3,4},{4,5},{5,6},{6,7},{7,8},{8,9},{9,10},{10,1... | collective-permute-start | bytes 98312 | tf_op jit(solution)/shard_map/ppermute | solution.py:464
  95.2 3.3 %collective-permute-start.23 = (f32[16,512]{1,0:T(8,128)S(1)}, f32[16,512]{1,0:T(8,128)S(1)}, u32[]{:S(2)}, u32[]{:S(2)}) collective-permute-start(f32[16,512]{1,0:T(8,128)S(1)} %get-tuple-element.105), channel_id=1, source_target_pairs={{1,0},{2,1},{3,2},{4,3},{5,4},{6,5},{7,6},{8,7},{9,8},{10,9},{11,1... | collective-permute-start | bytes 98312 | tf_op jit(solution)/shard_map/ppermute | solution.py:464
  (6 other events, 73.2 us)

commit v7 on v5

--- a/solution.py
+++ b/solution.py
@@ -392,23 +392,15 @@
     emit_partial(f, lines, ctl_ref, p_ref, (even, odd, low_y, high_y), st_ref)
     last = fold(f * ((1.0 + MIX2) * z_ref[...] - (CENTER * GAIN2) * b0))
     both = last + (CENTER * GAIN2 - MIX2) * d5_ref[...]
-    rows = [part.sum(axis=0, keepdims=True) for part in (d34_ref[0], d34_ref[1], both)]
     lane = lax.broadcasted_iota(jnp.int32, (1, 128), 1)
-    packed = jnp.zeros((1, 128), F32)
-    for i, row in enumerate(rows):
-        row = row + pltpu.roll(row, 64, 1)
-        row = row + pltpu.roll(row, 32, 1)
-        packed = jnp.where(lane // 32 == i, row, packed)
-    dots_ref[...] = jnp.broadcast_to(packed, dots_ref.shape)
+    sums = jnp.where(
+        lane == 0, jnp.sum(d34_ref[0]), jnp.where(lane == 1, jnp.sum(d34_ref[1]), jnp.sum(both)))
+    dots_ref[...] = jnp.broadcast_to(sums, dots_ref.shape)
 
 
 def last_kernel(dots_ref, ctl_ref, pin_ref, xe_ref, xo_ref, yb_ref, ya_ref, im_ref, dinv_ref, b1_ref, z_ref, r_ref,
                 sol_hbm, res_hbm, dir_hbm, s_ref, sol_ref, res_ref, dir_ref, sems):
-    lane = lax.broadcasted_iota(jnp.int32, (8, 128), 1)
-    row = lax.broadcasted_iota(jnp.int32, (8, 128), 0)
-    sums = jnp.sum(dots_ref[...], axis=0, keepdims=True)
-    sums = jnp.sum(jnp.where(lane // 32 == row, sums, 0.0), axis=1, keepdims=True)
-    first, curv, quad = sums[0:1], sums[1:2], sums[2:3]
+    first, curv, quad = dots_ref[0], dots_ref[1], dots_ref[2]
     step = first / curv
     ratio = (first - 2.0 * step * curv + step * step * quad) / first
     shape = (16, 16, COLS)
@@ -428,6 +420,7 @@
 
 
 VM = pl.BlockSpec(memory_space=pltpu.VMEM)
+SM = pl.BlockSpec(memory_space=pltpu.SMEM)
 HB = pl.BlockSpec(memory_space=pl.ANY)
 BIG = jax.ShapeDtypeStruct((ROWS, COLS), F32)
 FACE = jax.ShapeDtypeStruct((16, COLS), F32)
@@ -509,11 +502,11 @@
         ctl, part, *recv, im, dinv, z, d34, d5, *tail)
     total = lax.all_to_all(dots, "gy", 0, 0, tiled=True).sum(0)
     recv = exchange(faces)
-    total = lax.all_to_all(jnp.broadcast_to(total, (n_x, 128)), "gx", 0, 0, tiled=True)
+    total = lax.all_to_all(jnp.broadcast_to(total, (n_x, 128)), "gx", 0, 0, tiled=True).sum(0)
     shape = jax.ShapeDtypeStruct((16, 16, COLS), F32)
     scratch = [pltpu.VMEM((ROWS, COLS), F32)] + [pltpu.VMEM((16, 16, COLS), F32)] * 3 + [pltpu.SemaphoreType.DMA((3,))]
     return pl.pallas_call(
-        last_kernel, out_shape=(shape, shape, shape), in_specs=[VM] * 12, out_specs=(HB, HB, HB),
+        last_kernel, out_shape=(shape, shape, shape), in_specs=[SM] + [VM] * 11, out_specs=(HB, HB, HB),
         scratch_shapes=scratch, compiler_params=PARAMS)(total, ctl, part, *recv, im, dinv, b1, z, r)
 
 

time: 118 us -> 117 us (level)
  blocking collectives: 0 us -> 17.8 us
  starting transfers between devices: 80 us -> 70.7 us
  waiting for transfers between devices: 17.9 us -> 9.43 us
    all_to_all x0 -> x1, blocking collectives: none -> 17.8 us  [per_device(): lax.all_to_all(jnp.broadcast_to(total, (n_x, 128)), 'gx', 0, 0, tiled=True)]
    all_to_all x1 -> x0, starting transfers between devices: 9.34 us -> none  [per_device(): lax.all_to_all(jnp.broadcast_to(total, (n_x, 128)), 'gx', 0, 0, tiled=True)]
    all_to_all x1 -> x0, waiting for transfers between devices: 8.52 us -> none  [per_device(): lax.all_to_all(jnp.broadcast_to(total, (n_x, 128)), 'gx', 0, 0, tiled=True)]
  transfers between devices with their start and end apart: 26 -> 25, of which waited for: 12 -> 11; matrix products, arithmetic and copies ran while one was open for 1% -> 0% of each run, Pallas kernels for 0% -> 0%
where the time goes in v7:
time: 117 us; the launch traced here: 115 us
  starting transfers between devices  70.7 us (60%)
  blocking collectives  17.8 us (15%)
  Pallas kernels  16.5 us (14%)
  waiting for transfers between devices  9.43 us (8%)
    ppermute x6, starting transfers between devices, along_x(): lax.ppermute(even, 'gx', swaps(0, n_x))  38 us
    ppermute x12, starting transfers between devices, along_y(): return (lax.ppermute(high, 'gy', up_y), lax.ppermute(low, 'gy', down_y))  18.5 us
    all_to_all x1, blocking collectives, per_device(): lax.all_to_all(jnp.broadcast_to(total, (n_x, 128)), 'gx', 0, 0, tiled=True)  17.8 us
    all_to_all x1, starting transfers between devices, per_device(): total = lax.all_to_all(dots, 'gy', 0, 0, tiled=True).sum(0)  10.2 us
    ppermute x12, waiting for transfers between devices, along_y(): return (lax.ppermute(high, 'gy', up_y), lax.ppermute(low, 'gy', down_y))  7.89 us
    ppermute x6, starting transfers between devices, along_x(): lax.ppermute(odd, 'gx', swaps(1, n_x))  3.98 us
    pallas_call x1, Pallas kernels, per_device(): step_call(fifth_kernel, (BIG,) + PART + (dots_shape,), 21)  2.98 us
    pallas_call x1, Pallas kernels, per_device(): step_call(third_kernel, (BIG,) + PART + (d34_shape,), 20)  2.4 us
  transfers between devices with their start and end apart: 25, of which 11 were waited for; matrix products, arithmetic and copies ran while one was open for 0% of the time, Pallas kernels for 0%

profile of v7, /device:TPU:1, one launch (start us, length us, event | category | flops | bytes accessed | tf_op | source)
XLA Modules:
  0.0 115.4 jit_solution(5662599812833559621)
XLA Ops:
  0.8 2.3 %shard_map.166 = (f32[256,512]{1,0:T(8,128)S(1)}, f32[256,512]{1,0:T(8,128)S(1)}, f32[256,128]{1,0:T(8,128)S(1)}, f32[256,512]{1,0:T(8,128)S(1)}, f32[256,512]{1...) custom-call(f32[4,512]{1,0:T(4,128)S(1)} %broadcast_in_dim.4.ctl_ref, ...), custom_call_target="tpu_custom_call" | custom-call | tf_op jit(solution)/shard_map/pallas_call | solution.py:476
  3.1 5.0 %collective-permute-start = (f32[56,512]{1,0:T(8,128)S(1)}, f32[56,512]{1,0:T(8,128)S(1)}, u32[]{:S(2)}, u32[]{:S(2)}) collective-permute-start(f32[56,512]{1,0:T(8,128)S(1)} %get-tuple-element.55), channel_id=1, source_target_pairs={{0,16},{32,48},{64,80},{96,112},{128,144},{160,176},{192,208},{224... | collective-permute-start | bytes 344072 | tf_op jit(solution)/shard_map/ppermute | solution.py:458
  8.8 1.5 %collective-permute-done.even_ref.xe_ref = f32[56,512]{1,0:T(8,128)S(1)} collective-permute-done((f32[56,512]{1,0:T(8,128)S(1)}, f32[56,512]{1,0:T(8,128)S(1)}, u32[]{:S(2)}, u32[]{:S(2)}) %collective-permute-start) | collective-permute-done | bytes 114720 | tf_op jit(solution)/shard_map/ppermute | solution.py:458
  10.4 3.1 %collective-permute-start.2 = (f32[56,512]{1,0:T(8,128)S(1)}, f32[56,512]{1,0:T(8,128)S(1)}, u32[]{:S(2)}, u32[]{:S(2)}) collective-permute-start(f32[56,512]{1,0:T(8,128)S(1)} %get-tuple-element.59), channel_id=1, source_target_pairs={{0,1},{1,2},{2,3},{3,4},{4,5},{5,6},{6,7},{7,8},{8,9},{9,10},{10,1... | collective-permute-start | bytes 344072 | tf_op jit(solution)/shard_map/ppermute | solution.py:461
  13.5 3.5 %collective-permute-start.3 = (f32[56,512]{1,0:T(8,128)S(1)}, f32[56,512]{1,0:T(8,128)S(1)}, u32[]{:S(2)}, u32[]{:S(2)}) collective-permute-start(f32[56,512]{1,0:T(8,128)S(1)} %get-tuple-element.60), channel_id=1, source_target_pairs={{1,0},{2,1},{3,2},{4,3},{5,4},{6,5},{7,6},{8,7},{9,8},{10,9},{11,1... | collective-permute-start | bytes 344072 | tf_op jit(solution)/shard_map/ppermute | solution.py:461
  17.9 2.2 %shard_map.168 = (f32[256,512]{1,0:T(8,128)S(1)}, f32[256,512]{1,0:T(8,128)S(1)}, f32[64,512]{1,0:T(8,128)S(1)}, f32[8,512]{1,0:T(8,128)S(1)}, f32[8,512]{1,0:T(...) custom-call(f32[4,512]{1,0:T(4,128)S(1)} %broadcast_in_dim.4.ctl_ref, ...), custom_call_target="tpu_custom_call" | custom-call | tf_op jit(solution)/shard_map/pallas_call | solution.py:485
  20.2 7.8 %collective-permute-start.4 = (f32[16,512]{1,0:T(8,128)S(1)}, f32[16,512]{1,0:T(8,128)S(1)}, u32[]{:S(2)}, u32[]{:S(2)}) collective-permute-start(f32[16,512]{1,0:T(8,128)S(1)} %get-tuple-element.67), channel_id=1, source_target_pairs={{0,16},{32,48},{64,80},{96,112},{128,144},{160,176},{192,208},{224... | collective-permute-start | bytes 98312 | tf_op jit(solution)/shard_map/ppermute | solution.py:458
  29.0 2.2 %collective-permute-start.7 = (f32[16,512]{1,0:T(8,128)S(1)}, f32[16,512]{1,0:T(8,128)S(1)}, u32[]{:S(2)}, u32[]{:S(2)}) collective-permute-start(f32[16,512]{1,0:T(8,128)S(1)} %get-tuple-element.70), channel_id=1, source_target_pairs={{1,0},{2,1},{3,2},{4,3},{5,4},{6,5},{7,6},{8,7},{9,8},{10,9},{11,1... | collective-permute-start | bytes 98312 | tf_op jit(solution)/shard_map/ppermute | solution.py:461
  32.3 2.2 %shard_map.169 = (f32[256,512]{1,0:T(8,128)S(1)}, f32[256,512]{1,0:T(8,128)S(1)}, f32[16,512]{1,0:T(8,128)S(1)}, f32[16,512]{1,0:T(8,128)S(1)}, f32[16,512]{1,0:T(8,128)S(1)}, /*index=5*/f32[16,512]{1,0:T(8,128)S(1)}) custom-call(f32[4,512]{1,0:T(4,128)S(1)} %broadcast_in_dim.4.ctl_ref, f32[256,512]{1,0:T(8,128)S(1)} %get-tuple-element.66.pin_ref, ...), custom_call_target="tpu_custom_call" | custom-call | tf_op jit(solution)/shard_map/pallas_call | solution.py:490
  34.5 8.2 %collective-permute-start.8 = (f32[16,512]{1,0:T(8,128)S(1)}, f32[16,512]{1,0:T(8,128)S(1)}, u32[]{:S(2)}, u32[]{:S(2)}) collective-permute-start(f32[16,512]{1,0:T(8,128)S(1)} %get-tuple-element.77), channel_id=1, source_target_pairs={{0,16},{32,48},{64,80},{96,112},{128,144},{160,176},{192,208},{224... | collective-permute-start | bytes 98312 | tf_op jit(solution)/shard_map/ppermute | solution.py:458
  45.4 1.4 %collective-permute-done.11.ya_ref = f32[16,512]{1,0:T(8,128)S(1)} collective-permute-done((f32[16,512]{1,0:T(8,128)S(1)}, f32[16,512]{1,0:T(8,128)S(1)}, u32[]{:S(2)}, u32[]{:S(2)}) %collective-permute-start.11) | collective-permute-done | bytes 32800 | tf_op jit(solution)/shard_map/ppermute | solution.py:461
  46.8 2.4 %shard_map.170 = (f32[256,512]{1,0:T(8,128)S(1)}, f32[256,512]{1,0:T(8,128)S(1)}, f32[16,512]{1,0:T(8,128)S(1)}, f32[16,512]{1,0:T(8,128)S(1)}, f32[16,512]{1,0:...) custom-call(f32[4,512]{1,0:T(4,128)S(1)} %broadcast_in_dim.4.ctl_ref, ...), custom_call_target="tpu_custom_call" | custom-call | tf_op jit(solution)/shard_map/pallas_call | solution.py:493
  49.2 6.0 %collective-permute-start.12 = (f32[16,512]{1,0:T(8,128)S(1)}, f32[16,512]{1,0:T(8,128)S(1)}, u32[]{:S(2)}, u32[]{:S(2)}) collective-permute-start(f32[16,512]{1,0:T(8,128)S(1)} %get-tuple-element.83), channel_id=1, source_target_pairs={{0,16},{32,48},{64,80},{96,112},{128,144},{160,176},{192,208},{224... | collective-permute-start | bytes 98312 | tf_op jit(solution)/shard_map/ppermute | solution.py:458
  56.2 2.5 %collective-permute-start.15 = (f32[16,512]{1,0:T(8,128)S(1)}, f32[16,512]{1,0:T(8,128)S(1)}, u32[]{:S(2)}, u32[]{:S(2)}) collective-permute-start(f32[16,512]{1,0:T(8,128)S(1)} %get-tuple-element.86), channel_id=1, source_target_pairs={{1,0},{2,1},{3,2},{4,3},{5,4},{6,5},{7,6},{8,7},{9,8},{10,9},{11,1... | collective-permute-start | bytes 98312 | tf_op jit(solution)/shard_map/ppermute | solution.py:461
  59.3 1.3 %collective-permute-done.15.ya_ref = f32[16,512]{1,0:T(8,128)S(1)} collective-permute-done((f32[16,512]{1,0:T(8,128)S(1)}, f32[16,512]{1,0:T(8,128)S(1)}, u32[]{:S(2)}, u32[]{:S(2)}) %collective-permute-start.15) | collective-permute-done | bytes 32800 | tf_op jit(solution)/shard_map/ppermute | solution.py:461
  60.6 2.2 %shard_map.171 = (f32[256,512]{1,0:T(8,128)S(1)}, f32[256,512]{1,0:T(8,128)S(1)}, f32[16,512]{1,0:T(8,128)S(1)}, f32[16,512]{1,0:T(8,128)S(1)}, f32[16,512]{1,0:...) custom-call(f32[4,512]{1,0:T(4,128)S(1)} %broadcast_in_dim.4.ctl_ref, ...), custom_call_target="tpu_custom_call" | custom-call | tf_op jit(solution)/shard_map/pallas_call | solution.py:497
  62.8 6.7 %collective-permute-start.16 = (f32[16,512]{1,0:T(8,128)S(1)}, f32[16,512]{1,0:T(8,128)S(1)}, u32[]{:S(2)}, u32[]{:S(2)}) collective-permute-start(f32[16,512]{1,0:T(8,128)S(1)} %get-tuple-element.89), channel_id=1, source_target_pairs={{0,16},{32,48},{64,80},{96,112},{128,144},{160,176},{192,208},{224... | collective-permute-start | bytes 98312 | tf_op jit(solution)/shard_map/ppermute | solution.py:458
  70.5 3.1 %collective-permute-start.19 = (f32[16,512]{1,0:T(8,128)S(1)}, f32[16,512]{1,0:T(8,128)S(1)}, u32[]{:S(2)}, u32[]{:S(2)}) collective-permute-start(f32[16,512]{1,0:T(8,128)S(1)} %get-tuple-element.92), channel_id=1, source_target_pairs={{1,0},{2,1},{3,2},{4,3},{5,4},{6,5},{7,6},{8,7},{9,8},{10,9},{11,1... | collective-permute-start | bytes 98312 | tf_op jit(solution)/shard_map/ppermute | solution.py:461
  75.3 3.0 %shard_map.172 = (f32[256,512]{1,0:T(8,128)S(1)}, f32[256,512]{1,0:T(8,128)S(1)}, f32[16,512]{1,0:T(8,128)S(1)}, f32[16,512]{1,0:T(8,128)S(1)}, f32[16,512]{1,0:...) custom-call(f32[4,512]{1,0:T(4,128)S(1)} %broadcast_in_dim.4.ctl_ref, f32[256,512]{1,0:T(8,128)S(1)} %get-tuple-element.88.pin_ref, ...), custom_call_target="tpu_custom_call" | custom-call | tf_op jit(solution)/shard_map/pallas_call | solution.py:501
  78.3 10.2 %all-to-all-start = ((f32[16,1,128]{2,1,0:T(1,128)}), f32[16,1,128]{2,1,0:T(1,128)S(1)}, u32[]{:S(2)}, u32[]{:S(2)}) async-start(f32[16,1,128]{2,1,0:T(1,128)} %bitcast.5), calls=%async_computation | async-start | bytes 16384 | tf_op jit(solution)/shard_map/all_to_all | solution.py:503
  88.5 4.3 %collective-permute-start.20 = (f32[16,512]{1,0:T(8,128)S(1)}, f32[16,512]{1,0:T(8,128)S(1)}, u32[]{:S(2)}, u32[]{:S(2)}) collective-permute-start(f32[16,512]{1,0:T(8,128)S(1)} %get-tuple-element.98), channel_id=1, source_target_pairs={{0,16},{32,48},{64,80},{96,112},{128,144},{160,176},{192,208},{224... | collective-permute-start | bytes 98312 | tf_op jit(solution)/shard_map/ppermute | solution.py:458
  93.6 1.9 %collective-permute-start.22 = (f32[16,512]{1,0:T(8,128)S(1)}, f32[16,512]{1,0:T(8,128)S(1)}, u32[]{:S(2)}, u32[]{:S(2)}) collective-permute-start(f32[16,512]{1,0:T(8,128)S(1)} %get-tuple-element.100), channel_id=1, source_target_pairs={{0,1},{1,2},{2,3},{3,4},{4,5},{5,6},{6,7},{7,8},{8,9},{9,10},{10,1... | collective-permute-start | bytes 98312 | tf_op jit(solution)/shard_map/ppermute | solution.py:461
  95.5 17.8 %all_to_all.15 = f32[32,1,128]{2,1,0:T(1,128)S(1)} all-to-all(f32[32,1,128]{2,1,0:T(1,128)S(1)} %broadcast_in_dim.10), channel_id=1, replica_groups=mesh['gx'=32,'gy'=16] {'gx'}, dimensions={0} | all-to-all | bytes 32768 | tf_op jit(solution)/shard_map/all_to_all | solution.py:505
  113.4 2.1 %shard_map.173 = (f32[16,16,512]{2,1,0:T(8,128)}, f32[16,16,512]{2,1,0:T(8,128)}, f32[16,16,512]{2,1,0:T(8,128)}) custom-call(f32[128]{0:T(128)S(1)} %reduce_sum.19.dots_ref, f32[4,512]{1,0:T(4,128)S(1)} %broadcast_in_dim.4.ctl_ref, f32[256,512]{1,0:T(8,128)S(1)} %get-tuple-element.97.pin_ref, f32[16,512]{1,0:T(8,128)S(1)} %collective-permute-done.20.xe_ref, ...), custom_call_target="tpu_custom_call" | custom-call | tf_op jit(solution)/shard_map/pallas_call | solution.py:508
  (50 shorter events, 11.7 us)
Async XLA Ops:
  3.1 7.1 %collective-permute-start = (f32[56,512]{1,0:T(8,128)S(1)}, f32[56,512]{1,0:T(8,128)S(1)}, u32[]{:S(2)}, u32[]{:S(2)}) collective-permute-start(f32[56,512]{1,0:T(8,128)S(1)} %get-tuple-element.55), channel_id=1, source_target_pairs={{0,16},{32,48},{64,80},{96,112},{128,144},{160,176},{192,208},{224... | collective-permute-start | bytes 344072 | tf_op jit(solution)/shard_map/ppermute | solution.py:458
  8.1 2.2 %collective-permute-start.1 = (f32[56,512]{1,0:T(8,128)S(1)}, f32[56,512]{1,0:T(8,128)S(1)}, u32[]{:S(2)}, u32[]{:S(2)}) collective-permute-start(f32[56,512]{1,0:T(8,128)S(1)} %get-tuple-element.56), channel_id=1, source_target_pairs={{16,32},{48,64},{80,96},{112,128},{144,160},{176,192},{208,224},{2... | collective-permute-start | bytes 344072 | tf_op jit(solution)/shard_map/ppermute | solution.py:458
  10.4 7.4 %collective-permute-start.2 = (f32[56,512]{1,0:T(8,128)S(1)}, f32[56,512]{1,0:T(8,128)S(1)}, u32[]{:S(2)}, u32[]{:S(2)}) collective-permute-start(f32[56,512]{1,0:T(8,128)S(1)} %get-tuple-element.59), channel_id=1, source_target_pairs={{0,1},{1,2},{2,3},{3,4},{4,5},{5,6},{6,7},{7,8},{8,9},{9,10},{10,1... | collective-permute-start | bytes 344072 | tf_op jit(solution)/shard_map/ppermute | solution.py:461
  13.5 4.5 %collective-permute-start.3 = (f32[56,512]{1,0:T(8,128)S(1)}, f32[56,512]{1,0:T(8,128)S(1)}, u32[]{:S(2)}, u32[]{:S(2)}) collective-permute-start(f32[56,512]{1,0:T(8,128)S(1)} %get-tuple-element.60), channel_id=1, source_target_pairs={{1,0},{2,1},{3,2},{4,3},{5,4},{6,5},{7,6},{8,7},{9,8},{10,9},{11,1... | collective-permute-start | bytes 344072 | tf_op jit(solution)/shard_map/ppermute | solution.py:461
  20.2 11.0 %collective-permute-start.4 = (f32[16,512]{1,0:T(8,128)S(1)}, f32[16,512]{1,0:T(8,128)S(1)}, u32[]{:S(2)}, u32[]{:S(2)}) collective-permute-start(f32[16,512]{1,0:T(8,128)S(1)} %get-tuple-element.67), channel_id=1, source_target_pairs={{0,16},{32,48},{64,80},{96,112},{128,144},{160,176},{192,208},{224... | collective-permute-start | bytes 98312 | tf_op jit(solution)/shard_map/ppermute | solution.py:458
  28.0 3.2 %collective-permute-start.5 = (f32[16,512]{1,0:T(8,128)S(1)}, f32[16,512]{1,0:T(8,128)S(1)}, u32[]{:S(2)}, u32[]{:S(2)}) collective-permute-start(f32[16,512]{1,0:T(8,128)S(1)} %get-tuple-element.68), channel_id=1, source_target_pairs={{16,32},{48,64},{80,96},{112,128},{144,160},{176,192},{208,224},{2... | collective-permute-start | bytes 98312 | tf_op jit(solution)/shard_map/ppermute | solution.py:458
  28.7 3.2 %collective-permute-start.6 = (f32[16,512]{1,0:T(8,128)S(1)}, f32[16,512]{1,0:T(8,128)S(1)}, u32[]{:S(2)}, u32[]{:S(2)}) collective-permute-start(f32[16,512]{1,0:T(8,128)S(1)} %get-tuple-element.69), channel_id=1, source_target_pairs={{0,1},{1,2},{2,3},{3,4},{4,5},{5,6},{6,7},{7,8},{8,9},{9,10},{10,1... | collective-permute-start | bytes 98312 | tf_op jit(solution)/shard_map/ppermute | solution.py:461
  29.0 3.3 %collective-permute-start.7 = (f32[16,512]{1,0:T(8,128)S(1)}, f32[16,512]{1,0:T(8,128)S(1)}, u32[]{:S(2)}, u32[]{:S(2)}) collective-permute-start(f32[16,512]{1,0:T(8,128)S(1)} %get-tuple-element.70), channel_id=1, source_target_pairs={{1,0},{2,1},{3,2},{4,3},{5,4},{6,5},{7,6},{8,7},{9,8},{10,9},{11,1... | collective-permute-start | bytes 98312 | tf_op jit(solution)/shard_map/ppermute | solution.py:461
  34.5 10.2 %collective-permute-start.8 = (f32[16,512]{1,0:T(8,128)S(1)}, f32[16,512]{1,0:T(8,128)S(1)}, u32[]{:S(2)}, u32[]{:S(2)}) collective-permute-start(f32[16,512]{1,0:T(8,128)S(1)} %get-tuple-element.77), channel_id=1, source_target_pairs={{0,16},{32,48},{64,80},{96,112},{128,144},{160,176},{192,208},{224... | collective-permute-start | bytes 98312 | tf_op jit(solution)/shard_map/ppermute | solution.py:458
  43.4 2.0 %collective-permute-start.10 = (f32[16,512]{1,0:T(8,128)S(1)}, f32[16,512]{1,0:T(8,128)S(1)}, u32[]{:S(2)}, u32[]{:S(2)}) collective-permute-start(f32[16,512]{1,0:T(8,128)S(1)} %get-tuple-element.79), channel_id=1, source_target_pairs={{0,1},{1,2},{2,3},{3,4},{4,5},{5,6},{6,7},{7,8},{8,9},{9,10},{10,1... | collective-permute-start | bytes 98312 | tf_op jit(solution)/shard_map/ppermute | solution.py:461
  43.5 3.4 %collective-permute-start.11 = (f32[16,512]{1,0:T(8,128)S(1)}, f32[16,512]{1,0:T(8,128)S(1)}, u32[]{:S(2)}, u32[]{:S(2)}) collective-permute-start(f32[16,512]{1,0:T(8,128)S(1)} %get-tuple-element.80), channel_id=1, source_target_pairs={{1,0},{2,1},{3,2},{4,3},{5,4},{6,5},{7,6},{8,7},{9,8},{10,9},{11,1... | collective-permute-start | bytes 98312 | tf_op jit(solution)/shard_map/ppermute | solution.py:461
  49.2 9.4 %collective-permute-start.12 = (f32[16,512]{1,0:T(8,128)S(1)}, f32[16,512]{1,0:T(8,128)S(1)}, u32[]{:S(2)}, u32[]{:S(2)}) collective-permute-start(f32[16,512]{1,0:T(8,128)S(1)} %get-tuple-element.83), channel_id=1, source_target_pairs={{0,16},{32,48},{64,80},{96,112},{128,144},{160,176},{192,208},{224... | collective-permute-start | bytes 98312 | tf_op jit(solution)/shard_map/ppermute | solution.py:458
  55.2 3.4 %collective-permute-start.13 = (f32[16,512]{1,0:T(8,128)S(1)}, f32[16,512]{1,0:T(8,128)S(1)}, u32[]{:S(2)}, u32[]{:S(2)}) collective-permute-start(f32[16,512]{1,0:T(8,128)S(1)} %get-tuple-element.84), channel_id=1, source_target_pairs={{16,32},{48,64},{80,96},{112,128},{144,160},{176,192},{208,224},{2... | collective-permute-start | bytes 98312 | tf_op jit(solution)/shard_map/ppermute | solution.py:458
  55.9 3.4 %collective-permute-start.14 = (f32[16,512]{1,0:T(8,128)S(1)}, f32[16,512]{1,0:T(8,128)S(1)}, u32[]{:S(2)}, u32[]{:S(2)}) collective-permute-start(f32[16,512]{1,0:T(8,128)S(1)} %get-tuple-element.85), channel_id=1, source_target_pairs={{0,1},{1,2},{2,3},{3,4},{4,5},{5,6},{6,7},{7,8},{8,9},{9,10},{10,1... | collective-permute-start | bytes 98312 | tf_op jit(solution)/shard_map/ppermute | solution.py:461
  56.2 4.5 %collective-permute-start.15 = (f32[16,512]{1,0:T(8,128)S(1)}, f32[16,512]{1,0:T(8,128)S(1)}, u32[]{:S(2)}, u32[]{:S(2)}) collective-permute-start(f32[16,512]{1,0:T(8,128)S(1)} %get-tuple-element.86), channel_id=1, source_target_pairs={{1,0},{2,1},{3,2},{4,3},{5,4},{6,5},{7,6},{8,7},{9,8},{10,9},{11,1... | collective-permute-start | bytes 98312 | tf_op jit(solution)/shard_map/ppermute | solution.py:461
  62.8 10.8 %collective-permute-start.16 = (f32[16,512]{1,0:T(8,128)S(1)}, f32[16,512]{1,0:T(8,128)S(1)}, u32[]{:S(2)}, u32[]{:S(2)}) collective-permute-start(f32[16,512]{1,0:T(8,128)S(1)} %get-tuple-element.89), channel_id=1, source_target_pairs={{0,16},{32,48},{64,80},{96,112},{128,144},{160,176},{192,208},{224... | collective-permute-start | bytes 98312 | tf_op jit(solution)/shard_map/ppermute | solution.py:458
  69.5 4.1 %collective-permute-start.17 = (f32[16,512]{1,0:T(8,128)S(1)}, f32[16,512]{1,0:T(8,128)S(1)}, u32[]{:S(2)}, u32[]{:S(2)}) collective-permute-start(f32[16,512]{1,0:T(8,128)S(1)} %get-tuple-element.90), channel_id=1, source_target_pairs={{16,32},{48,64},{80,96},{112,128},{144,160},{176,192},{208,224},{2... | collective-permute-start | bytes 98312 | tf_op jit(solution)/shard_map/ppermute | solution.py:458
  70.2 4.1 %collective-permute-start.18 = (f32[16,512]{1,0:T(8,128)S(1)}, f32[16,512]{1,0:T(8,128)S(1)}, u32[]{:S(2)}, u32[]{:S(2)}) collective-permute-start(f32[16,512]{1,0:T(8,128)S(1)} %get-tuple-element.91), channel_id=1, source_target_pairs={{0,1},{1,2},{2,3},{3,4},{4,5},{5,6},{6,7},{7,8},{8,9},{9,10},{10,1... | collective-permute-start | bytes 98312 | tf_op jit(solution)/shard_map/ppermute | solution.py:461
  70.5 4.8 %collective-permute-start.19 = (f32[16,512]{1,0:T(8,128)S(1)}, f32[16,512]{1,0:T(8,128)S(1)}, u32[]{:S(2)}, u32[]{:S(2)}) collective-permute-start(f32[16,512]{1,0:T(8,128)S(1)} %get-tuple-element.92), channel_id=1, source_target_pairs={{1,0},{2,1},{3,2},{4,3},{5,4},{6,5},{7,6},{8,7},{9,8},{10,9},{11,1... | collective-permute-start | bytes 98312 | tf_op jit(solution)/shard_map/ppermute | solution.py:461
  78.3 17.2 %all-to-all-start = ((f32[16,1,128]{2,1,0:T(1,128)}), f32[16,1,128]{2,1,0:T(1,128)S(1)}, u32[]{:S(2)}, u32[]{:S(2)}) async-start(f32[16,1,128]{2,1,0:T(1,128)} %bitcast.5), calls=%async_computation | async-start | bytes 16384 | tf_op jit(solution)/shard_map/all_to_all | solution.py:503
  88.5 24.8 %collective-permute-start.20 = (f32[16,512]{1,0:T(8,128)S(1)}, f32[16,512]{1,0:T(8,128)S(1)}, u32[]{:S(2)}, u32[]{:S(2)}) collective-permute-start(f32[16,512]{1,0:T(8,128)S(1)} %get-tuple-element.98), channel_id=1, source_target_pairs={{0,16},{32,48},{64,80},{96,112},{128,144},{160,176},{192,208},{224... | collective-permute-start | bytes 98312 | tf_op jit(solution)/shard_map/ppermute | solution.py:458
  92.9 20.4 %collective-permute-start.21 = (f32[16,512]{1,0:T(8,128)S(1)}, f32[16,512]{1,0:T(8,128)S(1)}, u32[]{:S(2)}, u32[]{:S(2)}) collective-permute-start(f32[16,512]{1,0:T(8,128)S(1)} %get-tuple-element.99), channel_id=1, source_target_pairs={{16,32},{48,64},{80,96},{112,128},{144,160},{176,192},{208,224},{2... | collective-permute-start | bytes 98312 | tf_op jit(solution)/shard_map/ppermute | solution.py:458
  93.6 19.8 %collective-permute-start.22 = (f32[16,512]{1,0:T(8,128)S(1)}, f32[16,512]{1,0:T(8,128)S(1)}, u32[]{:S(2)}, u32[]{:S(2)}) collective-permute-start(f32[16,512]{1,0:T(8,128)S(1)} %get-tuple-element.100), channel_id=1, source_target_pairs={{0,1},{1,2},{2,3},{3,4},{4,5},{5,6},{6,7},{7,8},{8,9},{9,10},{10,1... | collective-permute-start | bytes 98312 | tf_op jit(solution)/shard_map/ppermute | solution.py:461
  95.5 17.9 %collective-permute-start.23 = (f32[16,512]{1,0:T(8,128)S(1)}, f32[16,512]{1,0:T(8,128)S(1)}, u32[]{:S(2)}, u32[]{:S(2)}) collective-permute-start(f32[16,512]{1,0:T(8,128)S(1)} %get-tuple-element.101), channel_id=1, source_target_pairs={{1,0},{2,1},{3,2},{4,3},{5,4},{6,5},{7,6},{8,7},{9,8},{10,9},{11,1... | collective-permute-start | bytes 98312 | tf_op jit(solution)/shard_map/ppermute | solution.py:461
  (6 other events, 73.2 us)

commit v8 on v7

--- a/solution.py
+++ b/solution.py
@@ -393,8 +393,9 @@
     last = fold(f * ((1.0 + MIX2) * z_ref[...] - (CENTER * GAIN2) * b0))
     both = last + (CENTER * GAIN2 - MIX2) * d5_ref[...]
     lane = lax.broadcasted_iota(jnp.int32, (1, 128), 1)
-    sums = jnp.where(
-        lane == 0, jnp.sum(d34_ref[0]), jnp.where(lane == 1, jnp.sum(d34_ref[1]), jnp.sum(both)))
+    rows = [part.sum(axis=0, keepdims=True) for part in (d34_ref[0], d34_ref[1], both)]
+    sums = jnp.sum(jnp.concatenate(rows + [jnp.zeros((5, 128), F32)], 0), axis=1, keepdims=True)
+    sums = jnp.where(lane == 0, sums[0:1], jnp.where(lane == 1, sums[1:2], sums[2:3]))
     dots_ref[...] = jnp.broadcast_to(sums, dots_ref.shape)
 
 

time: 117 us -> 117 us (level)
  no operation moved by 1% of the time
where the time goes in v8:
time: 117 us; the launch traced here: 115 us
  starting transfers between devices  70.7 us (60%)
  blocking collectives  17.8 us (15%)
  Pallas kernels  16.5 us (14%)
  waiting for transfers between devices  9.42 us (8%)
    ppermute x6, starting transfers between devices, along_x(): lax.ppermute(even, 'gx', swaps(0, n_x))  38 us
    ppermute x12, starting transfers between devices, along_y(): return (lax.ppermute(high, 'gy', up_y), lax.ppermute(low, 'gy', down_y))  18.5 us
    all_to_all x1, blocking collectives, per_device(): lax.all_to_all(jnp.broadcast_to(total, (n_x, 128)), 'gx', 0, 0, tiled=True)  17.8 us
    all_to_all x1, starting transfers between devices, per_device(): total = lax.all_to_all(dots, 'gy', 0, 0, tiled=True).sum(0)  10.2 us
    ppermute x12, waiting for transfers between devices, along_y(): return (lax.ppermute(high, 'gy', up_y), lax.ppermute(low, 'gy', down_y))  7.89 us
    ppermute x6, starting transfers between devices, along_x(): lax.ppermute(odd, 'gx', swaps(1, n_x))  3.98 us
    pallas_call x1, Pallas kernels, per_device(): step_call(fifth_kernel, (BIG,) + PART + (dots_shape,), 21)  2.96 us
    pallas_call x1, Pallas kernels, per_device(): step_call(third_kernel, (BIG,) + PART + (d34_shape,), 20)  2.4 us
  transfers between devices with their start and end apart: 25, of which 11 were waited for; matrix products, arithmetic and copies ran while one was open for 0% of the time, Pallas kernels for 0%

profile of v8, /device:TPU:1, one launch (start us, length us, event | category | flops | bytes accessed | tf_op | source)
XLA Modules:
  0.0 115.4 jit_solution(9494286702603425503)
XLA Ops:
  0.8 2.3 %shard_map.166 = (f32[256,512]{1,0:T(8,128)S(1)}, f32[256,512]{1,0:T(8,128)S(1)}, f32[256,128]{1,0:T(8,128)S(1)}, f32[256,512]{1,0:T(8,128)S(1)}, f32[256,512]{1...) custom-call(f32[4,512]{1,0:T(4,128)S(1)} %broadcast_in_dim.4.ctl_ref, ...), custom_call_target="tpu_custom_call" | custom-call | tf_op jit(solution)/shard_map/pallas_call | solution.py:477
  3.1 5.0 %collective-permute-start = (f32[56,512]{1,0:T(8,128)S(1)}, f32[56,512]{1,0:T(8,128)S(1)}, u32[]{:S(2)}, u32[]{:S(2)}) collective-permute-start(f32[56,512]{1,0:T(8,128)S(1)} %get-tuple-element.55), channel_id=1, source_target_pairs={{0,16},{32,48},{64,80},{96,112},{128,144},{160,176},{192,208},{224... | collective-permute-start | bytes 344072 | tf_op jit(solution)/shard_map/ppermute | solution.py:459
  8.8 1.5 %collective-permute-done.even_ref.xe_ref = f32[56,512]{1,0:T(8,128)S(1)} collective-permute-done((f32[56,512]{1,0:T(8,128)S(1)}, f32[56,512]{1,0:T(8,128)S(1)}, u32[]{:S(2)}, u32[]{:S(2)}) %collective-permute-start) | collective-permute-done | bytes 114720 | tf_op jit(solution)/shard_map/ppermute | solution.py:459
  10.4 3.1 %collective-permute-start.2 = (f32[56,512]{1,0:T(8,128)S(1)}, f32[56,512]{1,0:T(8,128)S(1)}, u32[]{:S(2)}, u32[]{:S(2)}) collective-permute-start(f32[56,512]{1,0:T(8,128)S(1)} %get-tuple-element.59), channel_id=1, source_target_pairs={{0,1},{1,2},{2,3},{3,4},{4,5},{5,6},{6,7},{7,8},{8,9},{9,10},{10,1... | collective-permute-start | bytes 344072 | tf_op jit(solution)/shard_map/ppermute | solution.py:462
  13.5 3.5 %collective-permute-start.3 = (f32[56,512]{1,0:T(8,128)S(1)}, f32[56,512]{1,0:T(8,128)S(1)}, u32[]{:S(2)}, u32[]{:S(2)}) collective-permute-start(f32[56,512]{1,0:T(8,128)S(1)} %get-tuple-element.60), channel_id=1, source_target_pairs={{1,0},{2,1},{3,2},{4,3},{5,4},{6,5},{7,6},{8,7},{9,8},{10,9},{11,1... | collective-permute-start | bytes 344072 | tf_op jit(solution)/shard_map/ppermute | solution.py:462
  17.9 2.2 %shard_map.168 = (f32[256,512]{1,0:T(8,128)S(1)}, f32[256,512]{1,0:T(8,128)S(1)}, f32[64,512]{1,0:T(8,128)S(1)}, f32[8,512]{1,0:T(8,128)S(1)}, f32[8,512]{1,0:T(...) custom-call(f32[4,512]{1,0:T(4,128)S(1)} %broadcast_in_dim.4.ctl_ref, ...), custom_call_target="tpu_custom_call" | custom-call | tf_op jit(solution)/shard_map/pallas_call | solution.py:486
  20.2 7.8 %collective-permute-start.4 = (f32[16,512]{1,0:T(8,128)S(1)}, f32[16,512]{1,0:T(8,128)S(1)}, u32[]{:S(2)}, u32[]{:S(2)}) collective-permute-start(f32[16,512]{1,0:T(8,128)S(1)} %get-tuple-element.67), channel_id=1, source_target_pairs={{0,16},{32,48},{64,80},{96,112},{128,144},{160,176},{192,208},{224... | collective-permute-start | bytes 98312 | tf_op jit(solution)/shard_map/ppermute | solution.py:459
  29.0 2.2 %collective-permute-start.7 = (f32[16,512]{1,0:T(8,128)S(1)}, f32[16,512]{1,0:T(8,128)S(1)}, u32[]{:S(2)}, u32[]{:S(2)}) collective-permute-start(f32[16,512]{1,0:T(8,128)S(1)} %get-tuple-element.70), channel_id=1, source_target_pairs={{1,0},{2,1},{3,2},{4,3},{5,4},{6,5},{7,6},{8,7},{9,8},{10,9},{11,1... | collective-permute-start | bytes 98312 | tf_op jit(solution)/shard_map/ppermute | solution.py:462
  32.3 2.2 %shard_map.169 = (f32[256,512]{1,0:T(8,128)S(1)}, f32[256,512]{1,0:T(8,128)S(1)}, f32[16,512]{1,0:T(8,128)S(1)}, f32[16,512]{1,0:T(8,128)S(1)}, f32[16,512]{1,0:T(8,128)S(1)}, /*index=5*/f32[16,512]{1,0:T(8,128)S(1)}) custom-call(f32[4,512]{1,0:T(4,128)S(1)} %broadcast_in_dim.4.ctl_ref, f32[256,512]{1,0:T(8,128)S(1)} %get-tuple-element.66.pin_ref, ...), custom_call_target="tpu_custom_call" | custom-call | tf_op jit(solution)/shard_map/pallas_call | solution.py:491
  34.5 8.2 %collective-permute-start.8 = (f32[16,512]{1,0:T(8,128)S(1)}, f32[16,512]{1,0:T(8,128)S(1)}, u32[]{:S(2)}, u32[]{:S(2)}) collective-permute-start(f32[16,512]{1,0:T(8,128)S(1)} %get-tuple-element.77), channel_id=1, source_target_pairs={{0,16},{32,48},{64,80},{96,112},{128,144},{160,176},{192,208},{224... | collective-permute-start | bytes 98312 | tf_op jit(solution)/shard_map/ppermute | solution.py:459
  45.4 1.4 %collective-permute-done.11.ya_ref = f32[16,512]{1,0:T(8,128)S(1)} collective-permute-done((f32[16,512]{1,0:T(8,128)S(1)}, f32[16,512]{1,0:T(8,128)S(1)}, u32[]{:S(2)}, u32[]{:S(2)}) %collective-permute-start.11) | collective-permute-done | bytes 32800 | tf_op jit(solution)/shard_map/ppermute | solution.py:462
  46.8 2.4 %shard_map.170 = (f32[256,512]{1,0:T(8,128)S(1)}, f32[256,512]{1,0:T(8,128)S(1)}, f32[16,512]{1,0:T(8,128)S(1)}, f32[16,512]{1,0:T(8,128)S(1)}, f32[16,512]{1,0:...) custom-call(f32[4,512]{1,0:T(4,128)S(1)} %broadcast_in_dim.4.ctl_ref, ...), custom_call_target="tpu_custom_call" | custom-call | tf_op jit(solution)/shard_map/pallas_call | solution.py:494
  49.2 6.0 %collective-permute-start.12 = (f32[16,512]{1,0:T(8,128)S(1)}, f32[16,512]{1,0:T(8,128)S(1)}, u32[]{:S(2)}, u32[]{:S(2)}) collective-permute-start(f32[16,512]{1,0:T(8,128)S(1)} %get-tuple-element.83), channel_id=1, source_target_pairs={{0,16},{32,48},{64,80},{96,112},{128,144},{160,176},{192,208},{224... | collective-permute-start | bytes 98312 | tf_op jit(solution)/shard_map/ppermute | solution.py:459
  56.2 2.5 %collective-permute-start.15 = (f32[16,512]{1,0:T(8,128)S(1)}, f32[16,512]{1,0:T(8,128)S(1)}, u32[]{:S(2)}, u32[]{:S(2)}) collective-permute-start(f32[16,512]{1,0:T(8,128)S(1)} %get-tuple-element.86), channel_id=1, source_target_pairs={{1,0},{2,1},{3,2},{4,3},{5,4},{6,5},{7,6},{8,7},{9,8},{10,9},{11,1... | collective-permute-start | bytes 98312 | tf_op jit(solution)/shard_map/ppermute | solution.py:462
  59.3 1.3 %collective-permute-done.15.ya_ref = f32[16,512]{1,0:T(8,128)S(1)} collective-permute-done((f32[16,512]{1,0:T(8,128)S(1)}, f32[16,512]{1,0:T(8,128)S(1)}, u32[]{:S(2)}, u32[]{:S(2)}) %collective-permute-start.15) | collective-permute-done | bytes 32800 | tf_op jit(solution)/shard_map/ppermute | solution.py:462
  60.6 2.2 %shard_map.171 = (f32[256,512]{1,0:T(8,128)S(1)}, f32[256,512]{1,0:T(8,128)S(1)}, f32[16,512]{1,0:T(8,128)S(1)}, f32[16,512]{1,0:T(8,128)S(1)}, f32[16,512]{1,0:...) custom-call(f32[4,512]{1,0:T(4,128)S(1)} %broadcast_in_dim.4.ctl_ref, ...), custom_call_target="tpu_custom_call" | custom-call | tf_op jit(solution)/shard_map/pallas_call | solution.py:498
  62.8 6.7 %collective-permute-start.16 = (f32[16,512]{1,0:T(8,128)S(1)}, f32[16,512]{1,0:T(8,128)S(1)}, u32[]{:S(2)}, u32[]{:S(2)}) collective-permute-start(f32[16,512]{1,0:T(8,128)S(1)} %get-tuple-element.89), channel_id=1, source_target_pairs={{0,16},{32,48},{64,80},{96,112},{128,144},{160,176},{192,208},{224... | collective-permute-start | bytes 98312 | tf_op jit(solution)/shard_map/ppermute | solution.py:459
  70.5 3.1 %collective-permute-start.19 = (f32[16,512]{1,0:T(8,128)S(1)}, f32[16,512]{1,0:T(8,128)S(1)}, u32[]{:S(2)}, u32[]{:S(2)}) collective-permute-start(f32[16,512]{1,0:T(8,128)S(1)} %get-tuple-element.92), channel_id=1, source_target_pairs={{1,0},{2,1},{3,2},{4,3},{5,4},{6,5},{7,6},{8,7},{9,8},{10,9},{11,1... | collective-permute-start | bytes 98312 | tf_op jit(solution)/shard_map/ppermute | solution.py:462
  75.3 3.0 %shard_map.172 = (f32[256,512]{1,0:T(8,128)S(1)}, f32[256,512]{1,0:T(8,128)S(1)}, f32[16,512]{1,0:T(8,128)S(1)}, f32[16,512]{1,0:T(8,128)S(1)}, f32[16,512]{1,0:...) custom-call(f32[4,512]{1,0:T(4,128)S(1)} %broadcast_in_dim.4.ctl_ref, f32[256,512]{1,0:T(8,128)S(1)} %get-tuple-element.88.pin_ref, ...), custom_call_target="tpu_custom_call" | custom-call | tf_op jit(solution)/shard_map/pallas_call | solution.py:502
  78.3 10.2 %all-to-all-start = ((f32[16,1,128]{2,1,0:T(1,128)}), f32[16,1,128]{2,1,0:T(1,128)S(1)}, u32[]{:S(2)}, u32[]{:S(2)}) async-start(f32[16,1,128]{2,1,0:T(1,128)} %bitcast.5), calls=%async_computation | async-start | bytes 16384 | tf_op jit(solution)/shard_map/all_to_all | solution.py:504
  88.5 4.4 %collective-permute-start.20 = (f32[16,512]{1,0:T(8,128)S(1)}, f32[16,512]{1,0:T(8,128)S(1)}, u32[]{:S(2)}, u32[]{:S(2)}) collective-permute-start(f32[16,512]{1,0:T(8,128)S(1)} %get-tuple-element.98), channel_id=1, source_target_pairs={{0,16},{32,48},{64,80},{96,112},{128,144},{160,176},{192,208},{224... | collective-permute-start | bytes 98312 | tf_op jit(solution)/shard_map/ppermute | solution.py:459
  93.5 1.9 %collective-permute-start.22 = (f32[16,512]{1,0:T(8,128)S(1)}, f32[16,512]{1,0:T(8,128)S(1)}, u32[]{:S(2)}, u32[]{:S(2)}) collective-permute-start(f32[16,512]{1,0:T(8,128)S(1)} %get-tuple-element.100), channel_id=1, source_target_pairs={{0,1},{1,2},{2,3},{3,4},{4,5},{5,6},{6,7},{7,8},{8,9},{9,10},{10,1... | collective-permute-start | bytes 98312 | tf_op jit(solution)/shard_map/ppermute | solution.py:462
  95.5 17.8 %all_to_all.15 = f32[32,1,128]{2,1,0:T(1,128)S(1)} all-to-all(f32[32,1,128]{2,1,0:T(1,128)S(1)} %broadcast_in_dim.10), channel_id=1, replica_groups=mesh['gx'=32,'gy'=16] {'gx'}, dimensions={0} | all-to-all | bytes 32768 | tf_op jit(solution)/shard_map/all_to_all | solution.py:506
  113.3 2.1 %shard_map.173 = (f32[16,16,512]{2,1,0:T(8,128)}, f32[16,16,512]{2,1,0:T(8,128)}, f32[16,16,512]{2,1,0:T(8,128)}) custom-call(f32[128]{0:T(128)S(1)} %reduce_sum.19.dots_ref, f32[4,512]{1,0:T(4,128)S(1)} %broadcast_in_dim.4.ctl_ref, f32[256,512]{1,0:T(8,128)S(1)} %get-tuple-element.97.pin_ref, f32[16,512]{1,0:T(8,128)S(1)} %collective-permute-done.20.xe_ref, ...), custom_call_target="tpu_custom_call" | custom-call | tf_op jit(solution)/shard_map/pallas_call | solution.py:509
  (50 shorter events, 11.6 us)
Async XLA Ops:
  3.1 7.1 %collective-permute-start = (f32[56,512]{1,0:T(8,128)S(1)}, f32[56,512]{1,0:T(8,128)S(1)}, u32[]{:S(2)}, u32[]{:S(2)}) collective-permute-start(f32[56,512]{1,0:T(8,128)S(1)} %get-tuple-element.55), channel_id=1, source_target_pairs={{0,16},{32,48},{64,80},{96,112},{128,144},{160,176},{192,208},{224... | collective-permute-start | bytes 344072 | tf_op jit(solution)/shard_map/ppermute | solution.py:459
  8.1 2.2 %collective-permute-start.1 = (f32[56,512]{1,0:T(8,128)S(1)}, f32[56,512]{1,0:T(8,128)S(1)}, u32[]{:S(2)}, u32[]{:S(2)}) collective-permute-start(f32[56,512]{1,0:T(8,128)S(1)} %get-tuple-element.56), channel_id=1, source_target_pairs={{16,32},{48,64},{80,96},{112,128},{144,160},{176,192},{208,224},{2... | collective-permute-start | bytes 344072 | tf_op jit(solution)/shard_map/ppermute | solution.py:459
  10.4 7.4 %collective-permute-start.2 = (f32[56,512]{1,0:T(8,128)S(1)}, f32[56,512]{1,0:T(8,128)S(1)}, u32[]{:S(2)}, u32[]{:S(2)}) collective-permute-start(f32[56,512]{1,0:T(8,128)S(1)} %get-tuple-element.59), channel_id=1, source_target_pairs={{0,1},{1,2},{2,3},{3,4},{4,5},{5,6},{6,7},{7,8},{8,9},{9,10},{10,1... | collective-permute-start | bytes 344072 | tf_op jit(solution)/shard_map/ppermute | solution.py:462
  13.5 4.5 %collective-permute-start.3 = (f32[56,512]{1,0:T(8,128)S(1)}, f32[56,512]{1,0:T(8,128)S(1)}, u32[]{:S(2)}, u32[]{:S(2)}) collective-permute-start(f32[56,512]{1,0:T(8,128)S(1)} %get-tuple-element.60), channel_id=1, source_target_pairs={{1,0},{2,1},{3,2},{4,3},{5,4},{6,5},{7,6},{8,7},{9,8},{10,9},{11,1... | collective-permute-start | bytes 344072 | tf_op jit(solution)/shard_map/ppermute | solution.py:462
  20.2 11.0 %collective-permute-start.4 = (f32[16,512]{1,0:T(8,128)S(1)}, f32[16,512]{1,0:T(8,128)S(1)}, u32[]{:S(2)}, u32[]{:S(2)}) collective-permute-start(f32[16,512]{1,0:T(8,128)S(1)} %get-tuple-element.67), channel_id=1, source_target_pairs={{0,16},{32,48},{64,80},{96,112},{128,144},{160,176},{192,208},{224... | collective-permute-start | bytes 98312 | tf_op jit(solution)/shard_map/ppermute | solution.py:459
  28.0 3.2 %collective-permute-start.5 = (f32[16,512]{1,0:T(8,128)S(1)}, f32[16,512]{1,0:T(8,128)S(1)}, u32[]{:S(2)}, u32[]{:S(2)}) collective-permute-start(f32[16,512]{1,0:T(8,128)S(1)} %get-tuple-element.68), channel_id=1, source_target_pairs={{16,32},{48,64},{80,96},{112,128},{144,160},{176,192},{208,224},{2... | collective-permute-start | bytes 98312 | tf_op jit(solution)/shard_map/ppermute | solution.py:459
  28.7 3.2 %collective-permute-start.6 = (f32[16,512]{1,0:T(8,128)S(1)}, f32[16,512]{1,0:T(8,128)S(1)}, u32[]{:S(2)}, u32[]{:S(2)}) collective-permute-start(f32[16,512]{1,0:T(8,128)S(1)} %get-tuple-element.69), channel_id=1, source_target_pairs={{0,1},{1,2},{2,3},{3,4},{4,5},{5,6},{6,7},{7,8},{8,9},{9,10},{10,1... | collective-permute-start | bytes 98312 | tf_op jit(solution)/shard_map/ppermute | solution.py:462
  29.0 3.3 %collective-permute-start.7 = (f32[16,512]{1,0:T(8,128)S(1)}, f32[16,512]{1,0:T(8,128)S(1)}, u32[]{:S(2)}, u32[]{:S(2)}) collective-permute-start(f32[16,512]{1,0:T(8,128)S(1)} %get-tuple-element.70), channel_id=1, source_target_pairs={{1,0},{2,1},{3,2},{4,3},{5,4},{6,5},{7,6},{8,7},{9,8},{10,9},{11,1... | collective-permute-start | bytes 98312 | tf_op jit(solution)/shard_map/ppermute | solution.py:462
  34.5 10.2 %collective-permute-start.8 = (f32[16,512]{1,0:T(8,128)S(1)}, f32[16,512]{1,0:T(8,128)S(1)}, u32[]{:S(2)}, u32[]{:S(2)}) collective-permute-start(f32[16,512]{1,0:T(8,128)S(1)} %get-tuple-element.77), channel_id=1, source_target_pairs={{0,16},{32,48},{64,80},{96,112},{128,144},{160,176},{192,208},{224... | collective-permute-start | bytes 98312 | tf_op jit(solution)/shard_map/ppermute | solution.py:459
  43.4 2.0 %collective-permute-start.10 = (f32[16,512]{1,0:T(8,128)S(1)}, f32[16,512]{1,0:T(8,128)S(1)}, u32[]{:S(2)}, u32[]{:S(2)}) collective-permute-start(f32[16,512]{1,0:T(8,128)S(1)} %get-tuple-element.79), channel_id=1, source_target_pairs={{0,1},{1,2},{2,3},{3,4},{4,5},{5,6},{6,7},{7,8},{8,9},{9,10},{10,1... | collective-permute-start | bytes 98312 | tf_op jit(solution)/shard_map/ppermute | solution.py:462
  43.5 3.4 %collective-permute-start.11 = (f32[16,512]{1,0:T(8,128)S(1)}, f32[16,512]{1,0:T(8,128)S(1)}, u32[]{:S(2)}, u32[]{:S(2)}) collective-permute-start(f32[16,512]{1,0:T(8,128)S(1)} %get-tuple-element.80), channel_id=1, source_target_pairs={{1,0},{2,1},{3,2},{4,3},{5,4},{6,5},{7,6},{8,7},{9,8},{10,9},{11,1... | collective-permute-start | bytes 98312 | tf_op jit(solution)/shard_map/ppermute | solution.py:462
  49.2 9.4 %collective-permute-start.12 = (f32[16,512]{1,0:T(8,128)S(1)}, f32[16,512]{1,0:T(8,128)S(1)}, u32[]{:S(2)}, u32[]{:S(2)}) collective-permute-start(f32[16,512]{1,0:T(8,128)S(1)} %get-tuple-element.83), channel_id=1, source_target_pairs={{0,16},{32,48},{64,80},{96,112},{128,144},{160,176},{192,208},{224... | collective-permute-start | bytes 98312 | tf_op jit(solution)/shard_map/ppermute | solution.py:459
  55.2 3.4 %collective-permute-start.13 = (f32[16,512]{1,0:T(8,128)S(1)}, f32[16,512]{1,0:T(8,128)S(1)}, u32[]{:S(2)}, u32[]{:S(2)}) collective-permute-start(f32[16,512]{1,0:T(8,128)S(1)} %get-tuple-element.84), channel_id=1, source_target_pairs={{16,32},{48,64},{80,96},{112,128},{144,160},{176,192},{208,224},{2... | collective-permute-start | bytes 98312 | tf_op jit(solution)/shard_map/ppermute | solution.py:459
  55.9 3.4 %collective-permute-start.14 = (f32[16,512]{1,0:T(8,128)S(1)}, f32[16,512]{1,0:T(8,128)S(1)}, u32[]{:S(2)}, u32[]{:S(2)}) collective-permute-start(f32[16,512]{1,0:T(8,128)S(1)} %get-tuple-element.85), channel_id=1, source_target_pairs={{0,1},{1,2},{2,3},{3,4},{4,5},{5,6},{6,7},{7,8},{8,9},{9,10},{10,1... | collective-permute-start | bytes 98312 | tf_op jit(solution)/shard_map/ppermute | solution.py:462
  56.2 4.5 %collective-permute-start.15 = (f32[16,512]{1,0:T(8,128)S(1)}, f32[16,512]{1,0:T(8,128)S(1)}, u32[]{:S(2)}, u32[]{:S(2)}) collective-permute-start(f32[16,512]{1,0:T(8,128)S(1)} %get-tuple-element.86), channel_id=1, source_target_pairs={{1,0},{2,1},{3,2},{4,3},{5,4},{6,5},{7,6},{8,7},{9,8},{10,9},{11,1... | collective-permute-start | bytes 98312 | tf_op jit(solution)/shard_map/ppermute | solution.py:462
  62.8 10.8 %collective-permute-start.16 = (f32[16,512]{1,0:T(8,128)S(1)}, f32[16,512]{1,0:T(8,128)S(1)}, u32[]{:S(2)}, u32[]{:S(2)}) collective-permute-start(f32[16,512]{1,0:T(8,128)S(1)} %get-tuple-element.89), channel_id=1, source_target_pairs={{0,16},{32,48},{64,80},{96,112},{128,144},{160,176},{192,208},{224... | collective-permute-start | bytes 98312 | tf_op jit(solution)/shard_map/ppermute | solution.py:459
  69.5 4.1 %collective-permute-start.17 = (f32[16,512]{1,0:T(8,128)S(1)}, f32[16,512]{1,0:T(8,128)S(1)}, u32[]{:S(2)}, u32[]{:S(2)}) collective-permute-start(f32[16,512]{1,0:T(8,128)S(1)} %get-tuple-element.90), channel_id=1, source_target_pairs={{16,32},{48,64},{80,96},{112,128},{144,160},{176,192},{208,224},{2... | collective-permute-start | bytes 98312 | tf_op jit(solution)/shard_map/ppermute | solution.py:459
  70.2 4.1 %collective-permute-start.18 = (f32[16,512]{1,0:T(8,128)S(1)}, f32[16,512]{1,0:T(8,128)S(1)}, u32[]{:S(2)}, u32[]{:S(2)}) collective-permute-start(f32[16,512]{1,0:T(8,128)S(1)} %get-tuple-element.91), channel_id=1, source_target_pairs={{0,1},{1,2},{2,3},{3,4},{4,5},{5,6},{6,7},{7,8},{8,9},{9,10},{10,1... | collective-permute-start | bytes 98312 | tf_op jit(solution)/shard_map/ppermute | solution.py:462
  70.5 4.8 %collective-permute-start.19 = (f32[16,512]{1,0:T(8,128)S(1)}, f32[16,512]{1,0:T(8,128)S(1)}, u32[]{:S(2)}, u32[]{:S(2)}) collective-permute-start(f32[16,512]{1,0:T(8,128)S(1)} %get-tuple-element.92), channel_id=1, source_target_pairs={{1,0},{2,1},{3,2},{4,3},{5,4},{6,5},{7,6},{8,7},{9,8},{10,9},{11,1... | collective-permute-start | bytes 98312 | tf_op jit(solution)/shard_map/ppermute | solution.py:462
  78.3 17.1 %all-to-all-start = ((f32[16,1,128]{2,1,0:T(1,128)}), f32[16,1,128]{2,1,0:T(1,128)S(1)}, u32[]{:S(2)}, u32[]{:S(2)}) async-start(f32[16,1,128]{2,1,0:T(1,128)} %bitcast.5), calls=%async_computation | async-start | bytes 16384 | tf_op jit(solution)/shard_map/all_to_all | solution.py:504
  88.5 24.8 %collective-permute-start.20 = (f32[16,512]{1,0:T(8,128)S(1)}, f32[16,512]{1,0:T(8,128)S(1)}, u32[]{:S(2)}, u32[]{:S(2)}) collective-permute-start(f32[16,512]{1,0:T(8,128)S(1)} %get-tuple-element.98), channel_id=1, source_target_pairs={{0,16},{32,48},{64,80},{96,112},{128,144},{160,176},{192,208},{224... | collective-permute-start | bytes 98312 | tf_op jit(solution)/shard_map/ppermute | solution.py:459
  92.9 20.4 %collective-permute-start.21 = (f32[16,512]{1,0:T(8,128)S(1)}, f32[16,512]{1,0:T(8,128)S(1)}, u32[]{:S(2)}, u32[]{:S(2)}) collective-permute-start(f32[16,512]{1,0:T(8,128)S(1)} %get-tuple-element.99), channel_id=1, source_target_pairs={{16,32},{48,64},{80,96},{112,128},{144,160},{176,192},{208,224},{2... | collective-permute-start | bytes 98312 | tf_op jit(solution)/shard_map/ppermute | solution.py:459
  93.5 19.8 %collective-permute-start.22 = (f32[16,512]{1,0:T(8,128)S(1)}, f32[16,512]{1,0:T(8,128)S(1)}, u32[]{:S(2)}, u32[]{:S(2)}) collective-permute-start(f32[16,512]{1,0:T(8,128)S(1)} %get-tuple-element.100), channel_id=1, source_target_pairs={{0,1},{1,2},{2,3},{3,4},{4,5},{5,6},{6,7},{7,8},{8,9},{9,10},{10,1... | collective-permute-start | bytes 98312 | tf_op jit(solution)/shard_map/ppermute | solution.py:462
  95.4 17.9 %collective-permute-start.23 = (f32[16,512]{1,0:T(8,128)S(1)}, f32[16,512]{1,0:T(8,128)S(1)}, u32[]{:S(2)}, u32[]{:S(2)}) collective-permute-start(f32[16,512]{1,0:T(8,128)S(1)} %get-tuple-element.101), channel_id=1, source_target_pairs={{1,0},{2,1},{3,2},{4,3},{5,4},{6,5},{7,6},{8,7},{9,8},{10,9},{11,1... | collective-permute-start | bytes 98312 | tf_op jit(solution)/shard_map/ppermute | solution.py:462
  (6 other events, 73.2 us)
